TPU v7x, 32 devices: a whole 2x2x4 slice. The times are simulated.
32 devices in a mesh: win: 2 (over y), row: 16 (over z, x, core).
Axes of the slice: x: 2, y: 2, z: 4, core: 2. Of those that a mesh axis runs over, the one named last changes fastest.
Arguments:
- raw: bfloat16 [4096, 16384], P(None, ('win', 'row')), parts along dimension 1, may hold values from -30 to 30, as said below
- fir_taps: float32 [16], replicated, may hold values from -1.5 to 1.5
- band_width: int32 [16], P('row'), may hold values from 1 to 8, as said below
- dead_count: int32 [16], P('row'), may hold values from 0 to 64, as said below
Outputs:
- correlations: bfloat16 [8192, 8, 8, 256], P(('win', 'row')), parts along dimension 0
There are 2 independent parts, one for each index of `win`. A program takes and returns all parts, laid end to end along the dimension named above; an argument that names none is the same for every part. Nothing has to cross between parts.
Inputs may be any that keep to these rules, and one draw needn't show every extreme that they name: `raw`: samples of the record. Row tile t pairs with column tiles t to t + band_width[t] - 1; band_width[t] <= 16 - t, and tile 0 pairs with 8 tiles. `dead_count`: some tile has 64 dead channels.
All inputs are finite; a program needn't handle non-finite values.
Results may differ from a plain program's by a relative error of at most 0.0069.
Values may be sent and summed in bfloat16 or wider, within the bound.
No kernel may reach another device: no remote copies, remote signals or barrier semaphores. Data moves between devices by JAX's collectives and lax.ppermute only.
A program may use at most 128 MiB of HBM per device.

v0:
```python
import math

import jax
import jax.numpy as jnp
from jax import lax
from jax.sharding import PartitionSpec as P

NT = 2048
NF = 512
DEC = 4
TAPS = 16
SMOOTH = 64
LAGS = 8
NB = 8


def from_behind(value, axis, steps):
    count = lax.axis_size(axis)
    initial, last = (max(0, -steps), min(count, count - steps))
    return lax.ppermute(value, axis, [(source, source + steps) for source in range(initial, last)])


def fir_decimate(padded, fir_taps, count):
    left_reach = (TAPS - DEC) // 2
    rows = padded.shape[0]
    width = padded.shape[1]
    phased = jnp.transpose(padded.reshape(rows, width // DEC, DEC), (2, 0, 1))
    filtered = jnp.zeros((rows, count), jnp.float32)
    for tap_index in range(TAPS):
        first_at = 2 * DEC - left_reach + tap_index
        phase_index = first_at % DEC
        block_start = first_at // DEC
        sampled = phased[phase_index, :, block_start : block_start + count]
        filtered = filtered + fir_taps[tap_index] * sampled
    return filtered


def spectral_table():
    sample_ids = jnp.arange(NT, dtype=jnp.int32)[:, None]
    bin_ids = jnp.arange(NF, dtype=jnp.int32)[None, :] + 1
    phases = (sample_ids * bin_ids % NT).astype(jnp.float32) * (2.0 * math.pi / NT)
    return jnp.concatenate([jnp.cos(phases), -jnp.sin(phases)], axis=1).astype(jnp.bfloat16)


def whiten(decimated):
    spectrum = jnp.dot(decimated, spectral_table(), preferred_element_type=jnp.float32)
    real_part = spectrum[:, :NF]
    imag_part = spectrum[:, NF:]
    power_bins = real_part * real_part + imag_part * imag_part
    bin_ids = jnp.arange(NF, dtype=jnp.int32)
    window = (jnp.abs(bin_ids[:, None] - bin_ids[None, :]) <= SMOOTH).astype(jnp.float32)
    counts = jnp.sum(window, axis=0)
    smoothed = (
        jnp.dot(
            power_bins, window, precision=lax.Precision.HIGHEST, preferred_element_type=jnp.float32
        )
        / counts
    )
    factor = lax.rsqrt(smoothed + 1e-05)
    return (real_part * factor, imag_part * factor)


def lag_rows(white_real, white_imag):
    lag_ids = jnp.arange(LAGS, dtype=jnp.int32) - LAGS // 2
    bin_ids = jnp.arange(NF, dtype=jnp.int32) + 1
    phases = ((lag_ids % NT)[:, None] * bin_ids[None, :] % NT).astype(jnp.float32) * (
        2.0 * math.pi / NT
    )
    cosine_table = jnp.cos(phases)[None]
    sine_table = jnp.sin(phases)[None]
    rotated_real = white_real[:, None, :] * cosine_table - white_imag[:, None, :] * sine_table
    rotated_imag = white_real[:, None, :] * sine_table + white_imag[:, None, :] * cosine_table
    stacked = jnp.concatenate([rotated_real, rotated_imag], axis=2).astype(jnp.bfloat16)
    return stacked.reshape(-1, 2 * NF)


def shards(raw, fir_taps, band_width, dead_count):
    band_span = band_width[0]
    dead_here = dead_count[0]
    channel_block = lax.all_to_all(raw, "row", split_axis=0, concat_axis=1, tiled=True)
    padded = jnp.pad(channel_block.astype(jnp.float32), ((0, 0), (2 * DEC, 2 * DEC)))
    filtered = fir_decimate(padded, fir_taps, NT)
    tile_rows = filtered.shape[0]
    keep_mask = (jnp.arange(tile_rows, dtype=jnp.int32) >= dead_here).astype(jnp.float32)[:, None]
    decimated = (filtered * keep_mask).astype(jnp.bfloat16)
    white_real, white_imag = whiten(decimated)
    white = jnp.concatenate([white_real, white_imag], axis=1).astype(jnp.bfloat16)
    lagged = lag_rows(white_real, white_imag)
    column_list = [white]
    for offset in range(1, NB):
        column_list.append(from_behind(white, "row", -offset))
    window_tiles = jnp.stack(column_list, axis=0)
    scales = (jnp.arange(NB, dtype=jnp.int32) < band_span).astype(jnp.float32) / math.sqrt(NF)
    column_block = window_tiles.reshape(NB * tile_rows, 2 * NF)
    product = lax.dot_general(
        lagged, column_block, (((1,), (1,)), ((), ())), preferred_element_type=jnp.float32
    )
    shaped = product.reshape(tile_rows, LAGS, NB, tile_rows)
    return (shaped * scales[None, None, :, None]).astype(jnp.bfloat16)


def solution(mesh):
    return jax.shard_map(
        shards,
        mesh=mesh,
        in_specs=(P(None, ("win", "row")), P(), P("row"), P("row")),
        out_specs=P(("win", "row"), None, None, None),
        check_vma=False,
    )
```

profile of v0, /device:TPU:1, one launch (start us, length us, event | category | flops | bytes accessed | tf_op | source)
XLA Modules:
  0.0 294.4 jit_solution(10741575521673612)
XLA Ops:
  0.0 7.5 %all-to-all-start = ((bf16[16,256,512]{2,1,0:T(8,128)(2,1)}), bf16[16,256,512]{2,1,0:T(8,128)(2,1)}, u32[]{:S(2)}, u32[]{:S(2)}) async-start(bf16[16,256,512]{2,1,0:T(8,128)(2,1)} %bitcast.59), calls=%async_computation | async-start | bytes 8388608 | tf_op jit(solution)/shard_map/all_to_all | solution.py:80
  9.8 18.2 %cosine_convert_fusion = (bf16[2048,512]{1,0:T(8,128)(2,1)S(1)}, bf16[2048,512]{1,0:T(8,128)(2,1)}) fusion(s32[512]{0:T(512)S(1)} %iota_add_fusion), kind=kLoop, calls=%fused_computation.19 | loop fusion | flops 17825792 | bytes 4196352 | tf_op jit(solution)/shard_map/convert.14
  28.0 57.6 %all-to-all-done = bf16[16,256,512]{2,1,0:T(8,128)(2,1)} async-done(((bf16[16,256,512]{2,1,0:T(8,128)(2,1)}), bf16[16,256,512]{2,1,0:T(8,128)(2,1)}, u32[]{:S(2)}, u32[]{:S(2)}) %all-to-all-start) | async-done | bytes 4194336 | tf_op jit(solution)/shard_map/all_to_all | solution.py:80
  85.5 6.4 %copy.11 = bf16[256,16,512]{0,2,1:T(8,128)(2,1)} copy(bf16[256,16,512]{2,0,1:T(8,128)(2,1)} %bitcast.2) | data formatting | bytes 8388608 | tf_op jit(solution)/shard_map/convert_element_type | solution.py:81
  91.9 5.2 %pad_convert_fusion = f32[256,8208]{0,1:T(8,128)} fusion(bf16[256,8192]{0,1:T(8,128)(2,1)} %bitcast.57), kind=kLoop, calls=%fused_computation.4 | loop fusion | flops 2101248 | bytes 12599296 | tf_op jit(solution)/shard_map/transpose | solution.py:27
  97.1 10.1 %reshape.192 = f32[256,2052,4]{0,2,1:T(4,128)} reshape(f32[256,8208]{0,1:T(8,128)} %pad_convert_fusion) | data formatting | bytes 16809984 | tf_op jit(solution)/shard_map/transpose | solution.py:27
  107.2 10.9 %copy.12 = f32[256,2052,4]{1,0,2:T(8,128)} copy(f32[256,2052,4]{0,2,1:T(4,128)} %reshape.192) | data formatting | bytes 16809984 | tf_op jit(solution)/shard_map/transpose | solution.py:27
  118.2 30.3 %fusion.3 = f32[256,1024]{1,0:T(8,128)S(1)} fusion(bf16[2048,512]{1,0:T(8,128)(2,1)} %get-tuple-element.16, bf16[2048,512]{1,0:T(8,128)(2,1)S(1)} %get-tuple-element.15, f32[4,256,2052]{2,1,0:T(8,128)} %bitcast.58, f32[256]{0:T(256)S(1)} %compare_convert_fusion, f32[]{:T(128)} %bitcast.19, f32[]{:T(128)} %bitcast.18, f32[]{:T(128)} %bitcast.17, ...), kind=kOutput, calls=%fused_computation.8 | convolution fusion | flops 1099431936 | bytes 38806528 | tf_op jit(solution)/shard_map/dot_general | solution.py:46
  149.2 1.9 collective-permute-start
  151.2 1.3 collective-permute-start.1
  152.5 1.3 collective-permute-start.2
  153.8 1.3 collective-permute-start.3
  155.1 1.3 collective-permute-start.4
  157.6 9.5 %collective-permute-done = bf16[256,1024]{1,0:T(8,128)(2,1)S(1)} collective-permute-done((bf16[256,1024]{1,0:T(8,128)(2,1)S(1)}, bf16[256,1024]{1,0:T(8,128)(2,1)S(1)}, u32[]{:S(2)}, u32[]{:S(2)}) %collective-permute-start) | collective-permute-done | bytes 524320 | tf_op jit(solution)/shard_map/ppermute | solution.py:20
  167.0 1.3 collective-permute-start.5
  168.4 3.1 %collective-permute-done.1 = bf16[256,1024]{1,0:T(8,128)(2,1)S(1)} collective-permute-done((bf16[256,1024]{1,0:T(8,128)(2,1)S(1)}, bf16[256,1024]{1,0:T(8,128)(2,1)S(1)}, u32[]{:S(2)}, u32[]{:S(2)}) %collective-permute-start.1) | collective-permute-done | bytes 524320 | tf_op jit(solution)/shard_map/ppermute | solution.py:20
  171.5 1.5 collective-permute-start.6
  173.0 25.6 %collective-permute-done.2 = bf16[256,1024]{1,0:T(8,128)(2,1)S(1)} collective-permute-done((bf16[256,1024]{1,0:T(8,128)(2,1)S(1)}, bf16[256,1024]{1,0:T(8,128)(2,1)S(1)}, u32[]{:S(2)}, u32[]{:S(2)}) %collective-permute-start.2) | collective-permute-done | bytes 524320 | tf_op jit(solution)/shard_map/ppermute | solution.py:20
  198.7 3.9 %collective-permute-done.3 = bf16[256,1024]{1,0:T(8,128)(2,1)S(1)} collective-permute-done((bf16[256,1024]{1,0:T(8,128)(2,1)S(1)}, bf16[256,1024]{1,0:T(8,128)(2,1)S(1)}, u32[]{:S(2)}, u32[]{:S(2)}) %collective-permute-start.3) | collective-permute-done | bytes 524320 | tf_op jit(solution)/shard_map/ppermute | solution.py:20
  202.6 2.3 collective-permute-done.4
  204.9 3.9 %collective-permute-done.5 = bf16[256,1024]{1,0:T(8,128)(2,1)S(1)} collective-permute-done((bf16[256,1024]{1,0:T(8,128)(2,1)S(1)}, bf16[256,1024]{1,0:T(8,128)(2,1)S(1)}, u32[]{:S(2)}, u32[]{:S(2)}) %collective-permute-start.5) | collective-permute-done | bytes 524320 | tf_op jit(solution)/shard_map/ppermute | solution.py:20
  208.8 62.8 %collective-permute-done.6 = bf16[256,1024]{1,0:T(8,128)(2,1)S(1)} collective-permute-done((bf16[256,1024]{1,0:T(8,128)(2,1)S(1)}, bf16[256,1024]{1,0:T(8,128)(2,1)S(1)}, u32[]{:S(2)}, u32[]{:S(2)}) %collective-permute-start.6) | collective-permute-done | bytes 524320 | tf_op jit(solution)/shard_map/ppermute | solution.py:20
  271.6 11.2 %multiply_convert_fusion = bf16[256,8,8,256]{3,0,2,1:T(8,128)(2,1)} fusion(f32[8]{0:T(128)S(1)} %compare_select_fusion.2, bf16[256,8,512]{2,0,1:T(8,128)(2,1)S(1)} %get-tuple-element.12, bf16[256,8,512]{2,0,1:T(8,128)(2,1)S(1)} %get-tuple-element.11, bf16[8,256,1024]{2,1,0:T(8,128)(2,1)S(1)} %bitcast_dynamic-update-slice_fusion), kind=kOutput, calls=%fused_computation | convolution fusion | flops 8606711808 | bytes 16777248 | tf_op jit(solution)/shard_map/dot_general | solution.py:95
  282.8 11.5 %copy.13 = bf16[256,8,8,256]{3,2,1,0:T(8,128)(2,1)} copy(bf16[256,8,8,256]{3,0,2,1:T(8,128)(2,1)} %multiply_convert_fusion) | data formatting | bytes 16777216 | tf_op jit(solution)/shard_map/convert_element_type | solution.py:99
  (20 shorter events, 3.2 us)
Async XLA Ops:
  0.0 8.9 %copy-start = (f32[16]{0:T(128)S(1)}, f32[16]{0:T(128)}, u32[]{:S(2)}) copy-start(f32[16]{0:T(128)} %param.5) | copy-start | bytes 196
  0.0 85.5 %all-to-all-start = ((bf16[16,256,512]{2,1,0:T(8,128)(2,1)}), bf16[16,256,512]{2,1,0:T(8,128)(2,1)}, u32[]{:S(2)}, u32[]{:S(2)}) async-start(bf16[16,256,512]{2,1,0:T(8,128)(2,1)} %bitcast.59), calls=%async_computation | async-start | bytes 8388608 | tf_op jit(solution)/shard_map/all_to_all | solution.py:80
  149.2 17.8 %collective-permute-start = (bf16[256,1024]{1,0:T(8,128)(2,1)S(1)}, bf16[256,1024]{1,0:T(8,128)(2,1)S(1)}, u32[]{:S(2)}, u32[]{:S(2)}) collective-permute-start(bf16[256,1024]{1,0:T(8,128)(2,1)S(1)} %pad_maximum_fusion), channel_id=1, source_target_pairs={{1,0},{2,1},{3,2},{4,3},{5,4},{6,5},{7,6},{8,7},{9,8},{10,9},{11,1... | collective-permute-start | bytes 1572872 | tf_op jit(solution)/shard_map/ppermute | solution.py:20
  151.2 20.3 %collective-permute-start.1 = (bf16[256,1024]{1,0:T(8,128)(2,1)S(1)}, bf16[256,1024]{1,0:T(8,128)(2,1)S(1)}, u32[]{:S(2)}, u32[]{:S(2)}) collective-permute-start(bf16[256,1024]{1,0:T(8,128)(2,1)S(1)} %pad_maximum_fusion), channel_id=1, source_target_pairs={{2,0},{3,1},{4,2},{5,3},{6,4},{7,5},{8,6},{9,7},{10,8},{11,9},{12,... | collective-permute-start | bytes 1572872 | tf_op jit(solution)/shard_map/ppermute | solution.py:20
  152.5 46.2 %collective-permute-start.2 = (bf16[256,1024]{1,0:T(8,128)(2,1)S(1)}, bf16[256,1024]{1,0:T(8,128)(2,1)S(1)}, u32[]{:S(2)}, u32[]{:S(2)}) collective-permute-start(bf16[256,1024]{1,0:T(8,128)(2,1)S(1)} %pad_maximum_fusion), channel_id=1, source_target_pairs={{3,0},{4,1},{5,2},{6,3},{7,4},{8,5},{9,6},{10,7},{11,8},{12,9},{13... | collective-permute-start | bytes 1572872 | tf_op jit(solution)/shard_map/ppermute | solution.py:20
  153.8 48.8 %collective-permute-start.3 = (bf16[256,1024]{1,0:T(8,128)(2,1)S(1)}, bf16[256,1024]{1,0:T(8,128)(2,1)S(1)}, u32[]{:S(2)}, u32[]{:S(2)}) collective-permute-start(bf16[256,1024]{1,0:T(8,128)(2,1)S(1)} %pad_maximum_fusion), channel_id=1, source_target_pairs={{4,0},{5,1},{6,2},{7,3},{8,4},{9,5},{10,6},{11,7},{12,8},{13,9},{1... | collective-permute-start | bytes 1572872 | tf_op jit(solution)/shard_map/ppermute | solution.py:20
  155.1 49.8 %collective-permute-start.4 = (bf16[256,1024]{1,0:T(8,128)(2,1)S(1)}, bf16[256,1024]{1,0:T(8,128)(2,1)S(1)}, u32[]{:S(2)}, u32[]{:S(2)}) collective-permute-start(bf16[256,1024]{1,0:T(8,128)(2,1)S(1)} %pad_maximum_fusion), channel_id=1, source_target_pairs={{5,0},{6,1},{7,2},{8,3},{9,4},{10,5},{11,6},{12,7},{13,8},{14,9},{... | collective-permute-start | bytes 1572872 | tf_op jit(solution)/shard_map/ppermute | solution.py:20
  167.0 41.8 %collective-permute-start.5 = (bf16[256,1024]{1,0:T(8,128)(2,1)S(1)}, bf16[256,1024]{1,0:T(8,128)(2,1)S(1)}, u32[]{:S(2)}, u32[]{:S(2)}) collective-permute-start(bf16[256,1024]{1,0:T(8,128)(2,1)S(1)} %pad_maximum_fusion), channel_id=1, source_target_pairs={{6,0},{7,1},{8,2},{9,3},{10,4},{11,5},{12,6},{13,7},{14,8},{15,9},... | collective-permute-start | bytes 1572872 | tf_op jit(solution)/shard_map/ppermute | solution.py:20
  171.5 100.1 %collective-permute-start.6 = (bf16[256,1024]{1,0:T(8,128)(2,1)S(1)}, bf16[256,1024]{1,0:T(8,128)(2,1)S(1)}, u32[]{:S(2)}, u32[]{:S(2)}) collective-permute-start(bf16[256,1024]{1,0:T(8,128)(2,1)S(1)} %pad_maximum_fusion), channel_id=1, source_target_pairs={{7,0},{8,1},{9,2},{10,3},{11,4},{12,5},{13,6},{14,7},{15,8},{23,16... | collective-permute-start | bytes 1572872 | tf_op jit(solution)/shard_map/ppermute | solution.py:20
where the time goes:
time: 295 us; the launch traced here: 294 us
  waiting for transfers between devices  169 us (57%)
  matrix products  42.2 us (14%)
  local copies, waits for them, and re-layouts  40 us (14%)
  other arithmetic  24.9 us (8%)
  starting transfers between devices  17.3 us (6%)
    ppermute x7, waiting for transfers between devices, from_behind(): lax.ppermute(value, axis, [(source, source + steps) for source in range(i...  111 us
    all_to_all x1, waiting for transfers between devices, shards(): lax.all_to_all(raw, 'row', split_axis=0, concat_axis=1, tiled=True)  57.6 us
    dot_general x1, matrix products, whiten(): jnp.dot(decimated, spectral_table(), preferred_element_type=jnp.float32)  30.3 us
    transpose x2, local copies, waits for them, and re-layouts, fir_decimate(): phased = jnp.transpose(padded.reshape(rows, width // DEC, DEC), (2, 0, 1))  21.1 us
    another operation x2, other arithmetic  19.3 us
    convert_element_type x1, local copies, waits for them, and re-layouts, shards(): return (shaped * scales[None, None, :, None]).astype(jnp.bfloat16)  11.5 us
    dot_general x1, matrix products, shards(): lax.dot_general(lagged, column_block, (((1,), (1,)), ((), ())), preferred...  11.2 us
    ppermute x7, starting transfers between devices, from_behind(): lax.ppermute(value, axis, [(source, source + steps) for source in range(i...  9.83 us
  transfers between devices with their start and end apart: 8, of which 8 were waited for; matrix products, arithmetic and copies ran while one was open for 7% of the time, Pallas kernels for 0%

commit v1 on v0

v1 whole, which is shorter than its diff:
```python
import functools
import math

import jax
import jax.numpy as jnp
import ml_dtypes
import numpy as np
from jax import lax
from jax.experimental import pallas as pl
from jax.experimental.pallas import tpu as pltpu
from jax.sharding import PartitionSpec as P

NT = 2048
NF = 512
DEC = 4
TAPS = 16
SMOOTH = 64
LAGS = 8
NB = 8
LEFT = (TAPS - DEC) // 2
LANES = 128
EDGE = 8
PLANE = 4
FLOAT = jnp.float32
HALF = jnp.bfloat16


def table_rows(samples):
    bins = np.arange(NF, dtype=np.int64)[None, :] + 1
    samples = np.asarray(samples, dtype=np.int64)[:, None]
    phases = (samples * bins % NT).astype(np.float64) * (2.0 * math.pi / NT)
    rows = np.concatenate([np.cos(phases), -np.sin(phases)], axis=1)
    inside = (samples >= 0) & (samples < NT)
    return np.where(inside, rows, 0.0).astype(ml_dtypes.bfloat16)


def edge_samples():
    blocks = NT // LANES
    offsets = np.array([-2, -1, LANES, LANES + 1] * 2)
    return (np.arange(blocks)[:, None] * LANES + offsets[None, :]).reshape(-1)


def window_table():
    ids = np.arange(NF)
    window = np.abs(ids[:, None] - ids[None, :]) <= SMOOTH
    counts = window.sum(axis=0).astype(np.float32)[None, :]
    return window.astype(ml_dtypes.bfloat16), counts


def lag_tables():
    lags = np.arange(LAGS, dtype=np.int64) - LAGS // 2
    bins = np.arange(NF, dtype=np.int64) + 1
    phases = ((lags % NT)[:, None] * bins[None, :] % NT) * (2.0 * math.pi / NT)
    return np.cos(phases).astype(np.float32), np.sin(phases).astype(np.float32)


def split(value):
    high = value.astype(HALF)
    low = (value - high.astype(FLOAT)).astype(HALF)
    return high, low


def spread_taps(taps, index):
    spread = jnp.zeros(index.shape, FLOAT)
    for tap in range(TAPS):
        spread = jnp.where(index == tap, taps[tap], spread)
    return spread


def filter_body(taps, raw, out, main, edge, *, channels):
    width = raw.shape[1]

    @pl.when(pl.program_id(0) == 0)
    def _():
        rows = lax.broadcasted_iota(jnp.int32, (width, LANES), 0)
        cols = lax.broadcasted_iota(jnp.int32, (width, LANES), 1)
        high, low = split(spread_taps(taps, rows - DEC * cols + LEFT))
        main[:, :LANES] = high
        main[:, LANES:] = low
        row = lax.broadcasted_iota(jnp.int32, (EDGE, 2 * LANES), 0) % 4
        lane = lax.broadcasted_iota(jnp.int32, (EDGE, 2 * LANES), 1)
        lane = jnp.where(lane < LANES, lane, lane + width - 2 * LANES)
        sample = jnp.where(row < 2, row - 2, row + LANES - 2)
        high, low = split(spread_taps(taps, lane - DEC * sample + LEFT))
        edge[...] = jnp.concatenate([high.astype(FLOAT), low.astype(FLOAT)], axis=0).astype(HALF)

    for tile in range(out.shape[0]):
        block = raw[pl.ds(tile * channels, channels), :]
        product = jnp.dot(block, main[...], preferred_element_type=FLOAT)
        out[tile, :channels, :] = (product[:, :LANES] + product[:, LANES:]).astype(HALF)
        ends = jnp.concatenate([block[:, :LANES], block[:, width - LANES :]], axis=1)
        partial = lax.dot_general(
            edge[...], ends, (((1,), (1,)), ((), ())), preferred_element_type=FLOAT
        )
        partial = partial[:EDGE] + partial[EDGE:]
        row = lax.broadcasted_iota(jnp.int32, (EDGE, LANES), 0)
        picked = jnp.where(row < 4, partial[:, :LANES], partial[:, LANES:])
        out[tile, channels:, :] = picked.astype(HALF)


def filter_blocks(raw, fir_taps, tiles):
    channels = raw.shape[0] // tiles
    width = raw.shape[1]
    step = 2
    return pl.pallas_call(
        functools.partial(filter_body, channels=channels),
        out_shape=jax.ShapeDtypeStruct((tiles, channels + EDGE, LANES), HALF),
        grid=(tiles // step,),
        in_specs=[
            pl.BlockSpec(memory_space=pltpu.SMEM),
            pl.BlockSpec((step * channels, width), lambda i: (i, 0)),
        ],
        out_specs=pl.BlockSpec((step, channels + EDGE, LANES), lambda i: (i, 0, 0)),
        scratch_shapes=[
            pltpu.VMEM((width, 2 * LANES), HALF),
            pltpu.VMEM((2 * EDGE, 2 * LANES), HALF),
        ],
        compiler_params=pltpu.CompilerParams(vmem_limit_bytes=16 << 20),
        name="filter",
    )(fir_taps, raw)


def filter_whole(channel_block, fir_taps):
    padded = jnp.pad(channel_block.astype(FLOAT), ((0, 0), (2 * DEC, 2 * DEC)))
    rows = padded.shape[0]
    phased = jnp.transpose(padded.reshape(rows, -1, DEC), (2, 0, 1))
    filtered = jnp.zeros((rows, NT), FLOAT)
    for tap in range(TAPS):
        first_at = 2 * DEC - LEFT + tap
        begin = first_at // DEC
        filtered = filtered + fir_taps[tap] * phased[first_at % DEC, :, begin : begin + NT]
    blocks = filtered.astype(HALF).reshape(rows, NT // LANES, LANES).transpose(1, 0, 2)
    return jnp.concatenate([blocks, jnp.zeros((NT // LANES, EDGE, LANES), HALF)], axis=1)


def whiten_body(dead, blocks, table, edge_table, window, counts, white, real, imag, total, ends):
    step = pl.program_id(0)
    group = blocks.shape[0]
    channels = white.shape[0]
    left = jnp.concatenate([blocks[i, :channels, :] for i in range(group)], axis=1)
    part = jnp.dot(left, table[...], preferred_element_type=FLOAT)
    for i in range(group):
        at = pl.multiple_of((step * group + i) * EDGE, EDGE)
        ends[pl.ds(at, EDGE), :] = blocks[i, channels:, :].astype(FLOAT)

    @pl.when(step == 0)
    def _():
        total[...] = part

    @pl.when(step > 0)
    def _():
        total[...] += part

    @pl.when(step == pl.num_programs(0) - 1)
    def _():
        turned = ends[...].T
        lane = lax.broadcasted_iota(jnp.int32, turned.shape, 1) % EDGE
        first = jnp.where(lane < 4, turned, 0.0)
        second = jnp.where(lane < 4, 0.0, turned)
        edges = jnp.concatenate([first, second], axis=0).astype(HALF)
        spectrum = total[...] + jnp.dot(edges, edge_table[...], preferred_element_type=FLOAT)
        channel = lax.broadcasted_iota(jnp.int32, spectrum.shape, 0)
        spectrum = jnp.where(channel < dead[0], 0.0, spectrum)
        re, im = spectrum[:, :NF], spectrum[:, NF:]
        high, low = split(re * re + im * im)
        summed = jnp.dot(high, window[...], preferred_element_type=FLOAT)
        summed += jnp.dot(low, window[...], preferred_element_type=FLOAT)
        factor = lax.rsqrt(summed / counts[...] + 1e-05)
        re, im = re * factor, im * factor
        real[...] = re
        imag[...] = im
        white[:, :NF] = re.astype(HALF)
        white[:, NF:] = im.astype(HALF)


def whiten(blocks, dead):
    count, height, _ = blocks.shape
    channels = height - EDGE
    group = 4
    window, counts = window_table()
    return pl.pallas_call(
        whiten_body,
        out_shape=(
            jax.ShapeDtypeStruct((channels, 2 * NF), HALF),
            jax.ShapeDtypeStruct((channels, NF), FLOAT),
            jax.ShapeDtypeStruct((channels, NF), FLOAT),
        ),
        grid=(count // group,),
        in_specs=[
            pl.BlockSpec(memory_space=pltpu.SMEM),
            pl.BlockSpec((group, height, LANES), lambda i: (i, 0, 0)),
            pl.BlockSpec((group * LANES, 2 * NF), lambda i: (i, 0)),
            pl.BlockSpec((count * EDGE, 2 * NF), lambda i: (0, 0)),
            pl.BlockSpec((NF, NF), lambda i: (0, 0)),
            pl.BlockSpec((1, NF), lambda i: (0, 0)),
        ],
        out_specs=(
            pl.BlockSpec((channels, 2 * NF), lambda i: (0, 0)),
            pl.BlockSpec((channels, NF), lambda i: (0, 0)),
            pl.BlockSpec((channels, NF), lambda i: (0, 0)),
        ),
        scratch_shapes=[
            pltpu.VMEM((channels, 2 * NF), FLOAT),
            pltpu.VMEM((count * EDGE, LANES), FLOAT),
        ],
        compiler_params=pltpu.CompilerParams(vmem_limit_bytes=32 << 20),
        name="whiten",
    )(
        dead,
        blocks,
        jnp.asarray(table_rows(np.arange(NT))),
        jnp.asarray(table_rows(edge_samples())),
        jnp.asarray(window),
        jnp.asarray(counts),
    )


def send(value, target, keep=lambda source: True):
    count = lax.axis_size("row")
    pairs = [(s, target(s)) for s in range(count) if keep(s) and 0 <= target(s) < count]
    return lax.ppermute(value, "row", pairs)


def gather_band(white):
    planes = [white]
    planes.append(send(white, lambda s: s - PLANE))
    planes.append(send(planes[1], lambda s: s - PLANE, lambda s: s % PLANE != 3))
    across = [
        send(planes[0], lambda s: s ^ 2, lambda s: s & 2 == 2),
        send(planes[1], lambda s: s ^ 2),
        send(planes[2], lambda s: s ^ 2, lambda s: s & 2 == 0),
    ]
    beside = [send(plane, lambda s: s ^ 1) for plane in planes]
    corner = [
        send(across[0], lambda s: s ^ 1, lambda s: s & 2 == 0),
        send(across[1], lambda s: s ^ 1),
        send(across[2], lambda s: s ^ 1, lambda s: s & 2 == 2),
    ]
    return [[planes[p], beside[p], across[p], corner[p]] for p in range(3)]


def correlate_body(place, real, imag, cosine, sine, *rest, rows):
    band, out, columns, lagged, wide, sems = rest[:12], rest[12], *rest[13:]
    channels = columns.shape[1]

    @pl.when(pl.program_id(0) == 0)
    def _():
        for offset in range(NB):
            for at in range(PLANE):
                plane, index = divmod(at + offset, PLANE)

                @pl.when(place[0] == at)
                def _():
                    source = band[plane * PLANE + (at ^ index)]
                    pltpu.make_async_copy(source, columns.at[offset], sems.at[offset]).start()

        for offset in range(NB):
            pltpu.make_async_copy(band[0], columns.at[offset], sems.at[offset]).wait()

    re, im = real[...], imag[...]
    for lag in range(LAGS):
        c, s = cosine[lag : lag + 1, :], sine[lag : lag + 1, :]
        lagged[pl.ds(lag * rows, rows), :NF] = (re * c - im * s).astype(HALF)
        lagged[pl.ds(lag * rows, rows), NF:] = (re * s + im * c).astype(HALF)
    for offset in range(NB):
        scale = jnp.where(offset < place[1], 1.0 / math.sqrt(NF), 0.0)
        product = lax.dot_general(
            lagged[...], columns[offset], (((1,), (1,)), ((), ())), preferred_element_type=FLOAT
        )
        product = product * scale
        for lag in range(LAGS):
            part = product[lag * rows : (lag + 1) * rows]
            for half in range(channels // LANES):
                columns_at = slice(half * LANES, (half + 1) * LANES)
                wide[half, pl.ds(lag * NB + offset, rows, LAGS * NB), :] = part[:, columns_at]
    for half in range(channels // LANES):
        block = wide[half].reshape(rows, LAGS, NB, LANES)
        out[:, :, :, half * LANES : (half + 1) * LANES] = block.astype(HALF)


def correlate(real, imag, band, place):
    channels = real.shape[0]
    rows = 32
    cosine, sine = lag_tables()
    flat = [tile for plane in band for tile in plane]
    return pl.pallas_call(
        functools.partial(correlate_body, rows=rows),
        out_shape=jax.ShapeDtypeStruct((channels, LAGS, NB, channels), HALF),
        grid=(channels // rows,),
        in_specs=[
            pl.BlockSpec(memory_space=pltpu.SMEM),
            pl.BlockSpec((rows, NF), lambda i: (i, 0)),
            pl.BlockSpec((rows, NF), lambda i: (i, 0)),
            pl.BlockSpec((LAGS, NF), lambda i: (0, 0)),
            pl.BlockSpec((LAGS, NF), lambda i: (0, 0)),
        ]
        + [pl.BlockSpec(memory_space=pl.ANY)] * len(flat),
        out_specs=pl.BlockSpec((rows, LAGS, NB, channels), lambda i: (i, 0, 0, 0)),
        scratch_shapes=[
            pltpu.VMEM((NB, channels, 2 * NF), HALF),
            pltpu.VMEM((LAGS * rows, 2 * NF), HALF),
            pltpu.VMEM((channels // LANES, rows * LAGS * NB, LANES), FLOAT),
            pltpu.SemaphoreType.DMA((NB,)),
        ],
        compiler_params=pltpu.CompilerParams(vmem_limit_bytes=32 << 20),
        name="correlate",
    )(place, real, imag, jnp.asarray(cosine), jnp.asarray(sine), *flat)


def shards(raw, fir_taps, band_width, dead_count):
    tiles = lax.axis_size("row")
    if raw.shape[1] == DEC * LANES:
        blocks = filter_blocks(raw, fir_taps, tiles)
        blocks = lax.all_to_all(blocks, "row", split_axis=0, concat_axis=0, tiled=True)
    else:
        channel_block = lax.all_to_all(raw, "row", split_axis=0, concat_axis=1, tiled=True)
        blocks = filter_whole(channel_block, fir_taps)
    white, real, imag = whiten(blocks, dead_count)
    band = gather_band(white)
    place = jnp.stack([lax.axis_index("row").astype(jnp.int32) % PLANE, band_width[0]])
    return correlate(real, imag, band, place)


def solution(mesh):
    return jax.shard_map(
        shards,
        mesh=mesh,
        in_specs=(P(None, ("win", "row")), P(), P("row"), P("row")),
        out_specs=P(("win", "row"), None, None, None),
        check_vma=False,
    )
```

time: 295 us -> 124 us (0.42)
  the two profiles are of different devices: /device:TPU:1 before, /device:TPU:3 now
where the time goes in v1:
time: 124 us; the launch traced here: 122 us
  waiting for transfers between devices  50 us (40%)
  Pallas kernels  34.2 us (28%)
  starting transfers between devices  29.3 us (24%)
  local copies, waits for them, and re-layouts  6.89 us (6%)
  between operations  1.4 us (1%)
    ppermute x11, waiting for transfers between devices, send(): return lax.ppermute(value, 'row', pairs)  26.5 us
    pallas_call x1, Pallas kernels, correlate(): pl.pallas_call(functools.partial(correlate_body, rows=rows), out_shape=ja...  25.9 us
    all_to_all x1, waiting for transfers between devices, shards(): lax.all_to_all(blocks, 'row', split_axis=0, concat_axis=0, tiled=True)  23.5 us
    ppermute x11, starting transfers between devices, send(): return lax.ppermute(value, 'row', pairs)  22.5 us
    unnamed x20, local copies, waits for them, and re-layouts  6.89 us
    all_to_all x1, starting transfers between devices, shards(): lax.all_to_all(blocks, 'row', split_axis=0, concat_axis=0, tiled=True)  6.8 us
    pallas_call x1, Pallas kernels, filter_blocks(): pl.pallas_call(functools.partial(filter_body, channels=channels), out_sha...  5.38 us
    pallas_call x1, Pallas kernels, whiten(): pl.pallas_call(whiten_body, out_shape=(jax.ShapeDtypeStruct((channels, 2...  2.92 us
  transfers between devices with their start and end apart: 12, of which 6 were waited for; matrix products, arithmetic and copies ran while one was open for 0% of the time, Pallas kernels for 0%

profile of v1, /device:TPU:3, one launch (start us, length us, event | category | flops | bytes accessed | tf_op | source)
XLA Modules:
  0.0 121.8 jit_solution(750157461018249591)
XLA Ops:
  0.0 2.2 %copy-done = bf16[4096,512]{1,0:T(8,128)(2,1)S(1)} copy-done((bf16[4096,512]{1,0:T(8,128)(2,1)S(1)}, bf16[4096,512]{1,0:T(8,128)(2,1)}, u32[]{:S(2)}) %copy-start) | copy-done | bytes 4194328
  2.9 5.4 %filter.1 = bf16[16,264,128]{2,1,0:T(8,128)(2,1)} custom-call(f32[16]{0:T(128)S(1)} %copy-done.9, bf16[4096,512]{1,0:T(8,128)(2,1)S(1)} %copy-done), custom_call_target="tpu_custom_call" | custom-call | tf_op jit(solution)/shard_map/filter/pallas_call | solution.py:105
  8.2 6.8 %all-to-all-start = ((bf16[16,264,128]{2,1,0:T(8,128)(2,1)}), bf16[16,264,128]{2,1,0:T(8,128)(2,1)S(1)}, u32[]{:S(2)}, u32[]{:S(2)}) async-start(bf16[16,264,128]{2,1,0:T(8,128)(2,1)} %filter.1), calls=%async_computation | async-start | bytes 2162688 | tf_op jit(solution)/shard_map/all_to_all | solution.py:314
  15.7 23.5 %all-to-all-done.blocks = bf16[16,264,128]{2,1,0:T(8,128)(2,1)S(1)} async-done(((bf16[16,264,128]{2,1,0:T(8,128)(2,1)}), bf16[16,264,128]{2,1,0:T(8,128)(2,1)S(1)}, u32[]{:S(2)}, u32[]{:S(2)}) %all-to-all-start) | async-done | bytes 1081376 | tf_op jit(solution)/shard_map/all_to_all | solution.py:314
  39.2 2.2 %copy-done.1 = bf16[2048,1024]{1,0:T(8,128)(2,1)S(1)} copy-done((bf16[2048,1024]{1,0:T(8,128)(2,1)S(1)}, bf16[2048,1024]{1,0:T(8,128)(2,1)}, u32[]{:S(2)}) %copy-start.1) | copy-done | bytes 4194328
  41.4 2.9 %whiten.1 = (bf16[256,1024]{1,0:T(8,128)(2,1)S(1)}, f32[256,512]{1,0:T(8,128)S(1)}, f32[256,512]{1,0:T(8,128)S(1)}) custom-call(s32[1]{0:T(128)S(6)} %copy.12.dead, bf16[16,264,128]{2,1,0:T(8,128)(2,1)S(1)} %all-to-all-done.blocks, bf16[2048,1024]{1,0:T(8,128)(2,1)S(1)} %copy-done.1, bf16[128,1024]{1,0:T(8,128)(2,1)S(1)} %copy-done.5, ...), custom_call_target="tpu_custom_call" | custom-call | tf_op jit(solution)/shard_map/whiten/pallas_call | solution.py:181
  44.3 1.3 %collective-permute-start.3 = (bf16[256,1024]{1,0:T(8,128)(2,1)S(1)}, bf16[256,1024]{1,0:T(8,128)(2,1)S(1)}, u32[]{:S(2)}, u32[]{:S(2)}) collective-permute-start(bf16[256,1024]{1,0:T(8,128)(2,1)S(1)} %get-tuple-element.10.rest_0_), channel_id=1, source_target_pairs={{4,0},{5,1},{6,2},{7,3},{8,4},{9,5},{10,6},{11,7},{12,8},{13,9},{1... | collective-permute-start | bytes 1572872 | tf_op jit(solution)/shard_map/ppermute | solution.py:221
  45.6 15.5 %collective-permute-done.3.rest_4_ = bf16[256,1024]{1,0:T(8,128)(2,1)S(1)} collective-permute-done((bf16[256,1024]{1,0:T(8,128)(2,1)S(1)}, bf16[256,1024]{1,0:T(8,128)(2,1)S(1)}, u32[]{:S(2)}, u32[]{:S(2)}) %collective-permute-start.3) | collective-permute-done | bytes 524320 | tf_op jit(solution)/shard_map/ppermute | solution.py:221
  61.1 0.7 collective-permute-start.7
  61.8 2.9 %collective-permute-start.1 = (bf16[256,1024]{1,0:T(8,128)(2,1)S(1)}, bf16[256,1024]{1,0:T(8,128)(2,1)S(1)}, u32[]{:S(2)}, u32[]{:S(2)}) collective-permute-start(bf16[256,1024]{1,0:T(8,128)(2,1)S(1)} %get-tuple-element.10.rest_0_), channel_id=1, source_target_pairs={{2,0},{3,1},{6,4},{7,5},{10,8},{11,9},{14,12},{15,13},{18,16},{19,... | collective-permute-start | bytes 1572872 | tf_op jit(solution)/shard_map/ppermute | solution.py:221
  64.7 0.7 collective-permute-start
  65.4 1.3 %collective-permute-start.9 = (bf16[256,1024]{1,0:T(8,128)(2,1)S(1)}, bf16[256,1024]{1,0:T(8,128)(2,1)}, u32[]{:S(2)}, u32[]{:S(2)}) collective-permute-start(bf16[256,1024]{1,0:T(8,128)(2,1)S(1)} %collective-permute-done.7.rest_8_), channel_id=1, source_target_pairs={{0,2},{1,3},{4,6},{5,7},{8,10},{9,11},{12,14},{13,15},{16,18},{17,... | collective-permute-start | bytes 1572872 | tf_op jit(solution)/shard_map/ppermute | solution.py:221
  66.7 7.5 %collective-permute-start.4 = (bf16[256,1024]{1,0:T(8,128)(2,1)S(1)}, bf16[256,1024]{1,0:T(8,128)(2,1)}, u32[]{:S(2)}, u32[]{:S(2)}) collective-permute-start(bf16[256,1024]{1,0:T(8,128)(2,1)S(1)} %collective-permute-done.3.rest_4_), channel_id=1, source_target_pairs={{0,1},{1,0},{2,3},{3,2},{4,5},{5,4},{6,7},{7,6},{8,9},{9,8},{10,11... | collective-permute-start | bytes 1572872 | tf_op jit(solution)/shard_map/ppermute | solution.py:221
  74.2 1.3 %collective-permute-done.1.rest_2_ = bf16[256,1024]{1,0:T(8,128)(2,1)S(1)} collective-permute-done((bf16[256,1024]{1,0:T(8,128)(2,1)S(1)}, bf16[256,1024]{1,0:T(8,128)(2,1)S(1)}, u32[]{:S(2)}, u32[]{:S(2)}) %collective-permute-start.1) | collective-permute-done | bytes 524320 | tf_op jit(solution)/shard_map/ppermute | solution.py:221
  75.5 1.5 %collective-permute-start.2 = (bf16[256,1024]{1,0:T(8,128)(2,1)S(1)}, bf16[256,1024]{1,0:T(8,128)(2,1)}, u32[]{:S(2)}, u32[]{:S(2)}) collective-permute-start(bf16[256,1024]{1,0:T(8,128)(2,1)S(1)} %collective-permute-done.1.rest_2_), channel_id=1, source_target_pairs={{0,1},{1,0},{4,5},{5,4},{8,9},{9,8},{12,13},{13,12},{16,17},{17,16... | collective-permute-start | bytes 1572872 | tf_op jit(solution)/shard_map/ppermute | solution.py:221
  77.0 0.8 copy-done.2
  77.8 2.1 %collective-permute-start.8 = (bf16[256,1024]{1,0:T(8,128)(2,1)S(1)}, bf16[256,1024]{1,0:T(8,128)(2,1)}, u32[]{:S(2)}, u32[]{:S(2)}) collective-permute-start(bf16[256,1024]{1,0:T(8,128)(2,1)S(1)} %collective-permute-done.7.rest_8_), channel_id=1, source_target_pairs={{0,1},{1,0},{2,3},{3,2},{4,5},{5,4},{6,7},{7,6},{8,9},{9,8},{10,11... | collective-permute-start | bytes 1572872 | tf_op jit(solution)/shard_map/ppermute | solution.py:221
  79.8 6.9 %collective-permute-done.5.rest_6_ = bf16[256,1024]{1,0:T(8,128)(2,1)} collective-permute-done((bf16[256,1024]{1,0:T(8,128)(2,1)S(1)}, bf16[256,1024]{1,0:T(8,128)(2,1)}, u32[]{:S(2)}, u32[]{:S(2)}) %collective-permute-start.5) | collective-permute-done | bytes 524320 | tf_op jit(solution)/shard_map/ppermute | solution.py:221
  86.8 1.2 %collective-permute-start.6 = (bf16[256,1024]{1,0:T(8,128)(2,1)}, bf16[256,1024]{1,0:T(8,128)(2,1)}, u32[]{:S(2)}, u32[]{:S(2)}) collective-permute-start(bf16[256,1024]{1,0:T(8,128)(2,1)} %collective-permute-done.5.rest_6_), channel_id=1, source_target_pairs={{0,1},{1,0},{2,3},{3,2},{4,5},{5,4},{6,7},{7,6},{8,9},{9,8},{10,11... | collective-permute-start | bytes 1572872 | tf_op jit(solution)/shard_map/ppermute | solution.py:221
  88.0 1.7 %collective-permute-done.9.rest_10_ = bf16[256,1024]{1,0:T(8,128)(2,1)} collective-permute-done((bf16[256,1024]{1,0:T(8,128)(2,1)S(1)}, bf16[256,1024]{1,0:T(8,128)(2,1)}, u32[]{:S(2)}, u32[]{:S(2)}) %collective-permute-start.9) | collective-permute-done | bytes 524320 | tf_op jit(solution)/shard_map/ppermute | solution.py:221
  89.7 3.3 %collective-permute-start.10 = (bf16[256,1024]{1,0:T(8,128)(2,1)}, bf16[256,1024]{1,0:T(8,128)(2,1)}, u32[]{:S(2)}, u32[]{:S(2)}) collective-permute-start(bf16[256,1024]{1,0:T(8,128)(2,1)} %collective-permute-done.9.rest_10_), channel_id=1, source_target_pairs={{2,3},{3,2},{6,7},{7,6},{10,11},{11,10},{14,15},{15,14},{18,19},{1... | collective-permute-start | bytes 1572872 | tf_op jit(solution)/shard_map/ppermute | solution.py:221
  93.8 1.1 collective-permute-done.10.rest_11_
  94.9 1.0 copy-done.3
  95.9 25.9 %correlate.1 = bf16[256,8,8,256]{3,2,1,0:T(8,128)(2,1)} custom-call(s32[2]{0:T(128)S(1)} %pad_add_fusion.place, f32[256,512]{1,0:T(8,128)S(1)} %get-tuple-element.8.real, f32[256,512]{1,0:T(8,128)S(1)} %get-tuple-element.9.imag, f32[8,512]{1,0:T(8,128)S(1)} %copy-done.7, f32[8,512]{1,0:T(8,128)S(1)} %copy-done.6, ...), custom_call_target="tpu_custom_call" | custom-call | tf_op jit(solution)/shard_map/correlate/pallas_call | solution.py:286
  (24 shorter events, 0.8 us)
Async XLA Ops:
  0.0 39.2 %copy-start.8 = (f32[1,512]{1,0:T(1,128)S(1)}, f32[1,512]{1,0:T(1,128)}, u32[]{:S(2)}) copy-start(f32[1,512]{1,0:T(1,128)} %constant.32.clone.counts) | copy-start | bytes 6148
  0.0 2.2 %copy-start = (bf16[4096,512]{1,0:T(8,128)(2,1)S(1)}, bf16[4096,512]{1,0:T(8,128)(2,1)}, u32[]{:S(2)}) copy-start(bf16[4096,512]{1,0:T(8,128)(2,1)} %raw.1) | copy-start | bytes 12582916
  2.2 0.7 copy-start.9
  2.9 36.3 %copy-start.4 = (bf16[512,512]{1,0:T(8,128)(2,1)S(1)}, bf16[512,512]{1,0:T(8,128)(2,1)}, u32[]{:S(2)}) copy-start(bf16[512,512]{1,0:T(8,128)(2,1)} %constant.31.clone.window) | copy-start | bytes 1572868
  2.9 36.3 %copy-start.5 = (bf16[128,1024]{1,0:T(8,128)(2,1)S(1)}, bf16[128,1024]{1,0:T(8,128)(2,1)}, u32[]{:S(2)}) copy-start(bf16[128,1024]{1,0:T(8,128)(2,1)} %constant.30.clone.edge_table) | copy-start | bytes 786436
  8.2 86.6 %copy-start.6 = (f32[8,512]{1,0:T(8,128)S(1)}, f32[8,512]{1,0:T(8,128)}, u32[]{:S(2)}) copy-start(f32[8,512]{1,0:T(8,128)} %constant.34.clone.sine) | copy-start | bytes 49156
  8.2 86.6 %copy-start.7 = (f32[8,512]{1,0:T(8,128)S(1)}, f32[8,512]{1,0:T(8,128)}, u32[]{:S(2)}) copy-start(f32[8,512]{1,0:T(8,128)} %constant.33.clone.cosine) | copy-start | bytes 49156
  8.2 30.9 %all-to-all-start = ((bf16[16,264,128]{2,1,0:T(8,128)(2,1)}), bf16[16,264,128]{2,1,0:T(8,128)(2,1)S(1)}, u32[]{:S(2)}, u32[]{:S(2)}) async-start(bf16[16,264,128]{2,1,0:T(8,128)(2,1)} %filter.1), calls=%async_computation | async-start | bytes 2162688 | tf_op jit(solution)/shard_map/all_to_all | solution.py:314
  39.2 2.2 %copy-start.1 = (bf16[2048,1024]{1,0:T(8,128)(2,1)S(1)}, bf16[2048,1024]{1,0:T(8,128)(2,1)}, u32[]{:S(2)}) copy-start(bf16[2048,1024]{1,0:T(8,128)(2,1)} %constant.29.clone.table) | copy-start | bytes 12582916
  44.3 16.8 %collective-permute-start.3 = (bf16[256,1024]{1,0:T(8,128)(2,1)S(1)}, bf16[256,1024]{1,0:T(8,128)(2,1)S(1)}, u32[]{:S(2)}, u32[]{:S(2)}) collective-permute-start(bf16[256,1024]{1,0:T(8,128)(2,1)S(1)} %get-tuple-element.10.rest_0_), channel_id=1, source_target_pairs={{4,0},{5,1},{6,2},{7,3},{8,4},{9,5},{10,6},{11,7},{12,8},{13,9},{1... | collective-permute-start | bytes 1572872 | tf_op jit(solution)/shard_map/ppermute | solution.py:221
  61.1 4.3 %collective-permute-start.7 = (bf16[256,1024]{1,0:T(8,128)(2,1)S(1)}, bf16[256,1024]{1,0:T(8,128)(2,1)S(1)}, u32[]{:S(2)}, u32[]{:S(2)}) collective-permute-start(bf16[256,1024]{1,0:T(8,128)(2,1)S(1)} %collective-permute-done.3.rest_4_), channel_id=1, source_target_pairs={{4,0},{5,1},{6,2},{8,4},{9,5},{10,6},{12,8},{13,9},{14,10},{20,16}... | collective-permute-start | bytes 1572872 | tf_op jit(solution)/shard_map/ppermute | solution.py:221
  61.8 13.7 %collective-permute-start.1 = (bf16[256,1024]{1,0:T(8,128)(2,1)S(1)}, bf16[256,1024]{1,0:T(8,128)(2,1)S(1)}, u32[]{:S(2)}, u32[]{:S(2)}) collective-permute-start(bf16[256,1024]{1,0:T(8,128)(2,1)S(1)} %get-tuple-element.10.rest_0_), channel_id=1, source_target_pairs={{2,0},{3,1},{6,4},{7,5},{10,8},{11,9},{14,12},{15,13},{18,16},{19,... | collective-permute-start | bytes 1572872 | tf_op jit(solution)/shard_map/ppermute | solution.py:221
  64.7 12.3 %collective-permute-start = (bf16[256,1024]{1,0:T(8,128)(2,1)S(1)}, bf16[256,1024]{1,0:T(8,128)(2,1)S(1)}, u32[]{:S(2)}, u32[]{:S(2)}) collective-permute-start(bf16[256,1024]{1,0:T(8,128)(2,1)S(1)} %get-tuple-element.10.rest_0_), channel_id=1, source_target_pairs={{0,1},{1,0},{2,3},{3,2},{4,5},{5,4},{6,7},{7,6},{8,9},{9,8},{10,11... | collective-permute-start | bytes 1572872 | tf_op jit(solution)/shard_map/ppermute | solution.py:221
  65.4 21.4 %collective-permute-start.5 = (bf16[256,1024]{1,0:T(8,128)(2,1)S(1)}, bf16[256,1024]{1,0:T(8,128)(2,1)}, u32[]{:S(2)}, u32[]{:S(2)}) collective-permute-start(bf16[256,1024]{1,0:T(8,128)(2,1)S(1)} %collective-permute-done.3.rest_4_), channel_id=1, source_target_pairs={{0,2},{1,3},{2,0},{3,1},{4,6},{5,7},{6,4},{7,5},{8,10},{9,11},{10,... | collective-permute-start | bytes 1572872 | tf_op jit(solution)/shard_map/ppermute | solution.py:221
  65.4 24.3 %collective-permute-start.9 = (bf16[256,1024]{1,0:T(8,128)(2,1)S(1)}, bf16[256,1024]{1,0:T(8,128)(2,1)}, u32[]{:S(2)}, u32[]{:S(2)}) collective-permute-start(bf16[256,1024]{1,0:T(8,128)(2,1)S(1)} %collective-permute-done.7.rest_8_), channel_id=1, source_target_pairs={{0,2},{1,3},{4,6},{5,7},{8,10},{9,11},{12,14},{13,15},{16,18},{17,... | collective-permute-start | bytes 1572872 | tf_op jit(solution)/shard_map/ppermute | solution.py:221
  66.7 27.0 %collective-permute-start.4 = (bf16[256,1024]{1,0:T(8,128)(2,1)S(1)}, bf16[256,1024]{1,0:T(8,128)(2,1)}, u32[]{:S(2)}, u32[]{:S(2)}) collective-permute-start(bf16[256,1024]{1,0:T(8,128)(2,1)S(1)} %collective-permute-done.3.rest_4_), channel_id=1, source_target_pairs={{0,1},{1,0},{2,3},{3,2},{4,5},{5,4},{6,7},{7,6},{8,9},{9,8},{10,11... | collective-permute-start | bytes 1572872 | tf_op jit(solution)/shard_map/ppermute | solution.py:221
  75.5 18.2 %collective-permute-start.2 = (bf16[256,1024]{1,0:T(8,128)(2,1)S(1)}, bf16[256,1024]{1,0:T(8,128)(2,1)}, u32[]{:S(2)}, u32[]{:S(2)}) collective-permute-start(bf16[256,1024]{1,0:T(8,128)(2,1)S(1)} %collective-permute-done.1.rest_2_), channel_id=1, source_target_pairs={{0,1},{1,0},{4,5},{5,4},{8,9},{9,8},{12,13},{13,12},{16,17},{17,16... | collective-permute-start | bytes 1572872 | tf_op jit(solution)/shard_map/ppermute | solution.py:221
  77.0 0.8 copy-start.2
  77.8 16.0 %collective-permute-start.8 = (bf16[256,1024]{1,0:T(8,128)(2,1)S(1)}, bf16[256,1024]{1,0:T(8,128)(2,1)}, u32[]{:S(2)}, u32[]{:S(2)}) collective-permute-start(bf16[256,1024]{1,0:T(8,128)(2,1)S(1)} %collective-permute-done.7.rest_8_), channel_id=1, source_target_pairs={{0,1},{1,0},{2,3},{3,2},{4,5},{5,4},{6,7},{7,6},{8,9},{9,8},{10,11... | collective-permute-start | bytes 1572872 | tf_op jit(solution)/shard_map/ppermute | solution.py:221
  86.8 7.0 %collective-permute-start.6 = (bf16[256,1024]{1,0:T(8,128)(2,1)}, bf16[256,1024]{1,0:T(8,128)(2,1)}, u32[]{:S(2)}, u32[]{:S(2)}) collective-permute-start(bf16[256,1024]{1,0:T(8,128)(2,1)} %collective-permute-done.5.rest_6_), channel_id=1, source_target_pairs={{0,1},{1,0},{2,3},{3,2},{4,5},{5,4},{6,7},{7,6},{8,9},{9,8},{10,11... | collective-permute-start | bytes 1572872 | tf_op jit(solution)/shard_map/ppermute | solution.py:221
  89.7 5.2 %collective-permute-start.10 = (bf16[256,1024]{1,0:T(8,128)(2,1)}, bf16[256,1024]{1,0:T(8,128)(2,1)}, u32[]{:S(2)}, u32[]{:S(2)}) collective-permute-start(bf16[256,1024]{1,0:T(8,128)(2,1)} %collective-permute-done.9.rest_10_), channel_id=1, source_target_pairs={{2,3},{3,2},{6,7},{7,6},{10,11},{11,10},{14,15},{15,14},{18,19},{1... | collective-permute-start | bytes 1572872 | tf_op jit(solution)/shard_map/ppermute | solution.py:221
  94.9 1.0 copy-start.3

commit v2 on v1

--- a/solution.py
+++ b/solution.py
@@ -20,7 +20,6 @@
 LEFT = (TAPS - DEC) // 2
 LANES = 128
 EDGE = 8
-PLANE = 4
 FLOAT = jnp.float32
 HALF = jnp.bfloat16
 
@@ -115,7 +114,7 @@
             pltpu.VMEM((width, 2 * LANES), HALF),
             pltpu.VMEM((2 * EDGE, 2 * LANES), HALF),
         ],
-        compiler_params=pltpu.CompilerParams(vmem_limit_bytes=16 << 20),
+        compiler_params=pltpu.CompilerParams(vmem_limit_bytes=60 << 20),
         name="filter",
     )(fir_taps, raw)
 
@@ -203,7 +202,7 @@
             pltpu.VMEM((channels, 2 * NF), FLOAT),
             pltpu.VMEM((count * EDGE, LANES), FLOAT),
         ],
-        compiler_params=pltpu.CompilerParams(vmem_limit_bytes=32 << 20),
+        compiler_params=pltpu.CompilerParams(vmem_limit_bytes=24 << 20),
         name="whiten",
     )(
         dead,
@@ -215,96 +214,178 @@
     )
 
 
-def send(value, target, keep=lambda source: True):
+def send(value, shift, keep=lambda source: True):
     count = lax.axis_size("row")
-    pairs = [(s, target(s)) for s in range(count) if keep(s) and 0 <= target(s) < count]
+    pairs = [(s, s - shift(s)) for s in range(count) if keep(s) and 0 <= s - shift(s) < count]
     return lax.ppermute(value, "row", pairs)
 
 
-def gather_band(white):
-    planes = [white]
-    planes.append(send(white, lambda s: s - PLANE))
-    planes.append(send(planes[1], lambda s: s - PLANE, lambda s: s % PLANE != 3))
-    across = [
-        send(planes[0], lambda s: s ^ 2, lambda s: s & 2 == 2),
-        send(planes[1], lambda s: s ^ 2),
-        send(planes[2], lambda s: s ^ 2, lambda s: s & 2 == 0),
+def beside(value, keep=lambda source: True):
+    return send(value, lambda s: s - (s ^ 1), keep)
+
+
+def gather_first(white):
+    one = beside(white, lambda s: s % 2 == 1)
+    return one, send(white, lambda s: 4), send(white, lambda s: s - (s ^ 2))
+
+
+def gather_second(four, across):
+    two = send(across, lambda s: 4, lambda s: s & 2 == 2)
+    six = send(four, lambda s: 2)
+    return two, six, send(four, lambda s: 3, lambda s: s % 2 == 0)
+
+
+WHOLE = pl.BlockSpec(memory_space=pltpu.VMEM)
+SCALAR = pl.BlockSpec(memory_space=pltpu.SMEM)
+
+
+def pair(left, columns, band, offset):
+    product = lax.dot_general(
+        left, columns, (((1,), (1,)), ((), ())), preferred_element_type=FLOAT
+    )
+    scale = jnp.where(offset < band[0], 1.0 / math.sqrt(NF), 0.0)
+    return (product * scale).astype(HALF)
+
+
+def by_parity(even, odd):
+    return jnp.where(lax.axis_index("row") % 2 == 0, even, odd)
+
+
+def cost(channels, tiles):
+    return pl.CostEstimate(
+        flops=2 * LAGS * tiles * channels * channels * 2 * NF,
+        bytes_accessed=2 * LAGS * channels * (2 * NF + tiles * channels),
+        transcendentals=0,
+    )
+
+
+def own_body(band, real, imag, cosine, sine, white, lagged, out):
+    c, s = cosine[0], sine[0]
+    re, im = real[...], imag[...]
+    lagged[0, :, :NF] = (re * c - im * s).astype(HALF)
+    lagged[0, :, NF:] = (re * s + im * c).astype(HALF)
+    out[0] = pair(lagged[0], white[...], band, 0)
+
+
+def correlate_own(band, real, imag, white):
+    channels = real.shape[0]
+    cosine, sine = lag_tables()
+    return pl.pallas_call(
+        own_body,
+        out_shape=(
+            jax.ShapeDtypeStruct((LAGS, channels, 2 * NF), HALF),
+            jax.ShapeDtypeStruct((LAGS, channels, channels), HALF),
+        ),
+        grid=(LAGS,),
+        in_specs=[
+            SCALAR,
+            WHOLE,
+            WHOLE,
+            pl.BlockSpec((1, 1, NF), lambda i: (i, 0, 0)),
+            pl.BlockSpec((1, 1, NF), lambda i: (i, 0, 0)),
+            WHOLE,
+        ],
+        out_specs=(
+            pl.BlockSpec((1, channels, 2 * NF), lambda i: (i, 0, 0)),
+            pl.BlockSpec((1, channels, channels), lambda i: (i, 0, 0)),
+        ),
+        compiler_params=pltpu.CompilerParams(vmem_limit_bytes=16 << 20),
+        cost_estimate=cost(channels, 1),
+        name="correlate_own",
+    )(band, real, imag, jnp.asarray(cosine[:, None]), jnp.asarray(sine[:, None]), white)
+
+
+def near_body(band, lagged, one, four, four_beside, out):
+    left = lagged[pl.program_id(0)]
+    out[0, 0] = pair(left, four[...], band, 4)
+    out[1, 0] = pair(left, four_beside[...], band, by_parity(5, 3))
+    out[2, 0] = pair(left, one[...], band, 1)
+
+
+def correlate_near(band, lagged, one, four, four_beside):
+    channels = lagged.shape[1]
+    return pl.pallas_call(
+        near_body,
+        out_shape=jax.ShapeDtypeStruct((3, LAGS, channels, channels), HALF),
+        grid=(LAGS,),
+        in_specs=[SCALAR, WHOLE, WHOLE, WHOLE, WHOLE],
+        out_specs=pl.BlockSpec((3, 1, channels, channels), lambda i: (0, i, 0, 0)),
+        compiler_params=pltpu.CompilerParams(vmem_limit_bytes=16 << 20),
+        cost_estimate=cost(channels, 3),
+        name="correlate_near",
+    )(band, lagged, one, four, four_beside)
+
+
+EVEN = (0, 3, 7, 8, 1, 2, 4, 5)
+ODD = (0, 8, 7, 2, 1, 5, 4, 6)
+
+
+def far_body(
+    band, lagged, own, near, six, six_beside, seven, two, two_beside, across, across_beside,
+    out, columns, sems, *, rows,
+):
+    step = pl.program_id(0)
+    channels = six.shape[0]
+    near_side = lax.axis_index("row") & 2 == 0
+
+    @pl.when(step == 0)
+    def _():
+        for slot, (here, there) in enumerate(((across, two), (across_beside, two_beside))):
+
+            @pl.when(near_side)
+            def _():
+                pltpu.make_async_copy(here, columns.at[slot], sems.at[slot]).start()
+
+            @pl.when(jnp.logical_not(near_side))
+            def _():
+                pltpu.make_async_copy(there, columns.at[slot], sems.at[slot]).start()
+
+        for slot in range(2):
+            pltpu.make_async_copy(two, columns.at[slot], sems.at[slot]).wait()
+
+    at = pl.ds(pl.multiple_of(step * rows, rows), rows)
+    left = lagged[:, at, :].reshape(LAGS * rows, 2 * NF)
+    far = [
+        pair(left, tile, band, offset).reshape(LAGS, rows, channels)
+        for tile, offset in (
+            (six[...], 6),
+            (six_beside[...], by_parity(7, 5)),
+            (seven[...], 7),
+            (columns[0], 2),
+            (columns[1], by_parity(3, 1)),
+        )
     ]
-    beside = [send(plane, lambda s: s ^ 1) for plane in planes]
-    corner = [
-        send(across[0], lambda s: s ^ 1, lambda s: s & 2 == 0),
-        send(across[1], lambda s: s ^ 1),
-        send(across[2], lambda s: s ^ 1, lambda s: s & 2 == 2),
-    ]
-    return [[planes[p], beside[p], across[p], corner[p]] for p in range(3)]
-
-
-def correlate_body(place, real, imag, cosine, sine, *rest, rows):
-    band, out, columns, lagged, wide, sems = rest[:12], rest[12], *rest[13:]
-    channels = columns.shape[1]
-
-    @pl.when(pl.program_id(0) == 0)
-    def _():
-        for offset in range(NB):
-            for at in range(PLANE):
-                plane, index = divmod(at + offset, PLANE)
-
-                @pl.when(place[0] == at)
-                def _():
-                    source = band[plane * PLANE + (at ^ index)]
-                    pltpu.make_async_copy(source, columns.at[offset], sems.at[offset]).start()
-
-        for offset in range(NB):
-            pltpu.make_async_copy(band[0], columns.at[offset], sems.at[offset]).wait()
-
-    re, im = real[...], imag[...]
+    even_row = lax.axis_index("row") % 2 == 0
     for lag in range(LAGS):
-        c, s = cosine[lag : lag + 1, :], sine[lag : lag + 1, :]
-        lagged[pl.ds(lag * rows, rows), :NF] = (re * c - im * s).astype(HALF)
-        lagged[pl.ds(lag * rows, rows), NF:] = (re * s + im * c).astype(HALF)
-    for offset in range(NB):
-        scale = jnp.where(offset < place[1], 1.0 / math.sqrt(NF), 0.0)
-        product = lax.dot_general(
-            lagged[...], columns[offset], (((1,), (1,)), ((), ())), preferred_element_type=FLOAT
-        )
-        product = product * scale
-        for lag in range(LAGS):
-            part = product[lag * rows : (lag + 1) * rows]
-            for half in range(channels // LANES):
-                columns_at = slice(half * LANES, (half + 1) * LANES)
-                wide[half, pl.ds(lag * NB + offset, rows, LAGS * NB), :] = part[:, columns_at]
-    for half in range(channels // LANES):
-        block = wide[half].reshape(rows, LAGS, NB, LANES)
-        out[:, :, :, half * LANES : (half + 1) * LANES] = block.astype(HALF)
-
-
-def correlate(real, imag, band, place):
-    channels = real.shape[0]
+        for half in range(channels // LANES):
+            lanes = slice(half * LANES, (half + 1) * LANES)
+            planes = [own[lag, at, lanes]]
+            planes += [near[index, lag, at, lanes] for index in range(3)]
+            planes += [plane[lag, :, lanes] for plane in far]
+            ordered = [
+                planes[even] if even == odd else jnp.where(even_row, planes[even], planes[odd])
+                for even, odd in zip(EVEN, ODD)
+            ]
+            out[:, lag, :, lanes] = pltpu.einshape("kab->akb", jnp.stack(ordered))
+
+
+def correlate_far(band, lagged, own, near, *tiles):
+    channels = lagged.shape[1]
     rows = 32
-    cosine, sine = lag_tables()
-    flat = [tile for plane in band for tile in plane]
     return pl.pallas_call(
-        functools.partial(correlate_body, rows=rows),
+        functools.partial(far_body, rows=rows),
         out_shape=jax.ShapeDtypeStruct((channels, LAGS, NB, channels), HALF),
         grid=(channels // rows,),
-        in_specs=[
-            pl.BlockSpec(memory_space=pltpu.SMEM),
-            pl.BlockSpec((rows, NF), lambda i: (i, 0)),
-            pl.BlockSpec((rows, NF), lambda i: (i, 0)),
-            pl.BlockSpec((LAGS, NF), lambda i: (0, 0)),
-            pl.BlockSpec((LAGS, NF), lambda i: (0, 0)),
-        ]
-        + [pl.BlockSpec(memory_space=pl.ANY)] * len(flat),
+        in_specs=[SCALAR] + [WHOLE] * 3 + [WHOLE] * 3 + [pl.BlockSpec(memory_space=pl.ANY)] * 4,
         out_specs=pl.BlockSpec((rows, LAGS, NB, channels), lambda i: (i, 0, 0, 0)),
         scratch_shapes=[
-            pltpu.VMEM((NB, channels, 2 * NF), HALF),
-            pltpu.VMEM((LAGS * rows, 2 * NF), HALF),
-            pltpu.VMEM((channels // LANES, rows * LAGS * NB, LANES), FLOAT),
-            pltpu.SemaphoreType.DMA((NB,)),
-        ],
-        compiler_params=pltpu.CompilerParams(vmem_limit_bytes=32 << 20),
-        name="correlate",
-    )(place, real, imag, jnp.asarray(cosine), jnp.asarray(sine), *flat)
+            pltpu.VMEM((2, channels, 2 * NF), HALF),
+            pltpu.SemaphoreType.DMA((2,)),
+        ],
+        compiler_params=pltpu.CompilerParams(vmem_limit_bytes=24 << 20),
+        cost_estimate=cost(channels, 5),
+        name="correlate_far",
+    )(band, lagged, own, near, *tiles)
 
 
 def shards(raw, fir_taps, band_width, dead_count):
@@ -316,9 +397,17 @@
         channel_block = lax.all_to_all(raw, "row", split_axis=0, concat_axis=1, tiled=True)
         blocks = filter_whole(channel_block, fir_taps)
     white, real, imag = whiten(blocks, dead_count)
-    band = gather_band(white)
-    place = jnp.stack([lax.axis_index("row").astype(jnp.int32) % PLANE, band_width[0]])
-    return correlate(real, imag, band, place)
+    one, four, across = gather_first(white)
+    lagged, own = correlate_own(band_width, real, imag, white)
+    four, across, lagged = lax.optimization_barrier((four, across, lagged))
+    two, six, seven = gather_second(four, across)
+    across_beside = beside(across, lambda s: s & 2 == 0)
+    near = correlate_near(band_width, lagged, one, four, beside(four))
+    two, six, seven, near = lax.optimization_barrier((two, six, seven, near))
+    two_beside = beside(two, lambda s: s & 2 == 2)
+    return correlate_far(
+        band_width, lagged, own, near, six, beside(six), seven, two, two_beside, across, across_beside
+    )
 
 
 def solution(mesh):

time: 124 us -> 101 us (0.81); the launches traced: 122 us -> 101 us
  starting transfers between devices: 29.3 us -> 20.9 us
  local copies, waits for them, and re-layouts: 6.89 us -> 2.2 us
  Pallas kernels: 34.2 us -> 30 us
  waiting for transfers between devices: 50 us -> 46.1 us
    ppermute x11 -> x10, starting transfers between devices: 22.5 us -> 14.1 us  [send(): return lax.ppermute(value, 'row', pairs)]
    pallas_call x1 -> x3, Pallas kernels: 25.9 us -> 19.4 us  [the longest x1 11.3 us: correlate_far(): pl.pallas_call(functools.partial(far_body, rows=rows), out_shape=jax.Shap...]
    unnamed x20 -> x12, local copies, waits for them, and re-layouts: 6.89 us -> 2.2 us
    ppermute x11 -> x10, waiting for transfers between devices: 26.5 us -> 22.7 us  [send(): return lax.ppermute(value, 'row', pairs)]
    pallas_call x1, Pallas kernels: 5.38 us -> 7.65 us  [filter_blocks(): pl.pallas_call(functools.partial(filter_body, channels=channels), out_sha...]
  transfers between devices with their start and end apart: 12 -> 11, of which waited for: 6 -> 6; matrix products, arithmetic and copies ran while one was open for 0% -> 0% of each run, Pallas kernels for 0% -> 8%
where the time goes in v2:
time: 101 us
  waiting for transfers between devices  46.1 us (46%)
  Pallas kernels  30 us (30%)
  starting transfers between devices  20.9 us (21%)
  local copies, waits for them, and re-layouts  2.2 us (2%)
  between operations  1.46 us (1%)
    all_to_all x1, waiting for transfers between devices, shards(): lax.all_to_all(blocks, 'row', split_axis=0, concat_axis=0, tiled=True)  23.5 us
    ppermute x10, waiting for transfers between devices, send(): return lax.ppermute(value, 'row', pairs)  22.7 us
    ppermute x10, starting transfers between devices, send(): return lax.ppermute(value, 'row', pairs)  14.1 us
    pallas_call x1, Pallas kernels, correlate_far(): pl.pallas_call(functools.partial(far_body, rows=rows), out_shape=jax.Shap...  11.3 us
    pallas_call x1, Pallas kernels, filter_blocks(): pl.pallas_call(functools.partial(filter_body, channels=channels), out_sha...  7.65 us
    all_to_all x1, starting transfers between devices, shards(): lax.all_to_all(blocks, 'row', split_axis=0, concat_axis=0, tiled=True)  6.8 us
    pallas_call x1, Pallas kernels, correlate_near(): pl.pallas_call(near_body, out_shape=jax.ShapeDtypeStruct((3, LAGS, channe...  5.08 us
    pallas_call x1, Pallas kernels, correlate_own(): pl.pallas_call(own_body, out_shape=(jax.ShapeDtypeStruct((LAGS, channels,...  2.99 us
  transfers between devices with their start and end apart: 11, of which 6 were waited for; matrix products, arithmetic and copies ran while one was open for 0% of the time, Pallas kernels for 8%

profile of v2, /device:TPU:3, one launch (start us, length us, event | category | flops | bytes accessed | tf_op | source)
XLA Modules:
  0.0 100.7 jit_solution(17723417960742042805)
XLA Ops:
  0.0 7.7 %filter.1 = bf16[16,264,128]{2,1,0:T(8,128)(2,1)} custom-call(f32[16]{0:T(128)} %taps.1, bf16[4096,512]{1,0:T(8,128)(2,1)} %raw.1), custom_call_target="tpu_custom_call" | custom-call | tf_op jit(solution)/shard_map/filter/pallas_call | solution.py:104
  7.7 6.8 %all-to-all-start = ((bf16[16,264,128]{2,1,0:T(8,128)(2,1)}), bf16[16,264,128]{2,1,0:T(8,128)(2,1)S(1)}, u32[]{:S(2)}, u32[]{:S(2)}) async-start(bf16[16,264,128]{2,1,0:T(8,128)(2,1)} %filter.1), calls=%async_computation | async-start | bytes 2162688 | tf_op jit(solution)/shard_map/all_to_all | solution.py:395
  15.1 23.5 %all-to-all-done.blocks = bf16[16,264,128]{2,1,0:T(8,128)(2,1)S(1)} async-done(((bf16[16,264,128]{2,1,0:T(8,128)(2,1)}), bf16[16,264,128]{2,1,0:T(8,128)(2,1)S(1)}, u32[]{:S(2)}, u32[]{:S(2)}) %all-to-all-start) | async-done | bytes 1081376 | tf_op jit(solution)/shard_map/all_to_all | solution.py:395
  38.6 0.0 copy-start
  38.6 2.2 %copy-done = bf16[2048,1024]{1,0:T(8,128)(2,1)S(1)} copy-done((bf16[2048,1024]{1,0:T(8,128)(2,1)S(1)}, bf16[2048,1024]{1,0:T(8,128)(2,1)}, u32[]{:S(2)}) %copy-start) | copy-done | bytes 4194328
  40.8 3.0 %whiten.1 = (bf16[256,1024]{1,0:T(8,128)(2,1)S(1)}, f32[256,512]{1,0:T(8,128)S(1)}, f32[256,512]{1,0:T(8,128)S(1)}) custom-call(s32[1]{0:T(128)S(6)} %copy.12.dead, bf16[16,264,128]{2,1,0:T(8,128)(2,1)S(1)} %all-to-all-done.blocks, bf16[2048,1024]{1,0:T(8,128)(2,1)S(1)} %copy-done, bf16[128,1024]{1,0:T(8,128)(2,1)S(1)} %copy-done.2, ...), custom_call_target="tpu_custom_call" | custom-call | tf_op jit(solution)/shard_map/whiten/pallas_call | solution.py:180
  43.8 0.1 collective-permute-start.1
  43.8 1.3 %collective-permute-start = (bf16[256,1024]{1,0:T(8,128)(2,1)S(1)}, bf16[256,1024]{1,0:T(8,128)(2,1)S(1)}, u32[]{:S(2)}, u32[]{:S(2)}) collective-permute-start(bf16[256,1024]{1,0:T(8,128)(2,1)S(1)} %get-tuple-element.17.white), channel_id=1, source_target_pairs={{4,0},{5,1},{6,2},{7,3},{8,4},{9,5},{10,6},{11,7},{12,8},{13,9},{1... | collective-permute-start | bytes 1572872 | tf_op jit(solution)/shard_map/ppermute | solution.py:220
  45.8 1.7 %collective-permute-start.5 = (bf16[256,1024]{1,0:T(8,128)(2,1)S(1)}, bf16[256,1024]{1,0:T(8,128)(2,1)S(1)}, u32[]{:S(2)}, u32[]{:S(2)}) collective-permute-start(bf16[256,1024]{1,0:T(8,128)(2,1)S(1)} %get-tuple-element.17.white), channel_id=1, source_target_pairs={{1,0},{3,2},{5,4},{7,6},{9,8},{11,10},{13,12},{15,14},{17,16},{19,... | collective-permute-start | bytes 1572872 | tf_op jit(solution)/shard_map/ppermute | solution.py:220
  47.6 3.0 %correlate_own.1 = (bf16[8,256,1024]{2,1,0:T(8,128)(2,1)S(1)}, bf16[8,256,256]{2,1,0:T(8,128)(2,1)S(1)}) custom-call(s32[1]{0:T(128)S(6)} %copy.11.band, f32[256,512]{1,0:T(8,128)S(1)} %get-tuple-element.18.real, f32[256,512]{1,0:T(8,128)S(1)} %get-tuple-element.19.imag, f32[8,1,512]{2,1,0:T(1,128)S(1)} %copy-done.5, f32[8,1,512]{2,1,0:T(1,128)S(1)} %copy-done.4, ...), custom_call_target="tpu_custom_call" | custom-call | flops 1073741824 | bytes 5242880 | tf_op jit(solution)/shard_map/correlate_own/pallas_call | solution.py:273
  50.6 7.0 %collective-permute-done.1.across = bf16[256,1024]{1,0:T(8,128)(2,1)S(1)} collective-permute-done((bf16[256,1024]{1,0:T(8,128)(2,1)S(1)}, bf16[256,1024]{1,0:T(8,128)(2,1)S(1)}, u32[]{:S(2)}, u32[]{:S(2)}) %collective-permute-start.1) | collective-permute-done | bytes 524320 | tf_op jit(solution)/shard_map/ppermute | solution.py:220
  57.6 3.3 %collective-permute-done.four = bf16[256,1024]{1,0:T(8,128)(2,1)S(1)} collective-permute-done((bf16[256,1024]{1,0:T(8,128)(2,1)S(1)}, bf16[256,1024]{1,0:T(8,128)(2,1)S(1)}, u32[]{:S(2)}, u32[]{:S(2)}) %collective-permute-start) | collective-permute-done | bytes 524320 | tf_op jit(solution)/shard_map/ppermute | solution.py:220
  60.9 0.6 collective-permute-start.6
  61.5 1.3 %collective-permute-start.2 = (bf16[256,1024]{1,0:T(8,128)(2,1)S(1)}, bf16[256,1024]{1,0:T(8,128)(2,1)S(1)}, u32[]{:S(2)}, u32[]{:S(2)}) collective-permute-start(bf16[256,1024]{1,0:T(8,128)(2,1)S(1)} %collective-permute-done.1.across), channel_id=1, source_target_pairs={{6,2},{7,3},{10,6},{11,7},{14,10},{15,11},{22,18},{23,19},{26,22},... | collective-permute-start | bytes 1572872 | tf_op jit(solution)/shard_map/ppermute | solution.py:220
  62.8 1.3 %collective-permute-start.4 = (bf16[256,1024]{1,0:T(8,128)(2,1)S(1)}, bf16[256,1024]{1,0:T(8,128)(2,1)S(1)}, u32[]{:S(2)}, u32[]{:S(2)}) collective-permute-start(bf16[256,1024]{1,0:T(8,128)(2,1)S(1)} %collective-permute-done.four), channel_id=1, source_target_pairs={{4,1},{6,3},{8,5},{10,7},{12,9},{14,11},{20,17},{22,19},{24,21},{2... | collective-permute-start | bytes 1572872 | tf_op jit(solution)/shard_map/ppermute | solution.py:220
  64.1 2.6 %collective-permute-start.3 = (bf16[256,1024]{1,0:T(8,128)(2,1)S(1)}, bf16[256,1024]{1,0:T(8,128)(2,1)S(1)}, u32[]{:S(2)}, u32[]{:S(2)}) collective-permute-start(bf16[256,1024]{1,0:T(8,128)(2,1)S(1)} %collective-permute-done.four), channel_id=1, source_target_pairs={{2,0},{3,1},{4,2},{5,3},{6,4},{7,5},{8,6},{9,7},{10,8},{11,9},{12,... | collective-permute-start | bytes 1572872 | tf_op jit(solution)/shard_map/ppermute | solution.py:220
  66.7 0.7 collective-permute-start.9
  67.4 5.1 %correlate_near.1.near = bf16[3,8,256,256]{3,2,1,0:T(8,128)(2,1)S(1)} custom-call(s32[1]{0:T(128)S(6)} %copy.11.band, bf16[8,256,1024]{2,1,0:T(8,128)(2,1)S(1)} %get-tuple-element.21.lagged, bf16[256,1024]{1,0:T(8,128)(2,1)S(1)} %collective-permute-done.5.one, bf16[256,1024]{1,0:T(8,128)(2,1)S(1)} %collective-permute-done.four, ...), custom_call_target="tpu_custom_call" | custom-call | flops 3221225472 | bytes 7340032 | tf_op jit(solution)/shard_map/correlate_near/pallas_call | solution.py:307
  72.5 4.5 %collective-permute-done.2.two = bf16[256,1024]{1,0:T(8,128)(2,1)S(1)} collective-permute-done((bf16[256,1024]{1,0:T(8,128)(2,1)S(1)}, bf16[256,1024]{1,0:T(8,128)(2,1)S(1)}, u32[]{:S(2)}, u32[]{:S(2)}) %collective-permute-start.2) | collective-permute-done | bytes 524320 | tf_op jit(solution)/shard_map/ppermute | solution.py:220
  76.9 6.0 %collective-permute-done.4.seven = bf16[256,1024]{1,0:T(8,128)(2,1)S(1)} collective-permute-done((bf16[256,1024]{1,0:T(8,128)(2,1)S(1)}, bf16[256,1024]{1,0:T(8,128)(2,1)S(1)}, u32[]{:S(2)}, u32[]{:S(2)}) %collective-permute-start.4) | collective-permute-done | bytes 524320 | tf_op jit(solution)/shard_map/ppermute | solution.py:220
  83.0 2.6 %collective-permute-start.7 = (bf16[256,1024]{1,0:T(8,128)(2,1)S(1)}, bf16[256,1024]{1,0:T(8,128)(2,1)S(1)}, u32[]{:S(2)}, u32[]{:S(2)}) collective-permute-start(bf16[256,1024]{1,0:T(8,128)(2,1)S(1)} %collective-permute-done.3.six), channel_id=1, source_target_pairs={{0,1},{1,0},{2,3},{3,2},{4,5},{5,4},{6,7},{7,6},{8,9},{9,8},{10,11... | collective-permute-start | bytes 1572872 | tf_op jit(solution)/shard_map/ppermute | solution.py:220
  85.6 1.9 %collective-permute-start.8 = (bf16[256,1024]{1,0:T(8,128)(2,1)S(1)}, bf16[256,1024]{1,0:T(8,128)(2,1)S(1)}, u32[]{:S(2)}, u32[]{:S(2)}) collective-permute-start(bf16[256,1024]{1,0:T(8,128)(2,1)S(1)} %collective-permute-done.2.two), channel_id=1, source_target_pairs={{2,3},{3,2},{6,7},{7,6},{10,11},{11,10},{14,15},{15,14},{18,19},{1... | collective-permute-start | bytes 1572872 | tf_op jit(solution)/shard_map/ppermute | solution.py:220
  87.5 1.9 %collective-permute-done.8.two_beside = bf16[256,1024]{1,0:T(8,128)(2,1)S(1)} collective-permute-done((bf16[256,1024]{1,0:T(8,128)(2,1)S(1)}, bf16[256,1024]{1,0:T(8,128)(2,1)S(1)}, u32[]{:S(2)}, u32[]{:S(2)}) %collective-permute-start.8) | collective-permute-done | bytes 524320 | tf_op jit(solution)/shard_map/ppermute | solution.py:220
  89.4 11.3 %correlate_far.1 = bf16[256,8,8,256]{3,2,1,0:T(8,128)(2,1)} custom-call(s32[1]{0:T(128)S(6)} %copy.11.band, bf16[8,256,1024]{2,1,0:T(8,128)(2,1)S(1)} %get-tuple-element.21.lagged, bf16[8,256,256]{2,1,0:T(8,128)(2,1)S(1)} %get-tuple-element.22.own, bf16[3,8,256,256]{3,2,1,0:T(8,128)(2,1)S(1)} %correlate_near.1.near, ...), custom_call_target="tpu_custom_call" | custom-call | flops 5368709120 | bytes 9437184 | tf_op jit(solution)/shard_map/correlate_far/pallas_call | solution.py:375
  (15 shorter events, 0.0 us)
Async XLA Ops:
  0.0 38.6 %copy-start.3 = (f32[1,512]{1,0:T(1,128)S(1)}, f32[1,512]{1,0:T(1,128)}, u32[]{:S(2)}) copy-start(f32[1,512]{1,0:T(1,128)} %constant.15.clone.counts) | copy-start | bytes 6148
  0.0 38.6 %copy-start.1 = (bf16[512,512]{1,0:T(8,128)(2,1)S(1)}, bf16[512,512]{1,0:T(8,128)(2,1)}, u32[]{:S(2)}) copy-start(bf16[512,512]{1,0:T(8,128)(2,1)} %constant.14.clone.window) | copy-start | bytes 1572868
  0.0 38.6 %copy-start.2 = (bf16[128,1024]{1,0:T(8,128)(2,1)S(1)}, bf16[128,1024]{1,0:T(8,128)(2,1)}, u32[]{:S(2)}) copy-start(bf16[128,1024]{1,0:T(8,128)(2,1)} %constant.13.clone.edge_table) | copy-start | bytes 786436
  7.7 39.9 %copy-start.4 = (f32[8,1,512]{2,1,0:T(1,128)S(1)}, f32[8,1,512]{2,1,0:T(1,128)}, u32[]{:S(2)}) copy-start(f32[8,1,512]{2,1,0:T(1,128)} %constant.17.clone.sine) | copy-start | bytes 49156
  7.7 39.9 %copy-start.5 = (f32[8,1,512]{2,1,0:T(1,128)S(1)}, f32[8,1,512]{2,1,0:T(1,128)}, u32[]{:S(2)}) copy-start(f32[8,1,512]{2,1,0:T(1,128)} %constant.16.clone.cosine) | copy-start | bytes 49156
  7.7 30.9 %all-to-all-start = ((bf16[16,264,128]{2,1,0:T(8,128)(2,1)}), bf16[16,264,128]{2,1,0:T(8,128)(2,1)S(1)}, u32[]{:S(2)}, u32[]{:S(2)}) async-start(bf16[16,264,128]{2,1,0:T(8,128)(2,1)} %filter.1), calls=%async_computation | async-start | bytes 2162688 | tf_op jit(solution)/shard_map/all_to_all | solution.py:395
  38.6 2.2 %copy-start = (bf16[2048,1024]{1,0:T(8,128)(2,1)S(1)}, bf16[2048,1024]{1,0:T(8,128)(2,1)}, u32[]{:S(2)}) copy-start(bf16[2048,1024]{1,0:T(8,128)(2,1)} %constant.12.clone.table) | copy-start | bytes 12582916
  43.8 13.8 %collective-permute-start.1 = (bf16[256,1024]{1,0:T(8,128)(2,1)S(1)}, bf16[256,1024]{1,0:T(8,128)(2,1)S(1)}, u32[]{:S(2)}, u32[]{:S(2)}) collective-permute-start(bf16[256,1024]{1,0:T(8,128)(2,1)S(1)} %get-tuple-element.17.white), channel_id=1, source_target_pairs={{0,2},{1,3},{2,0},{3,1},{4,6},{5,7},{6,4},{7,5},{8,10},{9,11},{10,... | collective-permute-start | bytes 1572872 | tf_op jit(solution)/shard_map/ppermute | solution.py:220
  43.8 17.1 %collective-permute-start = (bf16[256,1024]{1,0:T(8,128)(2,1)S(1)}, bf16[256,1024]{1,0:T(8,128)(2,1)S(1)}, u32[]{:S(2)}, u32[]{:S(2)}) collective-permute-start(bf16[256,1024]{1,0:T(8,128)(2,1)S(1)} %get-tuple-element.17.white), channel_id=1, source_target_pairs={{4,0},{5,1},{6,2},{7,3},{8,4},{9,5},{10,6},{11,7},{12,8},{13,9},{1... | collective-permute-start | bytes 1572872 | tf_op jit(solution)/shard_map/ppermute | solution.py:220
  45.8 20.9 %collective-permute-start.5 = (bf16[256,1024]{1,0:T(8,128)(2,1)S(1)}, bf16[256,1024]{1,0:T(8,128)(2,1)S(1)}, u32[]{:S(2)}, u32[]{:S(2)}) collective-permute-start(bf16[256,1024]{1,0:T(8,128)(2,1)S(1)} %get-tuple-element.17.white), channel_id=1, source_target_pairs={{1,0},{3,2},{5,4},{7,6},{9,8},{11,10},{13,12},{15,14},{17,16},{19,... | collective-permute-start | bytes 1572872 | tf_op jit(solution)/shard_map/ppermute | solution.py:220
  60.9 6.5 %collective-permute-start.6 = (bf16[256,1024]{1,0:T(8,128)(2,1)S(1)}, bf16[256,1024]{1,0:T(8,128)(2,1)S(1)}, u32[]{:S(2)}, u32[]{:S(2)}) collective-permute-start(bf16[256,1024]{1,0:T(8,128)(2,1)S(1)} %collective-permute-done.four), channel_id=1, source_target_pairs={{0,1},{1,0},{2,3},{3,2},{4,5},{5,4},{6,7},{7,6},{8,9},{9,8},{10,11... | collective-permute-start | bytes 1572872 | tf_op jit(solution)/shard_map/ppermute | solution.py:220
  61.5 15.4 %collective-permute-start.2 = (bf16[256,1024]{1,0:T(8,128)(2,1)S(1)}, bf16[256,1024]{1,0:T(8,128)(2,1)S(1)}, u32[]{:S(2)}, u32[]{:S(2)}) collective-permute-start(bf16[256,1024]{1,0:T(8,128)(2,1)S(1)} %collective-permute-done.1.across), channel_id=1, source_target_pairs={{6,2},{7,3},{10,6},{11,7},{14,10},{15,11},{22,18},{23,19},{26,22},... | collective-permute-start | bytes 1572872 | tf_op jit(solution)/shard_map/ppermute | solution.py:220
  62.8 20.2 %collective-permute-start.4 = (bf16[256,1024]{1,0:T(8,128)(2,1)S(1)}, bf16[256,1024]{1,0:T(8,128)(2,1)S(1)}, u32[]{:S(2)}, u32[]{:S(2)}) collective-permute-start(bf16[256,1024]{1,0:T(8,128)(2,1)S(1)} %collective-permute-done.four), channel_id=1, source_target_pairs={{4,1},{6,3},{8,5},{10,7},{12,9},{14,11},{20,17},{22,19},{24,21},{2... | collective-permute-start | bytes 1572872 | tf_op jit(solution)/shard_map/ppermute | solution.py:220
  64.1 18.9 %collective-permute-start.3 = (bf16[256,1024]{1,0:T(8,128)(2,1)S(1)}, bf16[256,1024]{1,0:T(8,128)(2,1)S(1)}, u32[]{:S(2)}, u32[]{:S(2)}) collective-permute-start(bf16[256,1024]{1,0:T(8,128)(2,1)S(1)} %collective-permute-done.four), channel_id=1, source_target_pairs={{2,0},{3,1},{4,2},{5,3},{6,4},{7,5},{8,6},{9,7},{10,8},{11,9},{12,... | collective-permute-start | bytes 1572872 | tf_op jit(solution)/shard_map/ppermute | solution.py:220
  66.7 20.8 %collective-permute-start.9 = (bf16[256,1024]{1,0:T(8,128)(2,1)S(1)}, bf16[256,1024]{1,0:T(8,128)(2,1)S(1)}, u32[]{:S(2)}, u32[]{:S(2)}) collective-permute-start(bf16[256,1024]{1,0:T(8,128)(2,1)S(1)} %collective-permute-done.1.across), channel_id=1, source_target_pairs={{0,1},{1,0},{4,5},{5,4},{8,9},{9,8},{12,13},{13,12},{16,17},{17,16... | collective-permute-start | bytes 1572872 | tf_op jit(solution)/shard_map/ppermute | solution.py:220
  83.0 4.6 %collective-permute-start.7 = (bf16[256,1024]{1,0:T(8,128)(2,1)S(1)}, bf16[256,1024]{1,0:T(8,128)(2,1)S(1)}, u32[]{:S(2)}, u32[]{:S(2)}) collective-permute-start(bf16[256,1024]{1,0:T(8,128)(2,1)S(1)} %collective-permute-done.3.six), channel_id=1, source_target_pairs={{0,1},{1,0},{2,3},{3,2},{4,5},{5,4},{6,7},{7,6},{8,9},{9,8},{10,11... | collective-permute-start | bytes 1572872 | tf_op jit(solution)/shard_map/ppermute | solution.py:220
  85.6 3.8 %collective-permute-start.8 = (bf16[256,1024]{1,0:T(8,128)(2,1)S(1)}, bf16[256,1024]{1,0:T(8,128)(2,1)S(1)}, u32[]{:S(2)}, u32[]{:S(2)}) collective-permute-start(bf16[256,1024]{1,0:T(8,128)(2,1)S(1)} %collective-permute-done.2.two), channel_id=1, source_target_pairs={{2,3},{3,2},{6,7},{7,6},{10,11},{11,10},{14,15},{15,14},{18,19},{1... | collective-permute-start | bytes 1572872 | tf_op jit(solution)/shard_map/ppermute | solution.py:220

commit v3 on v2

--- a/solution.py
+++ b/solution.py
@@ -66,11 +66,20 @@
     return spread
 
 
-def filter_body(taps, raw, out, main, edge, *, channels):
+def filter_body(taps, raw, other, own, held, main, edge, sems, *, channels):
     width = raw.shape[1]
-
-    @pl.when(pl.program_id(0) == 0)
+    step = pl.program_id(0)
+    group = own.shape[0]
+    count = held.shape[0] // 2
+    chip = lax.axis_index("row") // 2
+    parity = lax.axis_index("row") % 2
+
+    @pl.when(step == 0)
     def _():
+        for slot in range(2 * count):
+            tile = (chip ^ (slot % count)) * 2 + (parity ^ (1 - slot // count))
+            at = pl.ds(pl.multiple_of(tile * channels, channels), channels)
+            pltpu.make_async_copy(raw.at[at], held.at[slot], sems.at[slot]).start()
         rows = lax.broadcasted_iota(jnp.int32, (width, LANES), 0)
         cols = lax.broadcasted_iota(jnp.int32, (width, LANES), 1)
         high, low = split(spread_taps(taps, rows - DEC * cols + LEFT))
@@ -83,40 +92,67 @@
         high, low = split(spread_taps(taps, lane - DEC * sample + LEFT))
         edge[...] = jnp.concatenate([high.astype(FLOAT), low.astype(FLOAT)], axis=0).astype(HALF)
 
-    for tile in range(out.shape[0]):
-        block = raw[pl.ds(tile * channels, channels), :]
-        product = jnp.dot(block, main[...], preferred_element_type=FLOAT)
-        out[tile, :channels, :] = (product[:, :LANES] + product[:, LANES:]).astype(HALF)
-        ends = jnp.concatenate([block[:, :LANES], block[:, width - LANES :]], axis=1)
-        partial = lax.dot_general(
-            edge[...], ends, (((1,), (1,)), ((), ())), preferred_element_type=FLOAT
-        )
-        partial = partial[:EDGE] + partial[EDGE:]
-        row = lax.broadcasted_iota(jnp.int32, (EDGE, LANES), 0)
-        picked = jnp.where(row < 4, partial[:, :LANES], partial[:, LANES:])
-        out[tile, channels:, :] = picked.astype(HALF)
+    def run(out):
+        slots = [step * group + index for index in range(group)]
+        for slot in slots:
+            pltpu.make_async_copy(raw.at[pl.ds(0, channels)], held.at[slot], sems.at[slot]).wait()
+        for index, slot in enumerate(slots):
+            block = held[slot]
+            product = jnp.dot(block, main[...], preferred_element_type=FLOAT)
+            out[index, :channels, :] = (product[:, :LANES] + product[:, LANES:]).astype(HALF)
+            ends = jnp.concatenate([block[:, :LANES], block[:, width - LANES :]], axis=1)
+            partial = lax.dot_general(
+                edge[...], ends, (((1,), (1,)), ((), ())), preferred_element_type=FLOAT
+            )
+            partial = partial[:EDGE] + partial[EDGE:]
+            row = lax.broadcasted_iota(jnp.int32, (EDGE, LANES), 0)
+            picked = jnp.where(row < 4, partial[:, :LANES], partial[:, LANES:])
+            out[index, channels:, :] = picked.astype(HALF)
+
+    half = pl.num_programs(0) // 2
+    pl.when(step < half)(lambda: run(other))
+    pl.when(step >= half)(lambda: run(own))
 
 
 def filter_blocks(raw, fir_taps, tiles):
     channels = raw.shape[0] // tiles
     width = raw.shape[1]
-    step = 2
+    chips = tiles // 2
+    group = 4
+    half = chips // group
+    block = (group, channels + EDGE, LANES)
     return pl.pallas_call(
         functools.partial(filter_body, channels=channels),
-        out_shape=jax.ShapeDtypeStruct((tiles, channels + EDGE, LANES), HALF),
-        grid=(tiles // step,),
+        out_shape=(jax.ShapeDtypeStruct((chips, channels + EDGE, LANES), HALF),) * 2,
+        grid=(2 * half,),
         in_specs=[
             pl.BlockSpec(memory_space=pltpu.SMEM),
-            pl.BlockSpec((step * channels, width), lambda i: (i, 0)),
+            pl.BlockSpec(memory_space=pl.ANY),
         ],
-        out_specs=pl.BlockSpec((step, channels + EDGE, LANES), lambda i: (i, 0, 0)),
+        out_specs=(
+            pl.BlockSpec(block, lambda i: (jnp.minimum(i, half - 1), 0, 0)),
+            pl.BlockSpec(block, lambda i: (jnp.maximum(i - half, 0), 0, 0)),
+        ),
         scratch_shapes=[
+            pltpu.VMEM((tiles, channels, width), HALF),
             pltpu.VMEM((width, 2 * LANES), HALF),
             pltpu.VMEM((2 * EDGE, 2 * LANES), HALF),
+            pltpu.SemaphoreType.DMA((tiles,)),
         ],
-        compiler_params=pltpu.CompilerParams(vmem_limit_bytes=60 << 20),
+        compiler_params=pltpu.CompilerParams(vmem_limit_bytes=58 << 20),
         name="filter",
     )(fir_taps, raw)
+
+
+def transpose_blocks(raw, fir_taps, tiles):
+    other, own = filter_blocks(raw, fir_taps, tiles)
+    came = lax.ppermute(other, "row", [(s, s ^ 1) for s in range(tiles)])
+    pieces = [jnp.concatenate([own[d], came[d]], axis=0) for d in range(tiles // 2)]
+    pieces = lax.optimization_barrier(pieces)
+    return pieces[:1] + [
+        lax.ppermute(pieces[d], "row", [(s, s ^ (2 * d)) for s in range(tiles)])
+        for d in range(1, tiles // 2)
+    ]
 
 
 def filter_whole(channel_block, fir_taps):
@@ -129,88 +165,78 @@
         begin = first_at // DEC
         filtered = filtered + fir_taps[tap] * phased[first_at % DEC, :, begin : begin + NT]
     blocks = filtered.astype(HALF).reshape(rows, NT // LANES, LANES).transpose(1, 0, 2)
-    return jnp.concatenate([blocks, jnp.zeros((NT // LANES, EDGE, LANES), HALF)], axis=1)
-
-
-def whiten_body(dead, blocks, table, edge_table, window, counts, white, real, imag, total, ends):
-    step = pl.program_id(0)
-    group = blocks.shape[0]
+    blocks = jnp.concatenate([blocks, jnp.zeros((NT // LANES, EDGE, LANES), HALF)], axis=1)
+    return [blocks[d : d + 2].reshape(-1, LANES) for d in range(0, NT // LANES, 2)]
+
+
+def whiten_body(dead, table, edge_table, window, counts, *rest, count, ordered):
+    pieces, white, real, imag, ends = rest[:count], *rest[count:]
     channels = white.shape[0]
-    left = jnp.concatenate([blocks[i, :channels, :] for i in range(group)], axis=1)
-    part = jnp.dot(left, table[...], preferred_element_type=FLOAT)
-    for i in range(group):
-        at = pl.multiple_of((step * group + i) * EDGE, EDGE)
-        ends[pl.ds(at, EDGE), :] = blocks[i, channels:, :].astype(FLOAT)
-
-    @pl.when(step == 0)
-    def _():
-        total[...] = part
-
-    @pl.when(step > 0)
-    def _():
-        total[...] += part
-
-    @pl.when(step == pl.num_programs(0) - 1)
-    def _():
-        turned = ends[...].T
-        lane = lax.broadcasted_iota(jnp.int32, turned.shape, 1) % EDGE
-        first = jnp.where(lane < 4, turned, 0.0)
-        second = jnp.where(lane < 4, 0.0, turned)
-        edges = jnp.concatenate([first, second], axis=0).astype(HALF)
-        spectrum = total[...] + jnp.dot(edges, edge_table[...], preferred_element_type=FLOAT)
-        channel = lax.broadcasted_iota(jnp.int32, spectrum.shape, 0)
-        spectrum = jnp.where(channel < dead[0], 0.0, spectrum)
-        re, im = spectrum[:, :NF], spectrum[:, NF:]
-        high, low = split(re * re + im * im)
-        summed = jnp.dot(high, window[...], preferred_element_type=FLOAT)
-        summed += jnp.dot(low, window[...], preferred_element_type=FLOAT)
-        factor = lax.rsqrt(summed / counts[...] + 1e-05)
-        re, im = re * factor, im * factor
-        real[...] = re
-        imag[...] = im
-        white[:, :NF] = re.astype(HALF)
-        white[:, NF:] = im.astype(HALF)
-
-
-def whiten(blocks, dead):
-    count, height, _ = blocks.shape
-    channels = height - EDGE
-    group = 4
+    height = channels + EDGE
+    chip = 0 if ordered else lax.axis_index("row") // 2
+    parity = 0 if ordered else lax.axis_index("row") % 2
+
+    spectrum = jnp.zeros((channels, 2 * NF), FLOAT)
+    for index, piece in enumerate(pieces):
+        source = index if ordered else chip ^ index
+        mine, other = piece[:channels, :], piece[height : height + channels, :]
+        if ordered:
+            left = jnp.concatenate([mine, other], axis=1)
+        else:
+            left = jnp.concatenate(
+                [jnp.where(parity == 0, mine, other), jnp.where(parity == 0, other, mine)], axis=1
+            )
+        for part in range(2):
+            block = source * 2 + (part if ordered else part ^ parity)
+            at = pl.ds(pl.multiple_of(block * EDGE, EDGE), EDGE)
+            ends[at, :] = piece[part * height + channels : (part + 1) * height, :].astype(FLOAT)
+        at = pl.ds(pl.multiple_of(source * (2 * LANES), 2 * LANES), 2 * LANES)
+        spectrum += jnp.dot(left, table[at, :], preferred_element_type=FLOAT)
+
+    turned = ends[...].T
+    lane = lax.broadcasted_iota(jnp.int32, turned.shape, 1) % EDGE
+    first = jnp.where(lane < 4, turned, 0.0)
+    second = jnp.where(lane < 4, 0.0, turned)
+    edges = jnp.concatenate([first, second], axis=0).astype(HALF)
+    spectrum += jnp.dot(edges, edge_table[...], preferred_element_type=FLOAT)
+    channel = lax.broadcasted_iota(jnp.int32, spectrum.shape, 0)
+    spectrum = jnp.where(channel < dead[0], 0.0, spectrum)
+    re, im = spectrum[:, :NF], spectrum[:, NF:]
+    high, low = split(re * re + im * im)
+    summed = jnp.dot(high, window[...], preferred_element_type=FLOAT)
+    summed += jnp.dot(low, window[...], preferred_element_type=FLOAT)
+    factor = lax.rsqrt(summed / counts[...] + 1e-05)
+    re, im = re * factor, im * factor
+    real[...] = re
+    imag[...] = im
+    white[:, :NF] = re.astype(HALF)
+    white[:, NF:] = im.astype(HALF)
+
+
+def whiten(pieces, dead, ordered):
+    channels = pieces[0].shape[0] // 2 - EDGE
+    blocks = 2 * len(pieces)
     window, counts = window_table()
     return pl.pallas_call(
-        whiten_body,
+        functools.partial(whiten_body, count=len(pieces), ordered=ordered),
         out_shape=(
             jax.ShapeDtypeStruct((channels, 2 * NF), HALF),
             jax.ShapeDtypeStruct((channels, NF), FLOAT),
             jax.ShapeDtypeStruct((channels, NF), FLOAT),
         ),
-        grid=(count // group,),
-        in_specs=[
-            pl.BlockSpec(memory_space=pltpu.SMEM),
-            pl.BlockSpec((group, height, LANES), lambda i: (i, 0, 0)),
-            pl.BlockSpec((group * LANES, 2 * NF), lambda i: (i, 0)),
-            pl.BlockSpec((count * EDGE, 2 * NF), lambda i: (0, 0)),
-            pl.BlockSpec((NF, NF), lambda i: (0, 0)),
-            pl.BlockSpec((1, NF), lambda i: (0, 0)),
-        ],
-        out_specs=(
-            pl.BlockSpec((channels, 2 * NF), lambda i: (0, 0)),
-            pl.BlockSpec((channels, NF), lambda i: (0, 0)),
-            pl.BlockSpec((channels, NF), lambda i: (0, 0)),
-        ),
-        scratch_shapes=[
-            pltpu.VMEM((channels, 2 * NF), FLOAT),
-            pltpu.VMEM((count * EDGE, LANES), FLOAT),
-        ],
+        in_specs=[pl.BlockSpec(memory_space=pltpu.SMEM)]
+        + [pl.BlockSpec(memory_space=pltpu.VMEM)] * (4 + len(pieces)),
+        out_specs=(pl.BlockSpec(memory_space=pltpu.VMEM),) * 3,
+        scratch_shapes=[pltpu.VMEM((blocks * EDGE, LANES), FLOAT)],
         compiler_params=pltpu.CompilerParams(vmem_limit_bytes=24 << 20),
         name="whiten",
     )(
         dead,
-        blocks,
         jnp.asarray(table_rows(np.arange(NT))),
         jnp.asarray(table_rows(edge_samples())),
         jnp.asarray(window),
         jnp.asarray(counts),
+        *pieces,
     )
 
 
@@ -225,13 +251,14 @@
 
 
 def gather_first(white):
-    one = beside(white, lambda s: s % 2 == 1)
-    return one, send(white, lambda s: 4), send(white, lambda s: s - (s ^ 2))
+    four = send(white, lambda s: 4)
+    across = send(white, lambda s: s - (s ^ 2))
+    return beside(white, lambda s: s % 2 == 1), four, across
 
 
 def gather_second(four, across):
+    six = send(four, lambda s: 2)
     two = send(across, lambda s: 4, lambda s: s & 2 == 2)
-    six = send(four, lambda s: 2)
     return two, six, send(four, lambda s: 3, lambda s: s % 2 == 0)
 
 
@@ -391,12 +418,10 @@
 def shards(raw, fir_taps, band_width, dead_count):
     tiles = lax.axis_size("row")
     if raw.shape[1] == DEC * LANES:
-        blocks = filter_blocks(raw, fir_taps, tiles)
-        blocks = lax.all_to_all(blocks, "row", split_axis=0, concat_axis=0, tiled=True)
+        white, real, imag = whiten(transpose_blocks(raw, fir_taps, tiles), dead_count, False)
     else:
         channel_block = lax.all_to_all(raw, "row", split_axis=0, concat_axis=1, tiled=True)
-        blocks = filter_whole(channel_block, fir_taps)
-    white, real, imag = whiten(blocks, dead_count)
+        white, real, imag = whiten(filter_whole(channel_block, fir_taps), dead_count, True)
     one, four, across = gather_first(white)
     lagged, own = correlate_own(band_width, real, imag, white)
     four, across, lagged = lax.optimization_barrier((four, across, lagged))

time: 101 us -> 94.4 us (0.935)
  waiting for transfers between devices: 46.1 us -> 35.3 us
  starting transfers between devices: 20.9 us -> 28.3 us
  Pallas kernels: 30 us -> 27.1 us
    all_to_all x1 -> x0, waiting for transfers between devices: 23.5 us -> none  [shards(): lax.all_to_all(blocks, 'row', split_axis=0, concat_axis=0, tiled=True)]
    ppermute x0 -> x8, waiting for transfers between devices: none -> 12.9 us  [the longest x7 12.3 us: transpose_blocks(): lax.ppermute(pieces[d], 'row', [(s, s ^ 2 * d) for s in range(tiles)])]
    ppermute x0 -> x8, starting transfers between devices: none -> 10.1 us  [the longest x7 9.36 us: transpose_blocks(): lax.ppermute(pieces[d], 'row', [(s, s ^ 2 * d) for s in range(tiles)])]
    all_to_all x1 -> x0, starting transfers between devices: 6.8 us -> none  [shards(): lax.all_to_all(blocks, 'row', split_axis=0, concat_axis=0, tiled=True)]
    ppermute x10, starting transfers between devices: 14.1 us -> 18.2 us  [send(): return lax.ppermute(value, 'row', pairs)]
    unnamed x12, local copies, waits for them, and re-layouts: 2.2 us -> 0.03 us
    pallas_call x1, Pallas kernels: 7.65 us -> 5.85 us  [filter_blocks(): pl.pallas_call(functools.partial(filter_body, channels=channels), out_sha...]
    squeeze x0 -> x2, local copies, waits for them, and re-layouts: none -> 1.19 us  [the longest x1 1.15 us: transpose_blocks(): own[d]]
  transfers between devices with their start and end apart: 11 -> 18, of which waited for: 6 -> 8; matrix products, arithmetic and copies ran while one was open for 0% -> 1% of each run, Pallas kernels for 8% -> 9%
where the time goes in v3:
time: 94.4 us; the launch traced here: 93.5 us
  waiting for transfers between devices  35.3 us (37%)
  starting transfers between devices  28.3 us (30%)
  Pallas kernels  27.1 us (29%)
  between operations  1.54 us (2%)
  local copies, waits for them, and re-layouts  1.22 us (1%)
    ppermute x10, waiting for transfers between devices, send(): return lax.ppermute(value, 'row', pairs)  22.5 us
    ppermute x10, starting transfers between devices, send(): return lax.ppermute(value, 'row', pairs)  18.2 us
    ppermute x7, waiting for transfers between devices, transpose_blocks(): lax.ppermute(pieces[d], 'row', [(s, s ^ 2 * d) for s in range(tiles)])  12.3 us
    pallas_call x1, Pallas kernels, correlate_far(): pl.pallas_call(functools.partial(far_body, rows=rows), out_shape=jax.Shap...  11.3 us
    ppermute x7, starting transfers between devices, transpose_blocks(): lax.ppermute(pieces[d], 'row', [(s, s ^ 2 * d) for s in range(tiles)])  9.36 us
    pallas_call x1, Pallas kernels, filter_blocks(): pl.pallas_call(functools.partial(filter_body, channels=channels), out_sha...  5.85 us
    pallas_call x1, Pallas kernels, correlate_near(): pl.pallas_call(near_body, out_shape=jax.ShapeDtypeStruct((3, LAGS, channe...  5.08 us
    pallas_call x1, Pallas kernels, correlate_own(): pl.pallas_call(own_body, out_shape=(jax.ShapeDtypeStruct((LAGS, channels,...  2.99 us
  transfers between devices with their start and end apart: 18, of which 8 were waited for; matrix products, arithmetic and copies ran while one was open for 1% of the time, Pallas kernels for 9%

profile of v3, /device:TPU:3, one launch (start us, length us, event | category | flops | bytes accessed | tf_op | source)
XLA Modules:
  0.0 93.5 jit_solution(7061625481567042124)
XLA Ops:
  0.0 5.8 %filter.1 = (bf16[8,264,128]{2,1,0:T(8,128)(2,1)}, bf16[8,264,128]{2,1,0:T(8,128)(2,1)}) custom-call(f32[16]{0:T(128)} %taps.1, bf16[4096,512]{1,0:T(8,128)(2,1)} %raw.1), custom_call_target="tpu_custom_call" | custom-call | tf_op jit(solution)/shard_map/filter/pallas_call | solution.py:124
  8.6 1.5 %collective-permute-start.2 = (bf16[528,128]{1,0:T(8,128)(2,1)S(1)}, bf16[528,128]{1,0:T(8,128)(2,1)S(1)}, u32[]{:S(2)}, u32[]{:S(2)}) collective-permute-start(bf16[528,128]{1,0:T(8,128)(2,1)S(1)} %get-tuple-element.31), channel_id=1, source_target_pairs={{0,4},{1,5},{2,6},{3,7},{4,0},{5,1},{6,2},{7,3},{8,12},{9,13},{10,... | collective-permute-start | bytes 405512 | tf_op jit(solution)/shard_map/ppermute | solution.py:153
  11.3 2.3 %collective-permute-start.4 = (bf16[528,128]{1,0:T(8,128)(2,1)S(1)}, bf16[528,128]{1,0:T(8,128)(2,1)S(1)}, u32[]{:S(2)}, u32[]{:S(2)}) collective-permute-start(bf16[528,128]{1,0:T(8,128)(2,1)S(1)} %get-tuple-element.33), channel_id=1, source_target_pairs={{0,8},{1,9},{2,10},{3,11},{4,12},{5,13},{6,14},{7,15},{8,0},{9,1},... | collective-permute-start | bytes 405512 | tf_op jit(solution)/shard_map/ppermute | solution.py:153
  13.6 3.3 %collective-permute-start.6 = (bf16[528,128]{1,0:T(8,128)(2,1)S(1)}, bf16[528,128]{1,0:T(8,128)(2,1)S(1)}, u32[]{:S(2)}, u32[]{:S(2)}) collective-permute-start(bf16[528,128]{1,0:T(8,128)(2,1)S(1)} %get-tuple-element.35), channel_id=1, source_target_pairs={{0,12},{1,13},{2,14},{3,15},{4,8},{5,9},{6,10},{7,11},{8,4},{9,5},... | collective-permute-start | bytes 405512 | tf_op jit(solution)/shard_map/ppermute | solution.py:153
  18.6 3.3 %collective-permute-done.3.rest_3_ = bf16[528,128]{1,0:T(8,128)(2,1)S(1)} collective-permute-done((bf16[528,128]{1,0:T(8,128)(2,1)S(1)}, bf16[528,128]{1,0:T(8,128)(2,1)S(1)}, u32[]{:S(2)}, u32[]{:S(2)}) %collective-permute-start.3) | collective-permute-done | bytes 135200 | tf_op jit(solution)/shard_map/ppermute | solution.py:153
  21.9 5.5 %collective-permute-done.6.rest_6_ = bf16[528,128]{1,0:T(8,128)(2,1)S(1)} collective-permute-done((bf16[528,128]{1,0:T(8,128)(2,1)S(1)}, bf16[528,128]{1,0:T(8,128)(2,1)S(1)}, u32[]{:S(2)}, u32[]{:S(2)}) %collective-permute-start.6) | collective-permute-done | bytes 135200 | tf_op jit(solution)/shard_map/ppermute | solution.py:153
  27.4 3.5 %collective-permute-done.7.rest_7_ = bf16[528,128]{1,0:T(8,128)(2,1)S(1)} collective-permute-done((bf16[528,128]{1,0:T(8,128)(2,1)S(1)}, bf16[528,128]{1,0:T(8,128)(2,1)S(1)}, u32[]{:S(2)}, u32[]{:S(2)}) %collective-permute-start.7) | collective-permute-done | bytes 135200 | tf_op jit(solution)/shard_map/ppermute | solution.py:153
  30.9 1.9 %whiten.1 = (bf16[256,1024]{1,0:T(8,128)(2,1)S(1)}, f32[256,512]{1,0:T(8,128)S(1)}, f32[256,512]{1,0:T(8,128)S(1)}) custom-call(s32[1]{0:T(128)S(6)} %copy.12.dead, bf16[2048,1024]{1,0:T(8,128)(2,1)S(1)} %copy-done, bf16[128,1024]{1,0:T(8,128)(2,1)S(1)} %copy-done.2, bf16[512,512]{1,0:T(8,128)(2,1)S(1)} %copy-done.1, f32[1,512]{1,0:T(1,128)S(1)} %copy-done.3, ...), custom_call_target="tpu_custom_call" | custom-call | tf_op jit(solution)/shard_map/whiten/pallas_call | solution.py:220
  32.7 2.0 %collective-permute-start.9 = (bf16[256,1024]{1,0:T(8,128)(2,1)S(1)}, bf16[256,1024]{1,0:T(8,128)(2,1)S(1)}, u32[]{:S(2)}, u32[]{:S(2)}) collective-permute-start(bf16[256,1024]{1,0:T(8,128)(2,1)S(1)} %get-tuple-element.37.white), channel_id=1, source_target_pairs={{0,2},{1,3},{2,0},{3,1},{4,6},{5,7},{6,4},{7,5},{8,10},{9,11},{10,... | collective-permute-start | bytes 1572872 | tf_op jit(solution)/shard_map/ppermute | solution.py:246
  34.7 1.3 %collective-permute-start.8 = (bf16[256,1024]{1,0:T(8,128)(2,1)S(1)}, bf16[256,1024]{1,0:T(8,128)(2,1)S(1)}, u32[]{:S(2)}, u32[]{:S(2)}) collective-permute-start(bf16[256,1024]{1,0:T(8,128)(2,1)S(1)} %get-tuple-element.37.white), channel_id=1, source_target_pairs={{4,0},{5,1},{6,2},{7,3},{8,4},{9,5},{10,6},{11,7},{12,8},{13,9},{1... | collective-permute-start | bytes 1572872 | tf_op jit(solution)/shard_map/ppermute | solution.py:246
  36.7 4.4 %collective-permute-start.13 = (bf16[256,1024]{1,0:T(8,128)(2,1)S(1)}, bf16[256,1024]{1,0:T(8,128)(2,1)S(1)}, u32[]{:S(2)}, u32[]{:S(2)}) collective-permute-start(bf16[256,1024]{1,0:T(8,128)(2,1)S(1)} %get-tuple-element.37.white), channel_id=1, source_target_pairs={{1,0},{3,2},{5,4},{7,6},{9,8},{11,10},{13,12},{15,14},{17,16},{19,... | collective-permute-start | bytes 1572872 | tf_op jit(solution)/shard_map/ppermute | solution.py:246
  41.1 3.0 %correlate_own.1 = (bf16[8,256,1024]{2,1,0:T(8,128)(2,1)S(1)}, bf16[8,256,256]{2,1,0:T(8,128)(2,1)S(1)}) custom-call(s32[1]{0:T(128)S(6)} %copy.11.band, f32[256,512]{1,0:T(8,128)S(1)} %get-tuple-element.38.real, f32[256,512]{1,0:T(8,128)S(1)} %get-tuple-element.39.imag, f32[8,1,512]{2,1,0:T(1,128)S(1)} %copy-done.5, f32[8,1,512]{2,1,0:T(1,128)S(1)} %copy-done.4, ...), custom_call_target="tpu_custom_call" | custom-call | flops 1073741824 | bytes 5242880 | tf_op jit(solution)/shard_map/correlate_own/pallas_call | solution.py:300
  44.1 9.2 %collective-permute-done.8.four = bf16[256,1024]{1,0:T(8,128)(2,1)S(1)} collective-permute-done((bf16[256,1024]{1,0:T(8,128)(2,1)S(1)}, bf16[256,1024]{1,0:T(8,128)(2,1)S(1)}, u32[]{:S(2)}, u32[]{:S(2)}) %collective-permute-start.8) | collective-permute-done | bytes 524320 | tf_op jit(solution)/shard_map/ppermute | solution.py:246
  53.4 2.2 %collective-permute-start.14 = (bf16[256,1024]{1,0:T(8,128)(2,1)S(1)}, bf16[256,1024]{1,0:T(8,128)(2,1)S(1)}, u32[]{:S(2)}, u32[]{:S(2)}) collective-permute-start(bf16[256,1024]{1,0:T(8,128)(2,1)S(1)} %collective-permute-done.8.four), channel_id=1, source_target_pairs={{0,1},{1,0},{2,3},{3,2},{4,5},{5,4},{6,7},{7,6},{8,9},{9,8},{10,11... | collective-permute-start | bytes 1572872 | tf_op jit(solution)/shard_map/ppermute | solution.py:246
  55.6 1.3 %collective-permute-start.10 = (bf16[256,1024]{1,0:T(8,128)(2,1)S(1)}, bf16[256,1024]{1,0:T(8,128)(2,1)S(1)}, u32[]{:S(2)}, u32[]{:S(2)}) collective-permute-start(bf16[256,1024]{1,0:T(8,128)(2,1)S(1)} %collective-permute-done.9.across), channel_id=1, source_target_pairs={{6,2},{7,3},{10,6},{11,7},{14,10},{15,11},{22,18},{23,19},{26,22},... | collective-permute-start | bytes 1572872 | tf_op jit(solution)/shard_map/ppermute | solution.py:246
  56.9 1.3 %collective-permute-start.12 = (bf16[256,1024]{1,0:T(8,128)(2,1)S(1)}, bf16[256,1024]{1,0:T(8,128)(2,1)S(1)}, u32[]{:S(2)}, u32[]{:S(2)}) collective-permute-start(bf16[256,1024]{1,0:T(8,128)(2,1)S(1)} %collective-permute-done.8.four), channel_id=1, source_target_pairs={{4,1},{6,3},{8,5},{10,7},{12,9},{14,11},{20,17},{22,19},{24,21},{2... | collective-permute-start | bytes 1572872 | tf_op jit(solution)/shard_map/ppermute | solution.py:246
  58.2 1.9 %collective-permute-start.11 = (bf16[256,1024]{1,0:T(8,128)(2,1)S(1)}, bf16[256,1024]{1,0:T(8,128)(2,1)S(1)}, u32[]{:S(2)}, u32[]{:S(2)}) collective-permute-start(bf16[256,1024]{1,0:T(8,128)(2,1)S(1)} %collective-permute-done.8.four), channel_id=1, source_target_pairs={{2,0},{3,1},{4,2},{5,3},{6,4},{7,5},{8,6},{9,7},{10,8},{11,9},{12,... | collective-permute-start | bytes 1572872 | tf_op jit(solution)/shard_map/ppermute | solution.py:246
  60.8 5.1 %correlate_near.1.near = bf16[3,8,256,256]{3,2,1,0:T(8,128)(2,1)S(1)} custom-call(s32[1]{0:T(128)S(6)} %copy.11.band, bf16[8,256,1024]{2,1,0:T(8,128)(2,1)S(1)} %get-tuple-element.41.lagged, bf16[256,1024]{1,0:T(8,128)(2,1)S(1)} %collective-permute-done.13.one, bf16[256,1024]{1,0:T(8,128)(2,1)S(1)} %collective-permute-done.8.four, ...), custom_call_target="tpu_custom_call" | custom-call | flops 3221225472 | bytes 7340032 | tf_op jit(solution)/shard_map/correlate_near/pallas_call | solution.py:334
  65.9 5.5 %collective-permute-done.10.two = bf16[256,1024]{1,0:T(8,128)(2,1)S(1)} collective-permute-done((bf16[256,1024]{1,0:T(8,128)(2,1)S(1)}, bf16[256,1024]{1,0:T(8,128)(2,1)S(1)}, u32[]{:S(2)}, u32[]{:S(2)}) %collective-permute-start.10) | collective-permute-done | bytes 524320 | tf_op jit(solution)/shard_map/ppermute | solution.py:246
  71.4 5.8 %collective-permute-done.12.seven = bf16[256,1024]{1,0:T(8,128)(2,1)S(1)} collective-permute-done((bf16[256,1024]{1,0:T(8,128)(2,1)S(1)}, bf16[256,1024]{1,0:T(8,128)(2,1)S(1)}, u32[]{:S(2)}, u32[]{:S(2)}) %collective-permute-start.12) | collective-permute-done | bytes 524320 | tf_op jit(solution)/shard_map/ppermute | solution.py:246
  77.3 1.2 %collective-permute-start.15 = (bf16[256,1024]{1,0:T(8,128)(2,1)S(1)}, bf16[256,1024]{1,0:T(8,128)(2,1)S(1)}, u32[]{:S(2)}, u32[]{:S(2)}) collective-permute-start(bf16[256,1024]{1,0:T(8,128)(2,1)S(1)} %collective-permute-done.11.six), channel_id=1, source_target_pairs={{0,1},{1,0},{2,3},{3,2},{4,5},{5,4},{6,7},{7,6},{8,9},{9,8},{10,11... | collective-permute-start | bytes 1572872 | tf_op jit(solution)/shard_map/ppermute | solution.py:246
  78.4 1.9 %collective-permute-start.16 = (bf16[256,1024]{1,0:T(8,128)(2,1)S(1)}, bf16[256,1024]{1,0:T(8,128)(2,1)S(1)}, u32[]{:S(2)}, u32[]{:S(2)}) collective-permute-start(bf16[256,1024]{1,0:T(8,128)(2,1)S(1)} %collective-permute-done.10.two), channel_id=1, source_target_pairs={{2,3},{3,2},{6,7},{7,6},{10,11},{11,10},{14,15},{15,14},{18,19},{1... | collective-permute-start | bytes 1572872 | tf_op jit(solution)/shard_map/ppermute | solution.py:246
  80.4 1.9 %collective-permute-done.16.two_beside = bf16[256,1024]{1,0:T(8,128)(2,1)S(1)} collective-permute-done((bf16[256,1024]{1,0:T(8,128)(2,1)S(1)}, bf16[256,1024]{1,0:T(8,128)(2,1)S(1)}, u32[]{:S(2)}, u32[]{:S(2)}) %collective-permute-start.16) | collective-permute-done | bytes 524320 | tf_op jit(solution)/shard_map/ppermute | solution.py:246
  82.2 11.3 %correlate_far.1 = bf16[256,8,8,256]{3,2,1,0:T(8,128)(2,1)} custom-call(s32[1]{0:T(128)S(6)} %copy.11.band, bf16[8,256,1024]{2,1,0:T(8,128)(2,1)S(1)} %get-tuple-element.41.lagged, bf16[8,256,256]{2,1,0:T(8,128)(2,1)S(1)} %get-tuple-element.42.own, bf16[3,8,256,256]{3,2,1,0:T(8,128)(2,1)S(1)} %correlate_near.1.near, ...), custom_call_target="tpu_custom_call" | custom-call | flops 5368709120 | bytes 9437184 | tf_op jit(solution)/shard_map/correlate_far/pallas_call | solution.py:402
  (35 shorter events, 5.6 us)
Async XLA Ops:
  0.0 30.9 %copy-start = (bf16[2048,1024]{1,0:T(8,128)(2,1)S(1)}, bf16[2048,1024]{1,0:T(8,128)(2,1)}, u32[]{:S(2)}) copy-start(bf16[2048,1024]{1,0:T(8,128)(2,1)} %constant.12.clone.table) | copy-start | bytes 12582916
  0.0 30.9 %copy-start.1 = (bf16[512,512]{1,0:T(8,128)(2,1)S(1)}, bf16[512,512]{1,0:T(8,128)(2,1)}, u32[]{:S(2)}) copy-start(bf16[512,512]{1,0:T(8,128)(2,1)} %constant.14.clone.window) | copy-start | bytes 1572868
  0.0 30.9 %copy-start.2 = (bf16[128,1024]{1,0:T(8,128)(2,1)S(1)}, bf16[128,1024]{1,0:T(8,128)(2,1)}, u32[]{:S(2)}) copy-start(bf16[128,1024]{1,0:T(8,128)(2,1)} %constant.13.clone.edge_table) | copy-start | bytes 786436
  0.0 30.9 %copy-start.3 = (f32[1,512]{1,0:T(1,128)S(1)}, f32[1,512]{1,0:T(1,128)}, u32[]{:S(2)}) copy-start(f32[1,512]{1,0:T(1,128)} %constant.15.clone.counts) | copy-start | bytes 6148
  5.9 2.5 %collective-permute-start = (bf16[8,264,128]{2,1,0:T(8,128)(2,1)}, bf16[8,264,128]{2,1,0:T(8,128)(2,1)S(1)}, u32[]{:S(2)}, u32[]{:S(2)}) collective-permute-start(bf16[8,264,128]{2,1,0:T(8,128)(2,1)} %get-tuple-element.28), channel_id=1, source_target_pairs={{0,1},{1,0},{2,3},{3,2},{4,5},{5,4},{6,7},{7,6},{8,9},{9,8},{10,11... | collective-permute-start | bytes 1622024 | tf_op jit(solution)/shard_map/ppermute | solution.py:149
  8.4 32.7 %copy-start.4 = (f32[8,1,512]{2,1,0:T(1,128)S(1)}, f32[8,1,512]{2,1,0:T(1,128)}, u32[]{:S(2)}) copy-start(f32[8,1,512]{2,1,0:T(1,128)} %constant.17.clone.sine) | copy-start | bytes 49156
  8.4 32.7 %copy-start.5 = (f32[8,1,512]{2,1,0:T(1,128)S(1)}, f32[8,1,512]{2,1,0:T(1,128)}, u32[]{:S(2)}) copy-start(f32[8,1,512]{2,1,0:T(1,128)} %constant.16.clone.cosine) | copy-start | bytes 49156
  8.6 5.0 %collective-permute-start.1 = (bf16[528,128]{1,0:T(8,128)(2,1)S(1)}, bf16[528,128]{1,0:T(8,128)(2,1)S(1)}, u32[]{:S(2)}, u32[]{:S(2)}) collective-permute-start(bf16[528,128]{1,0:T(8,128)(2,1)S(1)} %get-tuple-element.30), channel_id=1, source_target_pairs={{0,2},{1,3},{2,0},{3,1},{4,6},{5,7},{6,4},{7,5},{8,10},{9,11},{10,... | collective-permute-start | bytes 405512 | tf_op jit(solution)/shard_map/ppermute | solution.py:153
  8.6 8.3 %collective-permute-start.2 = (bf16[528,128]{1,0:T(8,128)(2,1)S(1)}, bf16[528,128]{1,0:T(8,128)(2,1)S(1)}, u32[]{:S(2)}, u32[]{:S(2)}) collective-permute-start(bf16[528,128]{1,0:T(8,128)(2,1)S(1)} %get-tuple-element.31), channel_id=1, source_target_pairs={{0,4},{1,5},{2,6},{3,7},{4,0},{5,1},{6,2},{7,3},{8,12},{9,13},{10,... | collective-permute-start | bytes 405512 | tf_op jit(solution)/shard_map/ppermute | solution.py:153
  10.2 11.7 %collective-permute-start.3 = (bf16[528,128]{1,0:T(8,128)(2,1)S(1)}, bf16[528,128]{1,0:T(8,128)(2,1)S(1)}, u32[]{:S(2)}, u32[]{:S(2)}) collective-permute-start(bf16[528,128]{1,0:T(8,128)(2,1)S(1)} %get-tuple-element.32), channel_id=1, source_target_pairs={{0,6},{1,7},{2,4},{3,5},{4,2},{5,3},{6,0},{7,1},{8,14},{9,15},{10,... | collective-permute-start | bytes 405512 | tf_op jit(solution)/shard_map/ppermute | solution.py:153
  11.3 10.6 %collective-permute-start.4 = (bf16[528,128]{1,0:T(8,128)(2,1)S(1)}, bf16[528,128]{1,0:T(8,128)(2,1)S(1)}, u32[]{:S(2)}, u32[]{:S(2)}) collective-permute-start(bf16[528,128]{1,0:T(8,128)(2,1)S(1)} %get-tuple-element.33), channel_id=1, source_target_pairs={{0,8},{1,9},{2,10},{3,11},{4,12},{5,13},{6,14},{7,15},{8,0},{9,1},... | collective-permute-start | bytes 405512 | tf_op jit(solution)/shard_map/ppermute | solution.py:153
  13.6 8.3 %collective-permute-start.5 = (bf16[528,128]{1,0:T(8,128)(2,1)S(1)}, bf16[528,128]{1,0:T(8,128)(2,1)S(1)}, u32[]{:S(2)}, u32[]{:S(2)}) collective-permute-start(bf16[528,128]{1,0:T(8,128)(2,1)S(1)} %get-tuple-element.34), channel_id=1, source_target_pairs={{0,10},{1,11},{2,8},{3,9},{4,14},{5,15},{6,12},{7,13},{8,2},{9,3},... | collective-permute-start | bytes 405512 | tf_op jit(solution)/shard_map/ppermute | solution.py:153
  13.6 13.8 %collective-permute-start.6 = (bf16[528,128]{1,0:T(8,128)(2,1)S(1)}, bf16[528,128]{1,0:T(8,128)(2,1)S(1)}, u32[]{:S(2)}, u32[]{:S(2)}) collective-permute-start(bf16[528,128]{1,0:T(8,128)(2,1)S(1)} %get-tuple-element.35), channel_id=1, source_target_pairs={{0,12},{1,13},{2,14},{3,15},{4,8},{5,9},{6,10},{7,11},{8,4},{9,5},... | collective-permute-start | bytes 405512 | tf_op jit(solution)/shard_map/ppermute | solution.py:153
  17.0 13.9 %collective-permute-start.7 = (bf16[528,128]{1,0:T(8,128)(2,1)S(1)}, bf16[528,128]{1,0:T(8,128)(2,1)S(1)}, u32[]{:S(2)}, u32[]{:S(2)}) collective-permute-start(bf16[528,128]{1,0:T(8,128)(2,1)S(1)} %get-tuple-element.36), channel_id=1, source_target_pairs={{0,14},{1,15},{2,12},{3,13},{4,10},{5,11},{6,8},{7,9},{8,6},{9,7},... | collective-permute-start | bytes 405512 | tf_op jit(solution)/shard_map/ppermute | solution.py:153
  32.7 11.4 %collective-permute-start.9 = (bf16[256,1024]{1,0:T(8,128)(2,1)S(1)}, bf16[256,1024]{1,0:T(8,128)(2,1)S(1)}, u32[]{:S(2)}, u32[]{:S(2)}) collective-permute-start(bf16[256,1024]{1,0:T(8,128)(2,1)S(1)} %get-tuple-element.37.white), channel_id=1, source_target_pairs={{0,2},{1,3},{2,0},{3,1},{4,6},{5,7},{6,4},{7,5},{8,10},{9,11},{10,... | collective-permute-start | bytes 1572872 | tf_op jit(solution)/shard_map/ppermute | solution.py:246
  34.7 18.6 %collective-permute-start.8 = (bf16[256,1024]{1,0:T(8,128)(2,1)S(1)}, bf16[256,1024]{1,0:T(8,128)(2,1)S(1)}, u32[]{:S(2)}, u32[]{:S(2)}) collective-permute-start(bf16[256,1024]{1,0:T(8,128)(2,1)S(1)} %get-tuple-element.37.white), channel_id=1, source_target_pairs={{4,0},{5,1},{6,2},{7,3},{8,4},{9,5},{10,6},{11,7},{12,8},{13,9},{1... | collective-permute-start | bytes 1572872 | tf_op jit(solution)/shard_map/ppermute | solution.py:246
  36.7 23.4 %collective-permute-start.13 = (bf16[256,1024]{1,0:T(8,128)(2,1)S(1)}, bf16[256,1024]{1,0:T(8,128)(2,1)S(1)}, u32[]{:S(2)}, u32[]{:S(2)}) collective-permute-start(bf16[256,1024]{1,0:T(8,128)(2,1)S(1)} %get-tuple-element.37.white), channel_id=1, source_target_pairs={{1,0},{3,2},{5,4},{7,6},{9,8},{11,10},{13,12},{15,14},{17,16},{19,... | collective-permute-start | bytes 1572872 | tf_op jit(solution)/shard_map/ppermute | solution.py:246
  53.4 7.5 %collective-permute-start.14 = (bf16[256,1024]{1,0:T(8,128)(2,1)S(1)}, bf16[256,1024]{1,0:T(8,128)(2,1)S(1)}, u32[]{:S(2)}, u32[]{:S(2)}) collective-permute-start(bf16[256,1024]{1,0:T(8,128)(2,1)S(1)} %collective-permute-done.8.four), channel_id=1, source_target_pairs={{0,1},{1,0},{2,3},{3,2},{4,5},{5,4},{6,7},{7,6},{8,9},{9,8},{10,11... | collective-permute-start | bytes 1572872 | tf_op jit(solution)/shard_map/ppermute | solution.py:246
  55.6 15.9 %collective-permute-start.10 = (bf16[256,1024]{1,0:T(8,128)(2,1)S(1)}, bf16[256,1024]{1,0:T(8,128)(2,1)S(1)}, u32[]{:S(2)}, u32[]{:S(2)}) collective-permute-start(bf16[256,1024]{1,0:T(8,128)(2,1)S(1)} %collective-permute-done.9.across), channel_id=1, source_target_pairs={{6,2},{7,3},{10,6},{11,7},{14,10},{15,11},{22,18},{23,19},{26,22},... | collective-permute-start | bytes 1572872 | tf_op jit(solution)/shard_map/ppermute | solution.py:246
  56.9 20.4 %collective-permute-start.12 = (bf16[256,1024]{1,0:T(8,128)(2,1)S(1)}, bf16[256,1024]{1,0:T(8,128)(2,1)S(1)}, u32[]{:S(2)}, u32[]{:S(2)}) collective-permute-start(bf16[256,1024]{1,0:T(8,128)(2,1)S(1)} %collective-permute-done.8.four), channel_id=1, source_target_pairs={{4,1},{6,3},{8,5},{10,7},{12,9},{14,11},{20,17},{22,19},{24,21},{2... | collective-permute-start | bytes 1572872 | tf_op jit(solution)/shard_map/ppermute | solution.py:246
  58.2 19.1 %collective-permute-start.11 = (bf16[256,1024]{1,0:T(8,128)(2,1)S(1)}, bf16[256,1024]{1,0:T(8,128)(2,1)S(1)}, u32[]{:S(2)}, u32[]{:S(2)}) collective-permute-start(bf16[256,1024]{1,0:T(8,128)(2,1)S(1)} %collective-permute-done.8.four), channel_id=1, source_target_pairs={{2,0},{3,1},{4,2},{5,3},{6,4},{7,5},{8,6},{9,7},{10,8},{11,9},{12,... | collective-permute-start | bytes 1572872 | tf_op jit(solution)/shard_map/ppermute | solution.py:246
  60.1 20.2 %collective-permute-start.17 = (bf16[256,1024]{1,0:T(8,128)(2,1)S(1)}, bf16[256,1024]{1,0:T(8,128)(2,1)S(1)}, u32[]{:S(2)}, u32[]{:S(2)}) collective-permute-start(bf16[256,1024]{1,0:T(8,128)(2,1)S(1)} %collective-permute-done.9.across), channel_id=1, source_target_pairs={{0,1},{1,0},{4,5},{5,4},{8,9},{9,8},{12,13},{13,12},{16,17},{17,16... | collective-permute-start | bytes 1572872 | tf_op jit(solution)/shard_map/ppermute | solution.py:246
  77.3 3.1 %collective-permute-start.15 = (bf16[256,1024]{1,0:T(8,128)(2,1)S(1)}, bf16[256,1024]{1,0:T(8,128)(2,1)S(1)}, u32[]{:S(2)}, u32[]{:S(2)}) collective-permute-start(bf16[256,1024]{1,0:T(8,128)(2,1)S(1)} %collective-permute-done.11.six), channel_id=1, source_target_pairs={{0,1},{1,0},{2,3},{3,2},{4,5},{5,4},{6,7},{7,6},{8,9},{9,8},{10,11... | collective-permute-start | bytes 1572872 | tf_op jit(solution)/shard_map/ppermute | solution.py:246
  78.4 3.8 %collective-permute-start.16 = (bf16[256,1024]{1,0:T(8,128)(2,1)S(1)}, bf16[256,1024]{1,0:T(8,128)(2,1)S(1)}, u32[]{:S(2)}, u32[]{:S(2)}) collective-permute-start(bf16[256,1024]{1,0:T(8,128)(2,1)S(1)} %collective-permute-done.10.two), channel_id=1, source_target_pairs={{2,3},{3,2},{6,7},{7,6},{10,11},{11,10},{14,15},{15,14},{18,19},{1... | collective-permute-start | bytes 1572872 | tf_op jit(solution)/shard_map/ppermute | solution.py:246

commit v4 on v3

--- a/solution.py
+++ b/solution.py
@@ -322,78 +322,76 @@
     )(band, real, imag, jnp.asarray(cosine[:, None]), jnp.asarray(sine[:, None]), white)
 
 
-def near_body(band, lagged, one, four, four_beside, out):
+def near_body(band, lagged, one, four, four_beside, seven, two, across, out, columns, sem):
+    first = pl.program_id(0) == 0
+    near_side = lax.axis_index("row") & 2 == 0
+    pl.when(first & near_side)(pltpu.make_async_copy(across, columns, sem).start)
+    pl.when(first & jnp.logical_not(near_side))(pltpu.make_async_copy(two, columns, sem).start)
+    pl.when(first)(pltpu.make_async_copy(two, columns, sem).wait)
     left = lagged[pl.program_id(0)]
     out[0, 0] = pair(left, four[...], band, 4)
     out[1, 0] = pair(left, four_beside[...], band, by_parity(5, 3))
     out[2, 0] = pair(left, one[...], band, 1)
-
-
-def correlate_near(band, lagged, one, four, four_beside):
+    out[3, 0] = pair(left, seven[...], band, 7)
+    out[4, 0] = pair(left, columns[...], band, 2)
+
+
+def correlate_near(band, lagged, *tiles):
     channels = lagged.shape[1]
     return pl.pallas_call(
         near_body,
-        out_shape=jax.ShapeDtypeStruct((3, LAGS, channels, channels), HALF),
+        out_shape=jax.ShapeDtypeStruct((5, LAGS, channels, channels), HALF),
         grid=(LAGS,),
-        in_specs=[SCALAR, WHOLE, WHOLE, WHOLE, WHOLE],
-        out_specs=pl.BlockSpec((3, 1, channels, channels), lambda i: (0, i, 0, 0)),
+        in_specs=[SCALAR] + [WHOLE] * 5 + [pl.BlockSpec(memory_space=pl.ANY)] * 2,
+        out_specs=pl.BlockSpec((5, 1, channels, channels), lambda i: (0, i, 0, 0)),
+        scratch_shapes=[pltpu.VMEM((channels, 2 * NF), HALF), pltpu.SemaphoreType.DMA],
         compiler_params=pltpu.CompilerParams(vmem_limit_bytes=16 << 20),
-        cost_estimate=cost(channels, 3),
+        cost_estimate=cost(channels, 5),
         name="correlate_near",
-    )(band, lagged, one, four, four_beside)
-
-
-EVEN = (0, 3, 7, 8, 1, 2, 4, 5)
-ODD = (0, 8, 7, 2, 1, 5, 4, 6)
+    )(band, lagged, *tiles)
+
+
+EVEN = (0, 3, 5, 8, 1, 2, 6, 7)
+ODD = (0, 8, 5, 2, 1, 7, 6, 4)
 
 
 def far_body(
-    band, lagged, own, near, six, six_beside, seven, two, two_beside, across, across_beside,
-    out, columns, sems, *, rows,
+    band, lagged, own, near, six, six_beside, two_beside, across_beside, out, columns, sem,
+    *, rows,
 ):
     step = pl.program_id(0)
-    channels = six.shape[0]
+    channels = six_beside.shape[0]
+    first = step == 0
     near_side = lax.axis_index("row") & 2 == 0
-
-    @pl.when(step == 0)
-    def _():
-        for slot, (here, there) in enumerate(((across, two), (across_beside, two_beside))):
-
-            @pl.when(near_side)
-            def _():
-                pltpu.make_async_copy(here, columns.at[slot], sems.at[slot]).start()
-
-            @pl.when(jnp.logical_not(near_side))
-            def _():
-                pltpu.make_async_copy(there, columns.at[slot], sems.at[slot]).start()
-
-        for slot in range(2):
-            pltpu.make_async_copy(two, columns.at[slot], sems.at[slot]).wait()
-
-    at = pl.ds(pl.multiple_of(step * rows, rows), rows)
-    left = lagged[:, at, :].reshape(LAGS * rows, 2 * NF)
-    far = [
-        pair(left, tile, band, offset).reshape(LAGS, rows, channels)
-        for tile, offset in (
-            (six[...], 6),
-            (six_beside[...], by_parity(7, 5)),
-            (seven[...], 7),
-            (columns[0], 2),
-            (columns[1], by_parity(3, 1)),
-        )
-    ]
-    even_row = lax.axis_index("row") % 2 == 0
-    for lag in range(LAGS):
-        for half in range(channels // LANES):
-            lanes = slice(half * LANES, (half + 1) * LANES)
-            planes = [own[lag, at, lanes]]
-            planes += [near[index, lag, at, lanes] for index in range(3)]
-            planes += [plane[lag, :, lanes] for plane in far]
-            ordered = [
-                planes[even] if even == odd else jnp.where(even_row, planes[even], planes[odd])
-                for even, odd in zip(EVEN, ODD)
-            ]
-            out[:, lag, :, lanes] = pltpu.einshape("kab->akb", jnp.stack(ordered))
+    pl.when(first & near_side)(pltpu.make_async_copy(across_beside, columns, sem).start)
+    pl.when(first & jnp.logical_not(near_side))(
+        pltpu.make_async_copy(two_beside, columns, sem).start
+    )
+    pl.when(first)(pltpu.make_async_copy(two_beside, columns, sem).wait)
+
+    def run(order, offsets):
+        at = pl.ds(pl.multiple_of(step * rows, rows), rows)
+        left = lagged[:, at, :].reshape(LAGS * rows, 2 * NF)
+        far = [
+            pair(left, tile, band, offset).reshape(LAGS, rows, channels)
+            for tile, offset in zip((six[...], six_beside[...], columns[...]), offsets)
+        ]
+        for lag in range(LAGS):
+            for half in range(channels // LANES):
+                lanes = slice(half * LANES, (half + 1) * LANES)
+                planes = []
+                for plane in order:
+                    if plane == 0:
+                        planes.append(own[lag, at, lanes])
+                    elif plane < 6:
+                        planes.append(near[plane - 1, lag, at, lanes])
+                    else:
+                        planes.append(far[plane - 6][lag, :, lanes])
+                out[:, lag, :, lanes] = pltpu.einshape("kab->akb", jnp.stack(planes))
+
+    is_even = lax.axis_index("row") % 2 == 0
+    pl.when(is_even)(lambda: run(EVEN, (6, 7, 3)))
+    pl.when(jnp.logical_not(is_even))(lambda: run(ODD, (6, 5, 1)))
 
 
 def correlate_far(band, lagged, own, near, *tiles):
@@ -403,14 +401,11 @@
         functools.partial(far_body, rows=rows),
         out_shape=jax.ShapeDtypeStruct((channels, LAGS, NB, channels), HALF),
         grid=(channels // rows,),
-        in_specs=[SCALAR] + [WHOLE] * 3 + [WHOLE] * 3 + [pl.BlockSpec(memory_space=pl.ANY)] * 4,
+        in_specs=[SCALAR] + [WHOLE] * 5 + [pl.BlockSpec(memory_space=pl.ANY)] * 2,
         out_specs=pl.BlockSpec((rows, LAGS, NB, channels), lambda i: (i, 0, 0, 0)),
-        scratch_shapes=[
-            pltpu.VMEM((2, channels, 2 * NF), HALF),
-            pltpu.SemaphoreType.DMA((2,)),
-        ],
+        scratch_shapes=[pltpu.VMEM((channels, 2 * NF), HALF), pltpu.SemaphoreType.DMA],
         compiler_params=pltpu.CompilerParams(vmem_limit_bytes=24 << 20),
-        cost_estimate=cost(channels, 5),
+        cost_estimate=cost(channels, 3),
         name="correlate_far",
     )(band, lagged, own, near, *tiles)
 
@@ -427,12 +422,12 @@
     four, across, lagged = lax.optimization_barrier((four, across, lagged))
     two, six, seven = gather_second(four, across)
     across_beside = beside(across, lambda s: s & 2 == 0)
-    near = correlate_near(band_width, lagged, one, four, beside(four))
-    two, six, seven, near = lax.optimization_barrier((two, six, seven, near))
+    four_beside = beside(four)
+    near = correlate_near(band_width, lagged, one, four, four_beside, seven, two, across)
     two_beside = beside(two, lambda s: s & 2 == 2)
-    return correlate_far(
-        band_width, lagged, own, near, six, beside(six), seven, two, two_beside, across, across_beside
-    )
+    six, near, two_beside = lax.optimization_barrier((six, near, two_beside))
+    six_beside = beside(six)
+    return correlate_far(band_width, lagged, own, near, six, six_beside, two_beside, across_beside)
 
 
 def solution(mesh):

time: 94.4 us -> 92.6 us (0.981)
    pallas_call x1, Pallas kernels: 11.3 us -> 7.95 us  [correlate_far(): pl.pallas_call(functools.partial(far_body, rows=rows), out_shape=jax.Shap...]
    pallas_call x1, Pallas kernels: 5.08 us -> 7.56 us  [correlate_near(): pl.pallas_call(near_body, out_shape=jax.ShapeDtypeStruct((5, LAGS, channe...]
  transfers between devices with their start and end apart: 18 -> 18, of which waited for: 8 -> 9; matrix products, arithmetic and copies ran while one was open for 1% -> 1% of each run, Pallas kernels for 9% -> 11%
where the time goes in v4:
time: 92.6 us; the launch traced here: 92.3 us
  waiting for transfers between devices  35.3 us (38%)
  starting transfers between devices  27.9 us (30%)
  Pallas kernels  26.2 us (28%)
  between operations  1.54 us (2%)
  local copies, waits for them, and re-layouts  1.22 us (1%)
    ppermute x10, waiting for transfers between devices, send(): return lax.ppermute(value, 'row', pairs)  22.5 us
    ppermute x10, starting transfers between devices, send(): return lax.ppermute(value, 'row', pairs)  17.8 us
    ppermute x7, waiting for transfers between devices, transpose_blocks(): lax.ppermute(pieces[d], 'row', [(s, s ^ 2 * d) for s in range(tiles)])  12.3 us
    ppermute x7, starting transfers between devices, transpose_blocks(): lax.ppermute(pieces[d], 'row', [(s, s ^ 2 * d) for s in range(tiles)])  9.36 us
    pallas_call x1, Pallas kernels, correlate_far(): pl.pallas_call(functools.partial(far_body, rows=rows), out_shape=jax.Shap...  7.95 us
    pallas_call x1, Pallas kernels, correlate_near(): pl.pallas_call(near_body, out_shape=jax.ShapeDtypeStruct((5, LAGS, channe...  7.56 us
    pallas_call x1, Pallas kernels, filter_blocks(): pl.pallas_call(functools.partial(filter_body, channels=channels), out_sha...  5.85 us
    pallas_call x1, Pallas kernels, correlate_own(): pl.pallas_call(own_body, out_shape=(jax.ShapeDtypeStruct((LAGS, channels,...  2.99 us
  transfers between devices with their start and end apart: 18, of which 9 were waited for; matrix products, arithmetic and copies ran while one was open for 1% of the time, Pallas kernels for 11%

profile of v4, /device:TPU:3, one launch (start us, length us, event | category | flops | bytes accessed | tf_op | source)
XLA Modules:
  0.0 92.3 jit_solution(267013228053604825)
XLA Ops:
  0.0 5.8 %filter.1 = (bf16[8,264,128]{2,1,0:T(8,128)(2,1)}, bf16[8,264,128]{2,1,0:T(8,128)(2,1)}) custom-call(f32[16]{0:T(128)} %taps.1, bf16[4096,512]{1,0:T(8,128)(2,1)} %raw.1), custom_call_target="tpu_custom_call" | custom-call | tf_op jit(solution)/shard_map/filter/pallas_call | solution.py:124
  6.6 1.1 %slice_bitcast_fusion.8 = (bf16[264,128]{1,0:T(8,128)(2,1)S(1)}, bf16[264,128]{1,0:T(8,128)(2,1)S(1)}, bf16[264,128]{1,0:T(8,128)(2,1)S(1)}, bf16[264,128]{1,0:T...) fusion(bf16[8,264,128]{2,1,0:T(8,128)(2,1)} %get-tuple-element.26), kind=kLoop, calls=%fused_computation.16 | loop fusion | bytes 1081344 | tf_op jit(solution)/shard_map/squeeze | solution.py:150
  8.6 1.5 %collective-permute-start.2 = (bf16[528,128]{1,0:T(8,128)(2,1)S(1)}, bf16[528,128]{1,0:T(8,128)(2,1)S(1)}, u32[]{:S(2)}, u32[]{:S(2)}) collective-permute-start(bf16[528,128]{1,0:T(8,128)(2,1)S(1)} %get-tuple-element.30), channel_id=1, source_target_pairs={{0,4},{1,5},{2,6},{3,7},{4,0},{5,1},{6,2},{7,3},{8,12},{9,13},{10,... | collective-permute-start | bytes 405512 | tf_op jit(solution)/shard_map/ppermute | solution.py:153
  11.3 2.3 %collective-permute-start.4 = (bf16[528,128]{1,0:T(8,128)(2,1)S(1)}, bf16[528,128]{1,0:T(8,128)(2,1)S(1)}, u32[]{:S(2)}, u32[]{:S(2)}) collective-permute-start(bf16[528,128]{1,0:T(8,128)(2,1)S(1)} %get-tuple-element.32), channel_id=1, source_target_pairs={{0,8},{1,9},{2,10},{3,11},{4,12},{5,13},{6,14},{7,15},{8,0},{9,1},... | collective-permute-start | bytes 405512 | tf_op jit(solution)/shard_map/ppermute | solution.py:153
  13.6 3.3 %collective-permute-start.6 = (bf16[528,128]{1,0:T(8,128)(2,1)S(1)}, bf16[528,128]{1,0:T(8,128)(2,1)S(1)}, u32[]{:S(2)}, u32[]{:S(2)}) collective-permute-start(bf16[528,128]{1,0:T(8,128)(2,1)S(1)} %get-tuple-element.34), channel_id=1, source_target_pairs={{0,12},{1,13},{2,14},{3,15},{4,8},{5,9},{6,10},{7,11},{8,4},{9,5},... | collective-permute-start | bytes 405512 | tf_op jit(solution)/shard_map/ppermute | solution.py:153
  18.6 3.3 %collective-permute-done.3.rest_3_ = bf16[528,128]{1,0:T(8,128)(2,1)S(1)} collective-permute-done((bf16[528,128]{1,0:T(8,128)(2,1)S(1)}, bf16[528,128]{1,0:T(8,128)(2,1)S(1)}, u32[]{:S(2)}, u32[]{:S(2)}) %collective-permute-start.3) | collective-permute-done | bytes 135200 | tf_op jit(solution)/shard_map/ppermute | solution.py:153
  21.9 5.5 %collective-permute-done.6.rest_6_ = bf16[528,128]{1,0:T(8,128)(2,1)S(1)} collective-permute-done((bf16[528,128]{1,0:T(8,128)(2,1)S(1)}, bf16[528,128]{1,0:T(8,128)(2,1)S(1)}, u32[]{:S(2)}, u32[]{:S(2)}) %collective-permute-start.6) | collective-permute-done | bytes 135200 | tf_op jit(solution)/shard_map/ppermute | solution.py:153
  27.4 3.5 %collective-permute-done.7.rest_7_ = bf16[528,128]{1,0:T(8,128)(2,1)S(1)} collective-permute-done((bf16[528,128]{1,0:T(8,128)(2,1)S(1)}, bf16[528,128]{1,0:T(8,128)(2,1)S(1)}, u32[]{:S(2)}, u32[]{:S(2)}) %collective-permute-start.7) | collective-permute-done | bytes 135200 | tf_op jit(solution)/shard_map/ppermute | solution.py:153
  30.9 1.9 %whiten.1 = (bf16[256,1024]{1,0:T(8,128)(2,1)S(1)}, f32[256,512]{1,0:T(8,128)S(1)}, f32[256,512]{1,0:T(8,128)S(1)}) custom-call(s32[1]{0:T(128)S(6)} %copy.12.dead, bf16[2048,1024]{1,0:T(8,128)(2,1)S(1)} %copy-done, bf16[128,1024]{1,0:T(8,128)(2,1)S(1)} %copy-done.2, bf16[512,512]{1,0:T(8,128)(2,1)S(1)} %copy-done.1, f32[1,512]{1,0:T(1,128)S(1)} %copy-done.3, ...), custom_call_target="tpu_custom_call" | custom-call | tf_op jit(solution)/shard_map/whiten/pallas_call | solution.py:220
  32.7 2.0 %collective-permute-start.9 = (bf16[256,1024]{1,0:T(8,128)(2,1)S(1)}, bf16[256,1024]{1,0:T(8,128)(2,1)S(1)}, u32[]{:S(2)}, u32[]{:S(2)}) collective-permute-start(bf16[256,1024]{1,0:T(8,128)(2,1)S(1)} %get-tuple-element.36.white), channel_id=1, source_target_pairs={{0,2},{1,3},{2,0},{3,1},{4,6},{5,7},{6,4},{7,5},{8,10},{9,11},{10,... | collective-permute-start | bytes 1572872 | tf_op jit(solution)/shard_map/ppermute | solution.py:246
  34.7 1.3 %collective-permute-start.8 = (bf16[256,1024]{1,0:T(8,128)(2,1)S(1)}, bf16[256,1024]{1,0:T(8,128)(2,1)S(1)}, u32[]{:S(2)}, u32[]{:S(2)}) collective-permute-start(bf16[256,1024]{1,0:T(8,128)(2,1)S(1)} %get-tuple-element.36.white), channel_id=1, source_target_pairs={{4,0},{5,1},{6,2},{7,3},{8,4},{9,5},{10,6},{11,7},{12,8},{13,9},{1... | collective-permute-start | bytes 1572872 | tf_op jit(solution)/shard_map/ppermute | solution.py:246
  36.7 3.0 %correlate_own.1 = (bf16[8,256,1024]{2,1,0:T(8,128)(2,1)S(1)}, bf16[8,256,256]{2,1,0:T(8,128)(2,1)S(1)}) custom-call(s32[1]{0:T(128)S(6)} %copy.11.band, f32[256,512]{1,0:T(8,128)S(1)} %get-tuple-element.37.real, f32[256,512]{1,0:T(8,128)S(1)} %get-tuple-element.38.imag, f32[8,1,512]{2,1,0:T(1,128)S(1)} %copy-done.5, f32[8,1,512]{2,1,0:T(1,128)S(1)} %copy-done.4, ...), custom_call_target="tpu_custom_call" | custom-call | flops 1073741824 | bytes 5242880 | tf_op jit(solution)/shard_map/correlate_own/pallas_call | solution.py:300
  39.7 4.1 %collective-permute-done.9.across = bf16[256,1024]{1,0:T(8,128)(2,1)S(1)} collective-permute-done((bf16[256,1024]{1,0:T(8,128)(2,1)S(1)}, bf16[256,1024]{1,0:T(8,128)(2,1)S(1)}, u32[]{:S(2)}, u32[]{:S(2)}) %collective-permute-start.9) | collective-permute-done | bytes 524320 | tf_op jit(solution)/shard_map/ppermute | solution.py:246
  43.8 9.6 %collective-permute-done.8.four = bf16[256,1024]{1,0:T(8,128)(2,1)S(1)} collective-permute-done((bf16[256,1024]{1,0:T(8,128)(2,1)S(1)}, bf16[256,1024]{1,0:T(8,128)(2,1)S(1)}, u32[]{:S(2)}, u32[]{:S(2)}) %collective-permute-start.8) | collective-permute-done | bytes 524320 | tf_op jit(solution)/shard_map/ppermute | solution.py:246
  53.4 1.3 %collective-permute-start.14 = (bf16[256,1024]{1,0:T(8,128)(2,1)S(1)}, bf16[256,1024]{1,0:T(8,128)(2,1)S(1)}, u32[]{:S(2)}, u32[]{:S(2)}) collective-permute-start(bf16[256,1024]{1,0:T(8,128)(2,1)S(1)} %collective-permute-done.9.across), channel_id=1, source_target_pairs={{6,2},{7,3},{10,6},{11,7},{14,10},{15,11},{22,18},{23,19},{26,22},... | collective-permute-start | bytes 1572872 | tf_op jit(solution)/shard_map/ppermute | solution.py:246
  54.6 4.2 %collective-permute-start.11 = (bf16[256,1024]{1,0:T(8,128)(2,1)S(1)}, bf16[256,1024]{1,0:T(8,128)(2,1)S(1)}, u32[]{:S(2)}, u32[]{:S(2)}) collective-permute-start(bf16[256,1024]{1,0:T(8,128)(2,1)S(1)} %get-tuple-element.36.white), channel_id=1, source_target_pairs={{1,0},{3,2},{5,4},{7,6},{9,8},{11,10},{13,12},{15,14},{17,16},{19,... | collective-permute-start | bytes 1572872 | tf_op jit(solution)/shard_map/ppermute | solution.py:246
  58.8 1.3 %collective-permute-start.13 = (bf16[256,1024]{1,0:T(8,128)(2,1)S(1)}, bf16[256,1024]{1,0:T(8,128)(2,1)S(1)}, u32[]{:S(2)}, u32[]{:S(2)}) collective-permute-start(bf16[256,1024]{1,0:T(8,128)(2,1)S(1)} %collective-permute-done.8.four), channel_id=1, source_target_pairs={{4,1},{6,3},{8,5},{10,7},{12,9},{14,11},{20,17},{22,19},{24,21},{2... | collective-permute-start | bytes 1572872 | tf_op jit(solution)/shard_map/ppermute | solution.py:246
  60.2 1.9 %collective-permute-start.10 = (bf16[256,1024]{1,0:T(8,128)(2,1)S(1)}, bf16[256,1024]{1,0:T(8,128)(2,1)S(1)}, u32[]{:S(2)}, u32[]{:S(2)}) collective-permute-start(bf16[256,1024]{1,0:T(8,128)(2,1)S(1)} %collective-permute-done.8.four), channel_id=1, source_target_pairs={{2,0},{3,1},{4,2},{5,3},{6,4},{7,5},{8,6},{9,7},{10,8},{11,9},{12,... | collective-permute-start | bytes 1572872 | tf_op jit(solution)/shard_map/ppermute | solution.py:246
  62.1 4.3 %collective-permute-done.14.two = bf16[256,1024]{1,0:T(8,128)(2,1)S(1)} collective-permute-done((bf16[256,1024]{1,0:T(8,128)(2,1)S(1)}, bf16[256,1024]{1,0:T(8,128)(2,1)S(1)}, u32[]{:S(2)}, u32[]{:S(2)}) %collective-permute-start.14) | collective-permute-done | bytes 524320 | tf_op jit(solution)/shard_map/ppermute | solution.py:246
  66.4 5.0 %collective-permute-start.15 = (bf16[256,1024]{1,0:T(8,128)(2,1)S(1)}, bf16[256,1024]{1,0:T(8,128)(2,1)S(1)}, u32[]{:S(2)}, u32[]{:S(2)}) collective-permute-start(bf16[256,1024]{1,0:T(8,128)(2,1)S(1)} %collective-permute-done.14.two), channel_id=1, source_target_pairs={{2,3},{3,2},{6,7},{7,6},{10,11},{11,10},{14,15},{15,14},{18,19},{1... | collective-permute-start | bytes 1572872 | tf_op jit(solution)/shard_map/ppermute | solution.py:246
  72.2 2.6 %collective-permute-done.13.seven = bf16[256,1024]{1,0:T(8,128)(2,1)S(1)} collective-permute-done((bf16[256,1024]{1,0:T(8,128)(2,1)S(1)}, bf16[256,1024]{1,0:T(8,128)(2,1)S(1)}, u32[]{:S(2)}, u32[]{:S(2)}) %collective-permute-start.13) | collective-permute-done | bytes 524320 | tf_op jit(solution)/shard_map/ppermute | solution.py:246
  74.8 7.6 %correlate_near.1.near = bf16[5,8,256,256]{3,2,1,0:T(8,128)(2,1)S(1)} custom-call(s32[1]{0:T(128)S(6)} %copy.11.band, bf16[8,256,1024]{2,1,0:T(8,128)(2,1)S(1)} %get-tuple-element.40.lagged, bf16[256,1024]{1,0:T(8,128)(2,1)S(1)} %collective-permute-done.11.one, bf16[256,1024]{1,0:T(8,128)(2,1)S(1)} %collective-permute-done.8.four, ...), custom_call_target="tpu_custom_call" | custom-call | flops 5368709120 | bytes 9437184 | tf_op jit(solution)/shard_map/correlate_near/pallas_call | solution.py:341
  82.5 1.9 %collective-permute-done.16.six_beside = bf16[256,1024]{1,0:T(8,128)(2,1)S(1)} collective-permute-done((bf16[256,1024]{1,0:T(8,128)(2,1)S(1)}, bf16[256,1024]{1,0:T(8,128)(2,1)S(1)}, u32[]{:S(2)}, u32[]{:S(2)}) %collective-permute-start.16) | collective-permute-done | bytes 524320 | tf_op jit(solution)/shard_map/ppermute | solution.py:246
  84.4 8.0 %correlate_far.1 = bf16[256,8,8,256]{3,2,1,0:T(8,128)(2,1)} custom-call(s32[1]{0:T(128)S(6)} %copy.11.band, bf16[8,256,1024]{2,1,0:T(8,128)(2,1)S(1)} %get-tuple-element.40.lagged, bf16[8,256,256]{2,1,0:T(8,128)(2,1)S(1)} %get-tuple-element.41.own, bf16[5,8,256,256]{3,2,1,0:T(8,128)(2,1)S(1)} %correlate_near.1.near, ...), custom_call_target="tpu_custom_call" | custom-call | flops 3221225472 | bytes 7340032 | tf_op jit(solution)/shard_map/correlate_far/pallas_call | solution.py:400
  (35 shorter events, 4.5 us)
Async XLA Ops:
  0.0 30.9 %copy-start = (bf16[2048,1024]{1,0:T(8,128)(2,1)S(1)}, bf16[2048,1024]{1,0:T(8,128)(2,1)}, u32[]{:S(2)}) copy-start(bf16[2048,1024]{1,0:T(8,128)(2,1)} %constant.12.clone.table) | copy-start | bytes 12582916
  0.0 30.9 %copy-start.1 = (bf16[512,512]{1,0:T(8,128)(2,1)S(1)}, bf16[512,512]{1,0:T(8,128)(2,1)}, u32[]{:S(2)}) copy-start(bf16[512,512]{1,0:T(8,128)(2,1)} %constant.14.clone.window) | copy-start | bytes 1572868
  0.0 30.9 %copy-start.2 = (bf16[128,1024]{1,0:T(8,128)(2,1)S(1)}, bf16[128,1024]{1,0:T(8,128)(2,1)}, u32[]{:S(2)}) copy-start(bf16[128,1024]{1,0:T(8,128)(2,1)} %constant.13.clone.edge_table) | copy-start | bytes 786436
  0.0 30.9 %copy-start.3 = (f32[1,512]{1,0:T(1,128)S(1)}, f32[1,512]{1,0:T(1,128)}, u32[]{:S(2)}) copy-start(f32[1,512]{1,0:T(1,128)} %constant.15.clone.counts) | copy-start | bytes 6148
  5.9 2.5 %collective-permute-start = (bf16[8,264,128]{2,1,0:T(8,128)(2,1)}, bf16[8,264,128]{2,1,0:T(8,128)(2,1)S(1)}, u32[]{:S(2)}, u32[]{:S(2)}) collective-permute-start(bf16[8,264,128]{2,1,0:T(8,128)(2,1)} %get-tuple-element.27), channel_id=1, source_target_pairs={{0,1},{1,0},{2,3},{3,2},{4,5},{5,4},{6,7},{7,6},{8,9},{9,8},{10,11... | collective-permute-start | bytes 1622024 | tf_op jit(solution)/shard_map/ppermute | solution.py:149
  8.4 28.3 %copy-start.4 = (f32[8,1,512]{2,1,0:T(1,128)S(1)}, f32[8,1,512]{2,1,0:T(1,128)}, u32[]{:S(2)}) copy-start(f32[8,1,512]{2,1,0:T(1,128)} %constant.17.clone.sine) | copy-start | bytes 49156
  8.4 28.3 %copy-start.5 = (f32[8,1,512]{2,1,0:T(1,128)S(1)}, f32[8,1,512]{2,1,0:T(1,128)}, u32[]{:S(2)}) copy-start(f32[8,1,512]{2,1,0:T(1,128)} %constant.16.clone.cosine) | copy-start | bytes 49156
  8.6 5.0 %collective-permute-start.1 = (bf16[528,128]{1,0:T(8,128)(2,1)S(1)}, bf16[528,128]{1,0:T(8,128)(2,1)S(1)}, u32[]{:S(2)}, u32[]{:S(2)}) collective-permute-start(bf16[528,128]{1,0:T(8,128)(2,1)S(1)} %get-tuple-element.29), channel_id=1, source_target_pairs={{0,2},{1,3},{2,0},{3,1},{4,6},{5,7},{6,4},{7,5},{8,10},{9,11},{10,... | collective-permute-start | bytes 405512 | tf_op jit(solution)/shard_map/ppermute | solution.py:153
  8.6 8.3 %collective-permute-start.2 = (bf16[528,128]{1,0:T(8,128)(2,1)S(1)}, bf16[528,128]{1,0:T(8,128)(2,1)S(1)}, u32[]{:S(2)}, u32[]{:S(2)}) collective-permute-start(bf16[528,128]{1,0:T(8,128)(2,1)S(1)} %get-tuple-element.30), channel_id=1, source_target_pairs={{0,4},{1,5},{2,6},{3,7},{4,0},{5,1},{6,2},{7,3},{8,12},{9,13},{10,... | collective-permute-start | bytes 405512 | tf_op jit(solution)/shard_map/ppermute | solution.py:153
  10.2 11.7 %collective-permute-start.3 = (bf16[528,128]{1,0:T(8,128)(2,1)S(1)}, bf16[528,128]{1,0:T(8,128)(2,1)S(1)}, u32[]{:S(2)}, u32[]{:S(2)}) collective-permute-start(bf16[528,128]{1,0:T(8,128)(2,1)S(1)} %get-tuple-element.31), channel_id=1, source_target_pairs={{0,6},{1,7},{2,4},{3,5},{4,2},{5,3},{6,0},{7,1},{8,14},{9,15},{10,... | collective-permute-start | bytes 405512 | tf_op jit(solution)/shard_map/ppermute | solution.py:153
  11.3 10.6 %collective-permute-start.4 = (bf16[528,128]{1,0:T(8,128)(2,1)S(1)}, bf16[528,128]{1,0:T(8,128)(2,1)S(1)}, u32[]{:S(2)}, u32[]{:S(2)}) collective-permute-start(bf16[528,128]{1,0:T(8,128)(2,1)S(1)} %get-tuple-element.32), channel_id=1, source_target_pairs={{0,8},{1,9},{2,10},{3,11},{4,12},{5,13},{6,14},{7,15},{8,0},{9,1},... | collective-permute-start | bytes 405512 | tf_op jit(solution)/shard_map/ppermute | solution.py:153
  13.6 8.3 %collective-permute-start.5 = (bf16[528,128]{1,0:T(8,128)(2,1)S(1)}, bf16[528,128]{1,0:T(8,128)(2,1)S(1)}, u32[]{:S(2)}, u32[]{:S(2)}) collective-permute-start(bf16[528,128]{1,0:T(8,128)(2,1)S(1)} %get-tuple-element.33), channel_id=1, source_target_pairs={{0,10},{1,11},{2,8},{3,9},{4,14},{5,15},{6,12},{7,13},{8,2},{9,3},... | collective-permute-start | bytes 405512 | tf_op jit(solution)/shard_map/ppermute | solution.py:153
  13.6 13.8 %collective-permute-start.6 = (bf16[528,128]{1,0:T(8,128)(2,1)S(1)}, bf16[528,128]{1,0:T(8,128)(2,1)S(1)}, u32[]{:S(2)}, u32[]{:S(2)}) collective-permute-start(bf16[528,128]{1,0:T(8,128)(2,1)S(1)} %get-tuple-element.34), channel_id=1, source_target_pairs={{0,12},{1,13},{2,14},{3,15},{4,8},{5,9},{6,10},{7,11},{8,4},{9,5},... | collective-permute-start | bytes 405512 | tf_op jit(solution)/shard_map/ppermute | solution.py:153
  17.0 13.9 %collective-permute-start.7 = (bf16[528,128]{1,0:T(8,128)(2,1)S(1)}, bf16[528,128]{1,0:T(8,128)(2,1)S(1)}, u32[]{:S(2)}, u32[]{:S(2)}) collective-permute-start(bf16[528,128]{1,0:T(8,128)(2,1)S(1)} %get-tuple-element.35), channel_id=1, source_target_pairs={{0,14},{1,15},{2,12},{3,13},{4,10},{5,11},{6,8},{7,9},{8,6},{9,7},... | collective-permute-start | bytes 405512 | tf_op jit(solution)/shard_map/ppermute | solution.py:153
  32.7 11.0 %collective-permute-start.9 = (bf16[256,1024]{1,0:T(8,128)(2,1)S(1)}, bf16[256,1024]{1,0:T(8,128)(2,1)S(1)}, u32[]{:S(2)}, u32[]{:S(2)}) collective-permute-start(bf16[256,1024]{1,0:T(8,128)(2,1)S(1)} %get-tuple-element.36.white), channel_id=1, source_target_pairs={{0,2},{1,3},{2,0},{3,1},{4,6},{5,7},{6,4},{7,5},{8,10},{9,11},{10,... | collective-permute-start | bytes 1572872 | tf_op jit(solution)/shard_map/ppermute | solution.py:246
  34.7 18.6 %collective-permute-start.8 = (bf16[256,1024]{1,0:T(8,128)(2,1)S(1)}, bf16[256,1024]{1,0:T(8,128)(2,1)S(1)}, u32[]{:S(2)}, u32[]{:S(2)}) collective-permute-start(bf16[256,1024]{1,0:T(8,128)(2,1)S(1)} %get-tuple-element.36.white), channel_id=1, source_target_pairs={{4,0},{5,1},{6,2},{7,3},{8,4},{9,5},{10,6},{11,7},{12,8},{13,9},{1... | collective-permute-start | bytes 1572872 | tf_op jit(solution)/shard_map/ppermute | solution.py:246
  53.4 13.1 %collective-permute-start.14 = (bf16[256,1024]{1,0:T(8,128)(2,1)S(1)}, bf16[256,1024]{1,0:T(8,128)(2,1)S(1)}, u32[]{:S(2)}, u32[]{:S(2)}) collective-permute-start(bf16[256,1024]{1,0:T(8,128)(2,1)S(1)} %collective-permute-done.9.across), channel_id=1, source_target_pairs={{6,2},{7,3},{10,6},{11,7},{14,10},{15,11},{22,18},{23,19},{26,22},... | collective-permute-start | bytes 1572872 | tf_op jit(solution)/shard_map/ppermute | solution.py:246
  54.6 16.8 %collective-permute-start.11 = (bf16[256,1024]{1,0:T(8,128)(2,1)S(1)}, bf16[256,1024]{1,0:T(8,128)(2,1)S(1)}, u32[]{:S(2)}, u32[]{:S(2)}) collective-permute-start(bf16[256,1024]{1,0:T(8,128)(2,1)S(1)} %get-tuple-element.36.white), channel_id=1, source_target_pairs={{1,0},{3,2},{5,4},{7,6},{9,8},{11,10},{13,12},{15,14},{17,16},{19,... | collective-permute-start | bytes 1572872 | tf_op jit(solution)/shard_map/ppermute | solution.py:246
  58.8 16.0 %collective-permute-start.13 = (bf16[256,1024]{1,0:T(8,128)(2,1)S(1)}, bf16[256,1024]{1,0:T(8,128)(2,1)S(1)}, u32[]{:S(2)}, u32[]{:S(2)}) collective-permute-start(bf16[256,1024]{1,0:T(8,128)(2,1)S(1)} %collective-permute-done.8.four), channel_id=1, source_target_pairs={{4,1},{6,3},{8,5},{10,7},{12,9},{14,11},{20,17},{22,19},{24,21},{2... | collective-permute-start | bytes 1572872 | tf_op jit(solution)/shard_map/ppermute | solution.py:246
  60.1 14.7 %collective-permute-start.12 = (bf16[256,1024]{1,0:T(8,128)(2,1)S(1)}, bf16[256,1024]{1,0:T(8,128)(2,1)S(1)}, u32[]{:S(2)}, u32[]{:S(2)}) collective-permute-start(bf16[256,1024]{1,0:T(8,128)(2,1)S(1)} %collective-permute-done.8.four), channel_id=1, source_target_pairs={{0,1},{1,0},{2,3},{3,2},{4,5},{5,4},{6,7},{7,6},{8,9},{9,8},{10,11... | collective-permute-start | bytes 1572872 | tf_op jit(solution)/shard_map/ppermute | solution.py:246
  60.2 22.2 %collective-permute-start.10 = (bf16[256,1024]{1,0:T(8,128)(2,1)S(1)}, bf16[256,1024]{1,0:T(8,128)(2,1)S(1)}, u32[]{:S(2)}, u32[]{:S(2)}) collective-permute-start(bf16[256,1024]{1,0:T(8,128)(2,1)S(1)} %collective-permute-done.8.four), channel_id=1, source_target_pairs={{2,0},{3,1},{4,2},{5,3},{6,4},{7,5},{8,6},{9,7},{10,8},{11,9},{12,... | collective-permute-start | bytes 1572872 | tf_op jit(solution)/shard_map/ppermute | solution.py:246
  66.4 15.9 %collective-permute-start.15 = (bf16[256,1024]{1,0:T(8,128)(2,1)S(1)}, bf16[256,1024]{1,0:T(8,128)(2,1)S(1)}, u32[]{:S(2)}, u32[]{:S(2)}) collective-permute-start(bf16[256,1024]{1,0:T(8,128)(2,1)S(1)} %collective-permute-done.14.two), channel_id=1, source_target_pairs={{2,3},{3,2},{6,7},{7,6},{10,11},{11,10},{14,15},{15,14},{18,19},{1... | collective-permute-start | bytes 1572872 | tf_op jit(solution)/shard_map/ppermute | solution.py:246
  71.5 11.0 %collective-permute-start.17 = (bf16[256,1024]{1,0:T(8,128)(2,1)S(1)}, bf16[256,1024]{1,0:T(8,128)(2,1)S(1)}, u32[]{:S(2)}, u32[]{:S(2)}) collective-permute-start(bf16[256,1024]{1,0:T(8,128)(2,1)S(1)} %collective-permute-done.9.across), channel_id=1, source_target_pairs={{0,1},{1,0},{4,5},{5,4},{8,9},{9,8},{12,13},{13,12},{16,17},{17,16... | collective-permute-start | bytes 1572872 | tf_op jit(solution)/shard_map/ppermute | solution.py:246
  82.4 2.0 %collective-permute-start.16 = (bf16[256,1024]{1,0:T(8,128)(2,1)S(1)}, bf16[256,1024]{1,0:T(8,128)(2,1)S(1)}, u32[]{:S(2)}, u32[]{:S(2)}) collective-permute-start(bf16[256,1024]{1,0:T(8,128)(2,1)S(1)} %collective-permute-done.10.six), channel_id=1, source_target_pairs={{0,1},{1,0},{2,3},{3,2},{4,5},{5,4},{6,7},{7,6},{8,9},{9,8},{10,11... | collective-permute-start | bytes 1572872 | tf_op jit(solution)/shard_map/ppermute | solution.py:246

commit v5 on v4

--- a/solution.py
+++ b/solution.py
@@ -328,12 +328,15 @@
     pl.when(first & near_side)(pltpu.make_async_copy(across, columns, sem).start)
     pl.when(first & jnp.logical_not(near_side))(pltpu.make_async_copy(two, columns, sem).start)
     pl.when(first)(pltpu.make_async_copy(two, columns, sem).wait)
-    left = lagged[pl.program_id(0)]
-    out[0, 0] = pair(left, four[...], band, 4)
-    out[1, 0] = pair(left, four_beside[...], band, by_parity(5, 3))
-    out[2, 0] = pair(left, one[...], band, 1)
-    out[3, 0] = pair(left, seven[...], band, 7)
-    out[4, 0] = pair(left, columns[...], band, 2)
+    group, channels = out.shape[1], out.shape[2]
+    at = pl.ds(pl.program_id(0) * group, group)
+    left = lagged[at].reshape(group * channels, 2 * NF)
+    shape = (group, channels, channels)
+    out[0] = pair(left, four[...], band, 4).reshape(shape)
+    out[1] = pair(left, four_beside[...], band, by_parity(5, 3)).reshape(shape)
+    out[2] = pair(left, one[...], band, 1).reshape(shape)
+    out[3] = pair(left, seven[...], band, 7).reshape(shape)
+    out[4] = pair(left, columns[...], band, 2).reshape(shape)
 
 
 def correlate_near(band, lagged, *tiles):
@@ -341,11 +344,11 @@
     return pl.pallas_call(
         near_body,
         out_shape=jax.ShapeDtypeStruct((5, LAGS, channels, channels), HALF),
-        grid=(LAGS,),
+        grid=(LAGS // 2,),
         in_specs=[SCALAR] + [WHOLE] * 5 + [pl.BlockSpec(memory_space=pl.ANY)] * 2,
-        out_specs=pl.BlockSpec((5, 1, channels, channels), lambda i: (0, i, 0, 0)),
+        out_specs=pl.BlockSpec((5, 2, channels, channels), lambda i: (0, i, 0, 0)),
         scratch_shapes=[pltpu.VMEM((channels, 2 * NF), HALF), pltpu.SemaphoreType.DMA],
-        compiler_params=pltpu.CompilerParams(vmem_limit_bytes=16 << 20),
+        compiler_params=pltpu.CompilerParams(vmem_limit_bytes=24 << 20),
         cost_estimate=cost(channels, 5),
         name="correlate_near",
     )(band, lagged, *tiles)
@@ -396,7 +399,7 @@
 
 def correlate_far(band, lagged, own, near, *tiles):
     channels = lagged.shape[1]
-    rows = 32
+    rows = 64
     return pl.pallas_call(
         functools.partial(far_body, rows=rows),
         out_shape=jax.ShapeDtypeStruct((channels, LAGS, NB, channels), HALF),
@@ -404,7 +407,7 @@
         in_specs=[SCALAR] + [WHOLE] * 5 + [pl.BlockSpec(memory_space=pl.ANY)] * 2,
         out_specs=pl.BlockSpec((rows, LAGS, NB, channels), lambda i: (i, 0, 0, 0)),
         scratch_shapes=[pltpu.VMEM((channels, 2 * NF), HALF), pltpu.SemaphoreType.DMA],
-        compiler_params=pltpu.CompilerParams(vmem_limit_bytes=24 << 20),
+        compiler_params=pltpu.CompilerParams(vmem_limit_bytes=32 << 20),
         cost_estimate=cost(channels, 3),
         name="correlate_far",
     )(band, lagged, own, near, *tiles)
@@ -420,6 +423,8 @@
     one, four, across = gather_first(white)
     lagged, own = correlate_own(band_width, real, imag, white)
     four, across, lagged = lax.optimization_barrier((four, across, lagged))
+    one, lagged = lax.optimization_barrier((one, lagged))
+    across, lagged = lax.optimization_barrier((across, lagged))
     two, six, seven = gather_second(four, across)
     across_beside = beside(across, lambda s: s & 2 == 0)
     four_beside = beside(four)

time: 92.6 us -> 90.9 us (0.982)
  starting transfers between devices: 27.9 us -> 29.8 us
  waiting for transfers between devices: 35.3 us -> 33.4 us
  Pallas kernels: 26.2 us -> 24.6 us
    ppermute x10, waiting for transfers between devices: 22.5 us -> 20.5 us  [send(): return lax.ppermute(value, 'row', pairs)]
    ppermute x10, starting transfers between devices: 17.8 us -> 19.7 us  [send(): return lax.ppermute(value, 'row', pairs)]
  transfers between devices with their start and end apart: 18 -> 18, of which waited for: 9 -> 8; matrix products, arithmetic and copies ran while one was open for 1% -> 1% of each run, Pallas kernels for 11% -> 11%
where the time goes in v5:
time: 90.9 us; the launch traced here: 90.7 us
  waiting for transfers between devices  33.4 us (37%)
  starting transfers between devices  29.8 us (33%)
  Pallas kernels  24.6 us (27%)
  between operations  1.54 us (2%)
  local copies, waits for them, and re-layouts  1.22 us (1%)
    ppermute x10, waiting for transfers between devices, send(): return lax.ppermute(value, 'row', pairs)  20.5 us
    ppermute x10, starting transfers between devices, send(): return lax.ppermute(value, 'row', pairs)  19.7 us
    ppermute x7, waiting for transfers between devices, transpose_blocks(): lax.ppermute(pieces[d], 'row', [(s, s ^ 2 * d) for s in range(tiles)])  12.3 us
    ppermute x7, starting transfers between devices, transpose_blocks(): lax.ppermute(pieces[d], 'row', [(s, s ^ 2 * d) for s in range(tiles)])  9.36 us
    pallas_call x1, Pallas kernels, correlate_far(): pl.pallas_call(functools.partial(far_body, rows=rows), out_shape=jax.Shap...  7.15 us
    pallas_call x1, Pallas kernels, correlate_near(): pl.pallas_call(near_body, out_shape=jax.ShapeDtypeStruct((5, LAGS, channe...  6.69 us
    pallas_call x1, Pallas kernels, filter_blocks(): pl.pallas_call(functools.partial(filter_body, channels=channels), out_sha...  5.85 us
    pallas_call x1, Pallas kernels, correlate_own(): pl.pallas_call(own_body, out_shape=(jax.ShapeDtypeStruct((LAGS, channels,...  3.06 us
  transfers between devices with their start and end apart: 18, of which 8 were waited for; matrix products, arithmetic and copies ran while one was open for 1% of the time, Pallas kernels for 11%

profile of v5, /device:TPU:3, one launch (start us, length us, event | category | flops | bytes accessed | tf_op | source)
XLA Modules:
  0.0 90.7 jit_solution(1874529947290461700)
XLA Ops:
  0.0 5.8 %filter.1 = (bf16[8,264,128]{2,1,0:T(8,128)(2,1)}, bf16[8,264,128]{2,1,0:T(8,128)(2,1)}) custom-call(f32[16]{0:T(128)} %taps.1, bf16[4096,512]{1,0:T(8,128)(2,1)} %raw.1), custom_call_target="tpu_custom_call" | custom-call | tf_op jit(solution)/shard_map/filter/pallas_call | solution.py:124
  6.6 1.1 %slice_bitcast_fusion.8 = (bf16[264,128]{1,0:T(8,128)(2,1)S(1)}, bf16[264,128]{1,0:T(8,128)(2,1)S(1)}, bf16[264,128]{1,0:T(8,128)(2,1)S(1)}, bf16[264,128]{1,0:T...) fusion(bf16[8,264,128]{2,1,0:T(8,128)(2,1)} %get-tuple-element.30), kind=kLoop, calls=%fused_computation.16 | loop fusion | bytes 1081344 | tf_op jit(solution)/shard_map/squeeze | solution.py:150
  8.6 1.5 %collective-permute-start.2 = (bf16[528,128]{1,0:T(8,128)(2,1)S(1)}, bf16[528,128]{1,0:T(8,128)(2,1)S(1)}, u32[]{:S(2)}, u32[]{:S(2)}) collective-permute-start(bf16[528,128]{1,0:T(8,128)(2,1)S(1)} %get-tuple-element.34), channel_id=1, source_target_pairs={{0,4},{1,5},{2,6},{3,7},{4,0},{5,1},{6,2},{7,3},{8,12},{9,13},{10,... | collective-permute-start | bytes 405512 | tf_op jit(solution)/shard_map/ppermute | solution.py:153
  11.3 2.3 %collective-permute-start.4 = (bf16[528,128]{1,0:T(8,128)(2,1)S(1)}, bf16[528,128]{1,0:T(8,128)(2,1)S(1)}, u32[]{:S(2)}, u32[]{:S(2)}) collective-permute-start(bf16[528,128]{1,0:T(8,128)(2,1)S(1)} %get-tuple-element.36), channel_id=1, source_target_pairs={{0,8},{1,9},{2,10},{3,11},{4,12},{5,13},{6,14},{7,15},{8,0},{9,1},... | collective-permute-start | bytes 405512 | tf_op jit(solution)/shard_map/ppermute | solution.py:153
  13.6 3.3 %collective-permute-start.6 = (bf16[528,128]{1,0:T(8,128)(2,1)S(1)}, bf16[528,128]{1,0:T(8,128)(2,1)S(1)}, u32[]{:S(2)}, u32[]{:S(2)}) collective-permute-start(bf16[528,128]{1,0:T(8,128)(2,1)S(1)} %get-tuple-element.38), channel_id=1, source_target_pairs={{0,12},{1,13},{2,14},{3,15},{4,8},{5,9},{6,10},{7,11},{8,4},{9,5},... | collective-permute-start | bytes 405512 | tf_op jit(solution)/shard_map/ppermute | solution.py:153
  18.6 3.3 %collective-permute-done.3.rest_3_ = bf16[528,128]{1,0:T(8,128)(2,1)S(1)} collective-permute-done((bf16[528,128]{1,0:T(8,128)(2,1)S(1)}, bf16[528,128]{1,0:T(8,128)(2,1)S(1)}, u32[]{:S(2)}, u32[]{:S(2)}) %collective-permute-start.3) | collective-permute-done | bytes 135200 | tf_op jit(solution)/shard_map/ppermute | solution.py:153
  21.9 5.5 %collective-permute-done.6.rest_6_ = bf16[528,128]{1,0:T(8,128)(2,1)S(1)} collective-permute-done((bf16[528,128]{1,0:T(8,128)(2,1)S(1)}, bf16[528,128]{1,0:T(8,128)(2,1)S(1)}, u32[]{:S(2)}, u32[]{:S(2)}) %collective-permute-start.6) | collective-permute-done | bytes 135200 | tf_op jit(solution)/shard_map/ppermute | solution.py:153
  27.4 3.5 %collective-permute-done.7.rest_7_ = bf16[528,128]{1,0:T(8,128)(2,1)S(1)} collective-permute-done((bf16[528,128]{1,0:T(8,128)(2,1)S(1)}, bf16[528,128]{1,0:T(8,128)(2,1)S(1)}, u32[]{:S(2)}, u32[]{:S(2)}) %collective-permute-start.7) | collective-permute-done | bytes 135200 | tf_op jit(solution)/shard_map/ppermute | solution.py:153
  30.9 1.9 %whiten.1 = (bf16[256,1024]{1,0:T(8,128)(2,1)S(1)}, f32[256,512]{1,0:T(8,128)S(1)}, f32[256,512]{1,0:T(8,128)S(1)}) custom-call(s32[1]{0:T(128)S(6)} %copy.12.dead, bf16[2048,1024]{1,0:T(8,128)(2,1)S(1)} %copy-done, bf16[128,1024]{1,0:T(8,128)(2,1)S(1)} %copy-done.2, bf16[512,512]{1,0:T(8,128)(2,1)S(1)} %copy-done.1, f32[1,512]{1,0:T(1,128)S(1)} %copy-done.3, ...), custom_call_target="tpu_custom_call" | custom-call | tf_op jit(solution)/shard_map/whiten/pallas_call | solution.py:220
  32.7 2.0 %collective-permute-start.9 = (bf16[256,1024]{1,0:T(8,128)(2,1)S(1)}, bf16[256,1024]{1,0:T(8,128)(2,1)S(1)}, u32[]{:S(2)}, u32[]{:S(2)}) collective-permute-start(bf16[256,1024]{1,0:T(8,128)(2,1)S(1)} %get-tuple-element.40.white), channel_id=1, source_target_pairs={{0,2},{1,3},{2,0},{3,1},{4,6},{5,7},{6,4},{7,5},{8,10},{9,11},{10,... | collective-permute-start | bytes 1572872 | tf_op jit(solution)/shard_map/ppermute | solution.py:246
  34.7 1.3 %collective-permute-start.8 = (bf16[256,1024]{1,0:T(8,128)(2,1)S(1)}, bf16[256,1024]{1,0:T(8,128)(2,1)S(1)}, u32[]{:S(2)}, u32[]{:S(2)}) collective-permute-start(bf16[256,1024]{1,0:T(8,128)(2,1)S(1)} %get-tuple-element.40.white), channel_id=1, source_target_pairs={{4,0},{5,1},{6,2},{7,3},{8,4},{9,5},{10,6},{11,7},{12,8},{13,9},{1... | collective-permute-start | bytes 1572872 | tf_op jit(solution)/shard_map/ppermute | solution.py:246
  36.0 4.4 %collective-permute-start.10 = (bf16[256,1024]{1,0:T(8,128)(2,1)S(1)}, bf16[256,1024]{1,0:T(8,128)(2,1)S(1)}, u32[]{:S(2)}, u32[]{:S(2)}) collective-permute-start(bf16[256,1024]{1,0:T(8,128)(2,1)S(1)} %get-tuple-element.40.white), channel_id=1, source_target_pairs={{1,0},{3,2},{5,4},{7,6},{9,8},{11,10},{13,12},{15,14},{17,16},{19,... | collective-permute-start | bytes 1572872 | tf_op jit(solution)/shard_map/ppermute | solution.py:246
  41.1 3.1 %correlate_own.1 = (bf16[8,256,1024]{2,1,0:T(8,128)(2,1)S(1)}, bf16[8,256,256]{2,1,0:T(8,128)(2,1)S(1)}) custom-call(s32[1]{0:T(128)S(6)} %copy.11.band, f32[256,512]{1,0:T(8,128)S(1)} %get-tuple-element.41.real, f32[256,512]{1,0:T(8,128)S(1)} %get-tuple-element.42.imag, f32[8,1,512]{2,1,0:T(1,128)S(1)} %copy-done.5, f32[8,1,512]{2,1,0:T(1,128)S(1)} %copy-done.4, ...), custom_call_target="tpu_custom_call" | custom-call | flops 1073741824 | bytes 5242880 | tf_op jit(solution)/shard_map/correlate_own/pallas_call | solution.py:300
  44.2 9.1 %collective-permute-done.8.four = bf16[256,1024]{1,0:T(8,128)(2,1)S(1)} collective-permute-done((bf16[256,1024]{1,0:T(8,128)(2,1)S(1)}, bf16[256,1024]{1,0:T(8,128)(2,1)S(1)}, u32[]{:S(2)}, u32[]{:S(2)}) %collective-permute-start.8) | collective-permute-done | bytes 524320 | tf_op jit(solution)/shard_map/ppermute | solution.py:246
  53.4 1.3 %collective-permute-start.14 = (bf16[256,1024]{1,0:T(8,128)(2,1)S(1)}, bf16[256,1024]{1,0:T(8,128)(2,1)S(1)}, u32[]{:S(2)}, u32[]{:S(2)}) collective-permute-start(bf16[256,1024]{1,0:T(8,128)(2,1)S(1)} %collective-permute-done.9.across), channel_id=1, source_target_pairs={{6,2},{7,3},{10,6},{11,7},{14,10},{15,11},{22,18},{23,19},{26,22},... | collective-permute-start | bytes 1572872 | tf_op jit(solution)/shard_map/ppermute | solution.py:246
  54.6 1.3 %collective-permute-start.13 = (bf16[256,1024]{1,0:T(8,128)(2,1)S(1)}, bf16[256,1024]{1,0:T(8,128)(2,1)S(1)}, u32[]{:S(2)}, u32[]{:S(2)}) collective-permute-start(bf16[256,1024]{1,0:T(8,128)(2,1)S(1)} %collective-permute-done.8.four), channel_id=1, source_target_pairs={{4,1},{6,3},{8,5},{10,7},{12,9},{14,11},{20,17},{22,19},{24,21},{2... | collective-permute-start | bytes 1572872 | tf_op jit(solution)/shard_map/ppermute | solution.py:246
  55.9 1.7 %collective-permute-start.12 = (bf16[256,1024]{1,0:T(8,128)(2,1)S(1)}, bf16[256,1024]{1,0:T(8,128)(2,1)S(1)}, u32[]{:S(2)}, u32[]{:S(2)}) collective-permute-start(bf16[256,1024]{1,0:T(8,128)(2,1)S(1)} %collective-permute-done.8.four), channel_id=1, source_target_pairs={{0,1},{1,0},{2,3},{3,2},{4,5},{5,4},{6,7},{7,6},{8,9},{9,8},{10,11... | collective-permute-start | bytes 1572872 | tf_op jit(solution)/shard_map/ppermute | solution.py:246
  57.6 1.9 %collective-permute-start.11 = (bf16[256,1024]{1,0:T(8,128)(2,1)S(1)}, bf16[256,1024]{1,0:T(8,128)(2,1)S(1)}, u32[]{:S(2)}, u32[]{:S(2)}) collective-permute-start(bf16[256,1024]{1,0:T(8,128)(2,1)S(1)} %collective-permute-done.8.four), channel_id=1, source_target_pairs={{2,0},{3,1},{4,2},{5,3},{6,4},{7,5},{8,6},{9,7},{10,8},{11,9},{12,... | collective-permute-start | bytes 1572872 | tf_op jit(solution)/shard_map/ppermute | solution.py:246
  59.5 6.9 %collective-permute-done.14.two = bf16[256,1024]{1,0:T(8,128)(2,1)S(1)} collective-permute-done((bf16[256,1024]{1,0:T(8,128)(2,1)S(1)}, bf16[256,1024]{1,0:T(8,128)(2,1)S(1)}, u32[]{:S(2)}, u32[]{:S(2)}) %collective-permute-start.14) | collective-permute-done | bytes 524320 | tf_op jit(solution)/shard_map/ppermute | solution.py:246
  66.4 5.0 %collective-permute-start.15 = (bf16[256,1024]{1,0:T(8,128)(2,1)S(1)}, bf16[256,1024]{1,0:T(8,128)(2,1)S(1)}, u32[]{:S(2)}, u32[]{:S(2)}) collective-permute-start(bf16[256,1024]{1,0:T(8,128)(2,1)S(1)} %collective-permute-done.14.two), channel_id=1, source_target_pairs={{2,3},{3,2},{6,7},{7,6},{10,11},{11,10},{14,15},{15,14},{18,19},{1... | collective-permute-start | bytes 1572872 | tf_op jit(solution)/shard_map/ppermute | solution.py:246
  72.2 2.6 %collective-permute-done.13.seven = bf16[256,1024]{1,0:T(8,128)(2,1)S(1)} collective-permute-done((bf16[256,1024]{1,0:T(8,128)(2,1)S(1)}, bf16[256,1024]{1,0:T(8,128)(2,1)S(1)}, u32[]{:S(2)}, u32[]{:S(2)}) %collective-permute-start.13) | collective-permute-done | bytes 524320 | tf_op jit(solution)/shard_map/ppermute | solution.py:246
  74.8 6.7 %correlate_near.1.near = bf16[5,8,256,256]{3,2,1,0:T(8,128)(2,1)S(1)} custom-call(s32[1]{0:T(128)S(6)} %copy.11.band, bf16[8,256,1024]{2,1,0:T(8,128)(2,1)S(1)} %get-tuple-element.47.lagged, bf16[256,1024]{1,0:T(8,128)(2,1)S(1)} %collective-permute-done.10.one, bf16[256,1024]{1,0:T(8,128)(2,1)S(1)} %collective-permute-done.8.four, ...), custom_call_target="tpu_custom_call" | custom-call | flops 5368709120 | bytes 9437184 | tf_op jit(solution)/shard_map/correlate_near/pallas_call | solution.py:344
  81.6 1.9 %collective-permute-done.16.six_beside = bf16[256,1024]{1,0:T(8,128)(2,1)S(1)} collective-permute-done((bf16[256,1024]{1,0:T(8,128)(2,1)S(1)}, bf16[256,1024]{1,0:T(8,128)(2,1)S(1)}, u32[]{:S(2)}, u32[]{:S(2)}) %collective-permute-start.16) | collective-permute-done | bytes 524320 | tf_op jit(solution)/shard_map/ppermute | solution.py:246
  83.5 7.2 %correlate_far.1 = bf16[256,8,8,256]{3,2,1,0:T(8,128)(2,1)} custom-call(s32[1]{0:T(128)S(6)} %copy.11.band, bf16[8,256,1024]{2,1,0:T(8,128)(2,1)S(1)} %get-tuple-element.47.lagged, bf16[8,256,256]{2,1,0:T(8,128)(2,1)S(1)} %get-tuple-element.48.own, bf16[5,8,256,256]{3,2,1,0:T(8,128)(2,1)S(1)} %correlate_near.1.near, ...), custom_call_target="tpu_custom_call" | custom-call | flops 3221225472 | bytes 7340032 | tf_op jit(solution)/shard_map/correlate_far/pallas_call | solution.py:403
  (35 shorter events, 4.5 us)
Async XLA Ops:
  0.0 30.9 %copy-start = (bf16[2048,1024]{1,0:T(8,128)(2,1)S(1)}, bf16[2048,1024]{1,0:T(8,128)(2,1)}, u32[]{:S(2)}) copy-start(bf16[2048,1024]{1,0:T(8,128)(2,1)} %constant.12.clone.table) | copy-start | bytes 12582916
  0.0 30.9 %copy-start.1 = (bf16[512,512]{1,0:T(8,128)(2,1)S(1)}, bf16[512,512]{1,0:T(8,128)(2,1)}, u32[]{:S(2)}) copy-start(bf16[512,512]{1,0:T(8,128)(2,1)} %constant.14.clone.window) | copy-start | bytes 1572868
  0.0 30.9 %copy-start.2 = (bf16[128,1024]{1,0:T(8,128)(2,1)S(1)}, bf16[128,1024]{1,0:T(8,128)(2,1)}, u32[]{:S(2)}) copy-start(bf16[128,1024]{1,0:T(8,128)(2,1)} %constant.13.clone.edge_table) | copy-start | bytes 786436
  0.0 30.9 %copy-start.3 = (f32[1,512]{1,0:T(1,128)S(1)}, f32[1,512]{1,0:T(1,128)}, u32[]{:S(2)}) copy-start(f32[1,512]{1,0:T(1,128)} %constant.15.clone.counts) | copy-start | bytes 6148
  5.9 2.5 %collective-permute-start = (bf16[8,264,128]{2,1,0:T(8,128)(2,1)}, bf16[8,264,128]{2,1,0:T(8,128)(2,1)S(1)}, u32[]{:S(2)}, u32[]{:S(2)}) collective-permute-start(bf16[8,264,128]{2,1,0:T(8,128)(2,1)} %get-tuple-element.31), channel_id=1, source_target_pairs={{0,1},{1,0},{2,3},{3,2},{4,5},{5,4},{6,7},{7,6},{8,9},{9,8},{10,11... | collective-permute-start | bytes 1622024 | tf_op jit(solution)/shard_map/ppermute | solution.py:149
  8.4 32.7 %copy-start.4 = (f32[8,1,512]{2,1,0:T(1,128)S(1)}, f32[8,1,512]{2,1,0:T(1,128)}, u32[]{:S(2)}) copy-start(f32[8,1,512]{2,1,0:T(1,128)} %constant.17.clone.sine) | copy-start | bytes 49156
  8.4 32.7 %copy-start.5 = (f32[8,1,512]{2,1,0:T(1,128)S(1)}, f32[8,1,512]{2,1,0:T(1,128)}, u32[]{:S(2)}) copy-start(f32[8,1,512]{2,1,0:T(1,128)} %constant.16.clone.cosine) | copy-start | bytes 49156
  8.6 5.0 %collective-permute-start.1 = (bf16[528,128]{1,0:T(8,128)(2,1)S(1)}, bf16[528,128]{1,0:T(8,128)(2,1)S(1)}, u32[]{:S(2)}, u32[]{:S(2)}) collective-permute-start(bf16[528,128]{1,0:T(8,128)(2,1)S(1)} %get-tuple-element.33), channel_id=1, source_target_pairs={{0,2},{1,3},{2,0},{3,1},{4,6},{5,7},{6,4},{7,5},{8,10},{9,11},{10,... | collective-permute-start | bytes 405512 | tf_op jit(solution)/shard_map/ppermute | solution.py:153
  8.6 8.3 %collective-permute-start.2 = (bf16[528,128]{1,0:T(8,128)(2,1)S(1)}, bf16[528,128]{1,0:T(8,128)(2,1)S(1)}, u32[]{:S(2)}, u32[]{:S(2)}) collective-permute-start(bf16[528,128]{1,0:T(8,128)(2,1)S(1)} %get-tuple-element.34), channel_id=1, source_target_pairs={{0,4},{1,5},{2,6},{3,7},{4,0},{5,1},{6,2},{7,3},{8,12},{9,13},{10,... | collective-permute-start | bytes 405512 | tf_op jit(solution)/shard_map/ppermute | solution.py:153
  10.2 11.7 %collective-permute-start.3 = (bf16[528,128]{1,0:T(8,128)(2,1)S(1)}, bf16[528,128]{1,0:T(8,128)(2,1)S(1)}, u32[]{:S(2)}, u32[]{:S(2)}) collective-permute-start(bf16[528,128]{1,0:T(8,128)(2,1)S(1)} %get-tuple-element.35), channel_id=1, source_target_pairs={{0,6},{1,7},{2,4},{3,5},{4,2},{5,3},{6,0},{7,1},{8,14},{9,15},{10,... | collective-permute-start | bytes 405512 | tf_op jit(solution)/shard_map/ppermute | solution.py:153
  11.3 10.6 %collective-permute-start.4 = (bf16[528,128]{1,0:T(8,128)(2,1)S(1)}, bf16[528,128]{1,0:T(8,128)(2,1)S(1)}, u32[]{:S(2)}, u32[]{:S(2)}) collective-permute-start(bf16[528,128]{1,0:T(8,128)(2,1)S(1)} %get-tuple-element.36), channel_id=1, source_target_pairs={{0,8},{1,9},{2,10},{3,11},{4,12},{5,13},{6,14},{7,15},{8,0},{9,1},... | collective-permute-start | bytes 405512 | tf_op jit(solution)/shard_map/ppermute | solution.py:153
  13.6 8.3 %collective-permute-start.5 = (bf16[528,128]{1,0:T(8,128)(2,1)S(1)}, bf16[528,128]{1,0:T(8,128)(2,1)S(1)}, u32[]{:S(2)}, u32[]{:S(2)}) collective-permute-start(bf16[528,128]{1,0:T(8,128)(2,1)S(1)} %get-tuple-element.37), channel_id=1, source_target_pairs={{0,10},{1,11},{2,8},{3,9},{4,14},{5,15},{6,12},{7,13},{8,2},{9,3},... | collective-permute-start | bytes 405512 | tf_op jit(solution)/shard_map/ppermute | solution.py:153
  13.6 13.8 %collective-permute-start.6 = (bf16[528,128]{1,0:T(8,128)(2,1)S(1)}, bf16[528,128]{1,0:T(8,128)(2,1)S(1)}, u32[]{:S(2)}, u32[]{:S(2)}) collective-permute-start(bf16[528,128]{1,0:T(8,128)(2,1)S(1)} %get-tuple-element.38), channel_id=1, source_target_pairs={{0,12},{1,13},{2,14},{3,15},{4,8},{5,9},{6,10},{7,11},{8,4},{9,5},... | collective-permute-start | bytes 405512 | tf_op jit(solution)/shard_map/ppermute | solution.py:153
  17.0 13.9 %collective-permute-start.7 = (bf16[528,128]{1,0:T(8,128)(2,1)S(1)}, bf16[528,128]{1,0:T(8,128)(2,1)S(1)}, u32[]{:S(2)}, u32[]{:S(2)}) collective-permute-start(bf16[528,128]{1,0:T(8,128)(2,1)S(1)} %get-tuple-element.39), channel_id=1, source_target_pairs={{0,14},{1,15},{2,12},{3,13},{4,10},{5,11},{6,8},{7,9},{8,6},{9,7},... | collective-permute-start | bytes 405512 | tf_op jit(solution)/shard_map/ppermute | solution.py:153
  32.7 11.5 %collective-permute-start.9 = (bf16[256,1024]{1,0:T(8,128)(2,1)S(1)}, bf16[256,1024]{1,0:T(8,128)(2,1)S(1)}, u32[]{:S(2)}, u32[]{:S(2)}) collective-permute-start(bf16[256,1024]{1,0:T(8,128)(2,1)S(1)} %get-tuple-element.40.white), channel_id=1, source_target_pairs={{0,2},{1,3},{2,0},{3,1},{4,6},{5,7},{6,4},{7,5},{8,10},{9,11},{10,... | collective-permute-start | bytes 1572872 | tf_op jit(solution)/shard_map/ppermute | solution.py:246
  34.7 18.6 %collective-permute-start.8 = (bf16[256,1024]{1,0:T(8,128)(2,1)S(1)}, bf16[256,1024]{1,0:T(8,128)(2,1)S(1)}, u32[]{:S(2)}, u32[]{:S(2)}) collective-permute-start(bf16[256,1024]{1,0:T(8,128)(2,1)S(1)} %get-tuple-element.40.white), channel_id=1, source_target_pairs={{4,0},{5,1},{6,2},{7,3},{8,4},{9,5},{10,6},{11,7},{12,8},{13,9},{1... | collective-permute-start | bytes 1572872 | tf_op jit(solution)/shard_map/ppermute | solution.py:246
  36.0 17.3 %collective-permute-start.10 = (bf16[256,1024]{1,0:T(8,128)(2,1)S(1)}, bf16[256,1024]{1,0:T(8,128)(2,1)S(1)}, u32[]{:S(2)}, u32[]{:S(2)}) collective-permute-start(bf16[256,1024]{1,0:T(8,128)(2,1)S(1)} %get-tuple-element.40.white), channel_id=1, source_target_pairs={{1,0},{3,2},{5,4},{7,6},{9,8},{11,10},{13,12},{15,14},{17,16},{19,... | collective-permute-start | bytes 1572872 | tf_op jit(solution)/shard_map/ppermute | solution.py:246
  53.4 13.1 %collective-permute-start.14 = (bf16[256,1024]{1,0:T(8,128)(2,1)S(1)}, bf16[256,1024]{1,0:T(8,128)(2,1)S(1)}, u32[]{:S(2)}, u32[]{:S(2)}) collective-permute-start(bf16[256,1024]{1,0:T(8,128)(2,1)S(1)} %collective-permute-done.9.across), channel_id=1, source_target_pairs={{6,2},{7,3},{10,6},{11,7},{14,10},{15,11},{22,18},{23,19},{26,22},... | collective-permute-start | bytes 1572872 | tf_op jit(solution)/shard_map/ppermute | solution.py:246
  54.6 20.2 %collective-permute-start.13 = (bf16[256,1024]{1,0:T(8,128)(2,1)S(1)}, bf16[256,1024]{1,0:T(8,128)(2,1)S(1)}, u32[]{:S(2)}, u32[]{:S(2)}) collective-permute-start(bf16[256,1024]{1,0:T(8,128)(2,1)S(1)} %collective-permute-done.8.four), channel_id=1, source_target_pairs={{4,1},{6,3},{8,5},{10,7},{12,9},{14,11},{20,17},{22,19},{24,21},{2... | collective-permute-start | bytes 1572872 | tf_op jit(solution)/shard_map/ppermute | solution.py:246
  55.9 18.9 %collective-permute-start.12 = (bf16[256,1024]{1,0:T(8,128)(2,1)S(1)}, bf16[256,1024]{1,0:T(8,128)(2,1)S(1)}, u32[]{:S(2)}, u32[]{:S(2)}) collective-permute-start(bf16[256,1024]{1,0:T(8,128)(2,1)S(1)} %collective-permute-done.8.four), channel_id=1, source_target_pairs={{0,1},{1,0},{2,3},{3,2},{4,5},{5,4},{6,7},{7,6},{8,9},{9,8},{10,11... | collective-permute-start | bytes 1572872 | tf_op jit(solution)/shard_map/ppermute | solution.py:246
  57.6 23.9 %collective-permute-start.11 = (bf16[256,1024]{1,0:T(8,128)(2,1)S(1)}, bf16[256,1024]{1,0:T(8,128)(2,1)S(1)}, u32[]{:S(2)}, u32[]{:S(2)}) collective-permute-start(bf16[256,1024]{1,0:T(8,128)(2,1)S(1)} %collective-permute-done.8.four), channel_id=1, source_target_pairs={{2,0},{3,1},{4,2},{5,3},{6,4},{7,5},{8,6},{9,7},{10,8},{11,9},{12,... | collective-permute-start | bytes 1572872 | tf_op jit(solution)/shard_map/ppermute | solution.py:246
  66.4 15.1 %collective-permute-start.15 = (bf16[256,1024]{1,0:T(8,128)(2,1)S(1)}, bf16[256,1024]{1,0:T(8,128)(2,1)S(1)}, u32[]{:S(2)}, u32[]{:S(2)}) collective-permute-start(bf16[256,1024]{1,0:T(8,128)(2,1)S(1)} %collective-permute-done.14.two), channel_id=1, source_target_pairs={{2,3},{3,2},{6,7},{7,6},{10,11},{11,10},{14,15},{15,14},{18,19},{1... | collective-permute-start | bytes 1572872 | tf_op jit(solution)/shard_map/ppermute | solution.py:246
  71.5 10.1 %collective-permute-start.17 = (bf16[256,1024]{1,0:T(8,128)(2,1)S(1)}, bf16[256,1024]{1,0:T(8,128)(2,1)S(1)}, u32[]{:S(2)}, u32[]{:S(2)}) collective-permute-start(bf16[256,1024]{1,0:T(8,128)(2,1)S(1)} %collective-permute-done.9.across), channel_id=1, source_target_pairs={{0,1},{1,0},{4,5},{5,4},{8,9},{9,8},{12,13},{13,12},{16,17},{17,16... | collective-permute-start | bytes 1572872 | tf_op jit(solution)/shard_map/ppermute | solution.py:246
  81.5 2.0 %collective-permute-start.16 = (bf16[256,1024]{1,0:T(8,128)(2,1)S(1)}, bf16[256,1024]{1,0:T(8,128)(2,1)S(1)}, u32[]{:S(2)}, u32[]{:S(2)}) collective-permute-start(bf16[256,1024]{1,0:T(8,128)(2,1)S(1)} %collective-permute-done.11.six), channel_id=1, source_target_pairs={{0,1},{1,0},{2,3},{3,2},{4,5},{5,4},{6,7},{7,6},{8,9},{9,8},{10,11... | collective-permute-start | bytes 1572872 | tf_op jit(solution)/shard_map/ppermute | solution.py:246

commit v6 on v5

--- a/solution.py
+++ b/solution.py
@@ -344,9 +344,9 @@
     return pl.pallas_call(
         near_body,
         out_shape=jax.ShapeDtypeStruct((5, LAGS, channels, channels), HALF),
-        grid=(LAGS // 2,),
+        grid=(LAGS // 4,),
         in_specs=[SCALAR] + [WHOLE] * 5 + [pl.BlockSpec(memory_space=pl.ANY)] * 2,
-        out_specs=pl.BlockSpec((5, 2, channels, channels), lambda i: (0, i, 0, 0)),
+        out_specs=pl.BlockSpec((5, 4, channels, channels), lambda i: (0, i, 0, 0)),
         scratch_shapes=[pltpu.VMEM((channels, 2 * NF), HALF), pltpu.SemaphoreType.DMA],
         compiler_params=pltpu.CompilerParams(vmem_limit_bytes=24 << 20),
         cost_estimate=cost(channels, 5),

time: 90.9 us -> 90.5 us (level)
  transfers between devices with their start and end apart: 18 -> 18, of which waited for: 8 -> 8; matrix products, arithmetic and copies ran while one was open for 1% -> 1% of each run, Pallas kernels for 11% -> 10%
where the time goes in v6:
time: 90.5 us; the launch traced here: 90.2 us
  waiting for transfers between devices  33.4 us (37%)
  starting transfers between devices  29.8 us (33%)
  Pallas kernels  24.1 us (27%)
  between operations  1.54 us (2%)
  local copies, waits for them, and re-layouts  1.22 us (1%)
    ppermute x10, waiting for transfers between devices, send(): return lax.ppermute(value, 'row', pairs)  20.5 us
    ppermute x10, starting transfers between devices, send(): return lax.ppermute(value, 'row', pairs)  19.7 us
    ppermute x7, waiting for transfers between devices, transpose_blocks(): lax.ppermute(pieces[d], 'row', [(s, s ^ 2 * d) for s in range(tiles)])  12.3 us
    ppermute x7, starting transfers between devices, transpose_blocks(): lax.ppermute(pieces[d], 'row', [(s, s ^ 2 * d) for s in range(tiles)])  9.36 us
    pallas_call x1, Pallas kernels, correlate_far(): pl.pallas_call(functools.partial(far_body, rows=rows), out_shape=jax.Shap...  7.16 us
    pallas_call x1, Pallas kernels, correlate_near(): pl.pallas_call(near_body, out_shape=jax.ShapeDtypeStruct((5, LAGS, channe...  6.21 us
    pallas_call x1, Pallas kernels, filter_blocks(): pl.pallas_call(functools.partial(filter_body, channels=channels), out_sha...  5.85 us
    pallas_call x1, Pallas kernels, correlate_own(): pl.pallas_call(own_body, out_shape=(jax.ShapeDtypeStruct((LAGS, channels,...  3.06 us
  transfers between devices with their start and end apart: 18, of which 8 were waited for; matrix products, arithmetic and copies ran while one was open for 1% of the time, Pallas kernels for 10%

profile of v6, /device:TPU:3, one launch (start us, length us, event | category | flops | bytes accessed | tf_op | source)
XLA Modules:
  0.0 90.2 jit_solution(11457742719703570330)
XLA Ops:
  0.0 5.8 %filter.1 = (bf16[8,264,128]{2,1,0:T(8,128)(2,1)}, bf16[8,264,128]{2,1,0:T(8,128)(2,1)}) custom-call(f32[16]{0:T(128)} %taps.1, bf16[4096,512]{1,0:T(8,128)(2,1)} %raw.1), custom_call_target="tpu_custom_call" | custom-call | tf_op jit(solution)/shard_map/filter/pallas_call | solution.py:124
  6.6 1.1 %slice_bitcast_fusion.8 = (bf16[264,128]{1,0:T(8,128)(2,1)S(1)}, bf16[264,128]{1,0:T(8,128)(2,1)S(1)}, bf16[264,128]{1,0:T(8,128)(2,1)S(1)}, bf16[264,128]{1,0:T...) fusion(bf16[8,264,128]{2,1,0:T(8,128)(2,1)} %get-tuple-element.30), kind=kLoop, calls=%fused_computation.16 | loop fusion | bytes 1081344 | tf_op jit(solution)/shard_map/squeeze | solution.py:150
  8.6 1.5 %collective-permute-start.2 = (bf16[528,128]{1,0:T(8,128)(2,1)S(1)}, bf16[528,128]{1,0:T(8,128)(2,1)S(1)}, u32[]{:S(2)}, u32[]{:S(2)}) collective-permute-start(bf16[528,128]{1,0:T(8,128)(2,1)S(1)} %get-tuple-element.34), channel_id=1, source_target_pairs={{0,4},{1,5},{2,6},{3,7},{4,0},{5,1},{6,2},{7,3},{8,12},{9,13},{10,... | collective-permute-start | bytes 405512 | tf_op jit(solution)/shard_map/ppermute | solution.py:153
  11.3 2.3 %collective-permute-start.4 = (bf16[528,128]{1,0:T(8,128)(2,1)S(1)}, bf16[528,128]{1,0:T(8,128)(2,1)S(1)}, u32[]{:S(2)}, u32[]{:S(2)}) collective-permute-start(bf16[528,128]{1,0:T(8,128)(2,1)S(1)} %get-tuple-element.36), channel_id=1, source_target_pairs={{0,8},{1,9},{2,10},{3,11},{4,12},{5,13},{6,14},{7,15},{8,0},{9,1},... | collective-permute-start | bytes 405512 | tf_op jit(solution)/shard_map/ppermute | solution.py:153
  13.6 3.3 %collective-permute-start.6 = (bf16[528,128]{1,0:T(8,128)(2,1)S(1)}, bf16[528,128]{1,0:T(8,128)(2,1)S(1)}, u32[]{:S(2)}, u32[]{:S(2)}) collective-permute-start(bf16[528,128]{1,0:T(8,128)(2,1)S(1)} %get-tuple-element.38), channel_id=1, source_target_pairs={{0,12},{1,13},{2,14},{3,15},{4,8},{5,9},{6,10},{7,11},{8,4},{9,5},... | collective-permute-start | bytes 405512 | tf_op jit(solution)/shard_map/ppermute | solution.py:153
  18.6 3.3 %collective-permute-done.3.rest_3_ = bf16[528,128]{1,0:T(8,128)(2,1)S(1)} collective-permute-done((bf16[528,128]{1,0:T(8,128)(2,1)S(1)}, bf16[528,128]{1,0:T(8,128)(2,1)S(1)}, u32[]{:S(2)}, u32[]{:S(2)}) %collective-permute-start.3) | collective-permute-done | bytes 135200 | tf_op jit(solution)/shard_map/ppermute | solution.py:153
  21.9 5.5 %collective-permute-done.6.rest_6_ = bf16[528,128]{1,0:T(8,128)(2,1)S(1)} collective-permute-done((bf16[528,128]{1,0:T(8,128)(2,1)S(1)}, bf16[528,128]{1,0:T(8,128)(2,1)S(1)}, u32[]{:S(2)}, u32[]{:S(2)}) %collective-permute-start.6) | collective-permute-done | bytes 135200 | tf_op jit(solution)/shard_map/ppermute | solution.py:153
  27.4 3.5 %collective-permute-done.7.rest_7_ = bf16[528,128]{1,0:T(8,128)(2,1)S(1)} collective-permute-done((bf16[528,128]{1,0:T(8,128)(2,1)S(1)}, bf16[528,128]{1,0:T(8,128)(2,1)S(1)}, u32[]{:S(2)}, u32[]{:S(2)}) %collective-permute-start.7) | collective-permute-done | bytes 135200 | tf_op jit(solution)/shard_map/ppermute | solution.py:153
  30.9 1.9 %whiten.1 = (bf16[256,1024]{1,0:T(8,128)(2,1)S(1)}, f32[256,512]{1,0:T(8,128)S(1)}, f32[256,512]{1,0:T(8,128)S(1)}) custom-call(s32[1]{0:T(128)S(6)} %copy.12.dead, bf16[2048,1024]{1,0:T(8,128)(2,1)S(1)} %copy-done, bf16[128,1024]{1,0:T(8,128)(2,1)S(1)} %copy-done.2, bf16[512,512]{1,0:T(8,128)(2,1)S(1)} %copy-done.1, f32[1,512]{1,0:T(1,128)S(1)} %copy-done.3, ...), custom_call_target="tpu_custom_call" | custom-call | tf_op jit(solution)/shard_map/whiten/pallas_call | solution.py:220
  32.7 2.0 %collective-permute-start.9 = (bf16[256,1024]{1,0:T(8,128)(2,1)S(1)}, bf16[256,1024]{1,0:T(8,128)(2,1)S(1)}, u32[]{:S(2)}, u32[]{:S(2)}) collective-permute-start(bf16[256,1024]{1,0:T(8,128)(2,1)S(1)} %get-tuple-element.40.white), channel_id=1, source_target_pairs={{0,2},{1,3},{2,0},{3,1},{4,6},{5,7},{6,4},{7,5},{8,10},{9,11},{10,... | collective-permute-start | bytes 1572872 | tf_op jit(solution)/shard_map/ppermute | solution.py:246
  34.7 1.3 %collective-permute-start.8 = (bf16[256,1024]{1,0:T(8,128)(2,1)S(1)}, bf16[256,1024]{1,0:T(8,128)(2,1)S(1)}, u32[]{:S(2)}, u32[]{:S(2)}) collective-permute-start(bf16[256,1024]{1,0:T(8,128)(2,1)S(1)} %get-tuple-element.40.white), channel_id=1, source_target_pairs={{4,0},{5,1},{6,2},{7,3},{8,4},{9,5},{10,6},{11,7},{12,8},{13,9},{1... | collective-permute-start | bytes 1572872 | tf_op jit(solution)/shard_map/ppermute | solution.py:246
  36.0 4.4 %collective-permute-start.10 = (bf16[256,1024]{1,0:T(8,128)(2,1)S(1)}, bf16[256,1024]{1,0:T(8,128)(2,1)S(1)}, u32[]{:S(2)}, u32[]{:S(2)}) collective-permute-start(bf16[256,1024]{1,0:T(8,128)(2,1)S(1)} %get-tuple-element.40.white), channel_id=1, source_target_pairs={{1,0},{3,2},{5,4},{7,6},{9,8},{11,10},{13,12},{15,14},{17,16},{19,... | collective-permute-start | bytes 1572872 | tf_op jit(solution)/shard_map/ppermute | solution.py:246
  41.1 3.1 %correlate_own.1 = (bf16[8,256,1024]{2,1,0:T(8,128)(2,1)S(1)}, bf16[8,256,256]{2,1,0:T(8,128)(2,1)S(1)}) custom-call(s32[1]{0:T(128)S(6)} %copy.11.band, f32[256,512]{1,0:T(8,128)S(1)} %get-tuple-element.41.real, f32[256,512]{1,0:T(8,128)S(1)} %get-tuple-element.42.imag, f32[8,1,512]{2,1,0:T(1,128)S(1)} %copy-done.5, f32[8,1,512]{2,1,0:T(1,128)S(1)} %copy-done.4, ...), custom_call_target="tpu_custom_call" | custom-call | flops 1073741824 | bytes 5242880 | tf_op jit(solution)/shard_map/correlate_own/pallas_call | solution.py:300
  44.2 9.1 %collective-permute-done.8.four = bf16[256,1024]{1,0:T(8,128)(2,1)S(1)} collective-permute-done((bf16[256,1024]{1,0:T(8,128)(2,1)S(1)}, bf16[256,1024]{1,0:T(8,128)(2,1)S(1)}, u32[]{:S(2)}, u32[]{:S(2)}) %collective-permute-start.8) | collective-permute-done | bytes 524320 | tf_op jit(solution)/shard_map/ppermute | solution.py:246
  53.4 1.3 %collective-permute-start.14 = (bf16[256,1024]{1,0:T(8,128)(2,1)S(1)}, bf16[256,1024]{1,0:T(8,128)(2,1)S(1)}, u32[]{:S(2)}, u32[]{:S(2)}) collective-permute-start(bf16[256,1024]{1,0:T(8,128)(2,1)S(1)} %collective-permute-done.9.across), channel_id=1, source_target_pairs={{6,2},{7,3},{10,6},{11,7},{14,10},{15,11},{22,18},{23,19},{26,22},... | collective-permute-start | bytes 1572872 | tf_op jit(solution)/shard_map/ppermute | solution.py:246
  54.6 1.3 %collective-permute-start.13 = (bf16[256,1024]{1,0:T(8,128)(2,1)S(1)}, bf16[256,1024]{1,0:T(8,128)(2,1)S(1)}, u32[]{:S(2)}, u32[]{:S(2)}) collective-permute-start(bf16[256,1024]{1,0:T(8,128)(2,1)S(1)} %collective-permute-done.8.four), channel_id=1, source_target_pairs={{4,1},{6,3},{8,5},{10,7},{12,9},{14,11},{20,17},{22,19},{24,21},{2... | collective-permute-start | bytes 1572872 | tf_op jit(solution)/shard_map/ppermute | solution.py:246
  55.9 1.7 %collective-permute-start.12 = (bf16[256,1024]{1,0:T(8,128)(2,1)S(1)}, bf16[256,1024]{1,0:T(8,128)(2,1)S(1)}, u32[]{:S(2)}, u32[]{:S(2)}) collective-permute-start(bf16[256,1024]{1,0:T(8,128)(2,1)S(1)} %collective-permute-done.8.four), channel_id=1, source_target_pairs={{0,1},{1,0},{2,3},{3,2},{4,5},{5,4},{6,7},{7,6},{8,9},{9,8},{10,11... | collective-permute-start | bytes 1572872 | tf_op jit(solution)/shard_map/ppermute | solution.py:246
  57.6 1.9 %collective-permute-start.11 = (bf16[256,1024]{1,0:T(8,128)(2,1)S(1)}, bf16[256,1024]{1,0:T(8,128)(2,1)S(1)}, u32[]{:S(2)}, u32[]{:S(2)}) collective-permute-start(bf16[256,1024]{1,0:T(8,128)(2,1)S(1)} %collective-permute-done.8.four), channel_id=1, source_target_pairs={{2,0},{3,1},{4,2},{5,3},{6,4},{7,5},{8,6},{9,7},{10,8},{11,9},{12,... | collective-permute-start | bytes 1572872 | tf_op jit(solution)/shard_map/ppermute | solution.py:246
  59.5 6.9 %collective-permute-done.14.two = bf16[256,1024]{1,0:T(8,128)(2,1)S(1)} collective-permute-done((bf16[256,1024]{1,0:T(8,128)(2,1)S(1)}, bf16[256,1024]{1,0:T(8,128)(2,1)S(1)}, u32[]{:S(2)}, u32[]{:S(2)}) %collective-permute-start.14) | collective-permute-done | bytes 524320 | tf_op jit(solution)/shard_map/ppermute | solution.py:246
  66.4 5.0 %collective-permute-start.15 = (bf16[256,1024]{1,0:T(8,128)(2,1)S(1)}, bf16[256,1024]{1,0:T(8,128)(2,1)S(1)}, u32[]{:S(2)}, u32[]{:S(2)}) collective-permute-start(bf16[256,1024]{1,0:T(8,128)(2,1)S(1)} %collective-permute-done.14.two), channel_id=1, source_target_pairs={{2,3},{3,2},{6,7},{7,6},{10,11},{11,10},{14,15},{15,14},{18,19},{1... | collective-permute-start | bytes 1572872 | tf_op jit(solution)/shard_map/ppermute | solution.py:246
  72.2 2.6 %collective-permute-done.13.seven = bf16[256,1024]{1,0:T(8,128)(2,1)S(1)} collective-permute-done((bf16[256,1024]{1,0:T(8,128)(2,1)S(1)}, bf16[256,1024]{1,0:T(8,128)(2,1)S(1)}, u32[]{:S(2)}, u32[]{:S(2)}) %collective-permute-start.13) | collective-permute-done | bytes 524320 | tf_op jit(solution)/shard_map/ppermute | solution.py:246
  74.8 6.2 %correlate_near.1.near = bf16[5,8,256,256]{3,2,1,0:T(8,128)(2,1)S(1)} custom-call(s32[1]{0:T(128)S(6)} %copy.11.band, bf16[8,256,1024]{2,1,0:T(8,128)(2,1)S(1)} %get-tuple-element.47.lagged, bf16[256,1024]{1,0:T(8,128)(2,1)S(1)} %collective-permute-done.10.one, bf16[256,1024]{1,0:T(8,128)(2,1)S(1)} %collective-permute-done.8.four, ...), custom_call_target="tpu_custom_call" | custom-call | flops 5368709120 | bytes 9437184 | tf_op jit(solution)/shard_map/correlate_near/pallas_call | solution.py:344
  81.1 1.9 %collective-permute-done.16.six_beside = bf16[256,1024]{1,0:T(8,128)(2,1)S(1)} collective-permute-done((bf16[256,1024]{1,0:T(8,128)(2,1)S(1)}, bf16[256,1024]{1,0:T(8,128)(2,1)S(1)}, u32[]{:S(2)}, u32[]{:S(2)}) %collective-permute-start.16) | collective-permute-done | bytes 524320 | tf_op jit(solution)/shard_map/ppermute | solution.py:246
  83.0 7.2 %correlate_far.1 = bf16[256,8,8,256]{3,2,1,0:T(8,128)(2,1)} custom-call(s32[1]{0:T(128)S(6)} %copy.11.band, bf16[8,256,1024]{2,1,0:T(8,128)(2,1)S(1)} %get-tuple-element.47.lagged, bf16[8,256,256]{2,1,0:T(8,128)(2,1)S(1)} %get-tuple-element.48.own, bf16[5,8,256,256]{3,2,1,0:T(8,128)(2,1)S(1)} %correlate_near.1.near, ...), custom_call_target="tpu_custom_call" | custom-call | flops 3221225472 | bytes 7340032 | tf_op jit(solution)/shard_map/correlate_far/pallas_call | solution.py:403
  (35 shorter events, 4.5 us)
Async XLA Ops:
  0.0 30.9 %copy-start = (bf16[2048,1024]{1,0:T(8,128)(2,1)S(1)}, bf16[2048,1024]{1,0:T(8,128)(2,1)}, u32[]{:S(2)}) copy-start(bf16[2048,1024]{1,0:T(8,128)(2,1)} %constant.12.clone.table) | copy-start | bytes 12582916
  0.0 30.9 %copy-start.1 = (bf16[512,512]{1,0:T(8,128)(2,1)S(1)}, bf16[512,512]{1,0:T(8,128)(2,1)}, u32[]{:S(2)}) copy-start(bf16[512,512]{1,0:T(8,128)(2,1)} %constant.14.clone.window) | copy-start | bytes 1572868
  0.0 30.9 %copy-start.2 = (bf16[128,1024]{1,0:T(8,128)(2,1)S(1)}, bf16[128,1024]{1,0:T(8,128)(2,1)}, u32[]{:S(2)}) copy-start(bf16[128,1024]{1,0:T(8,128)(2,1)} %constant.13.clone.edge_table) | copy-start | bytes 786436
  0.0 30.9 %copy-start.3 = (f32[1,512]{1,0:T(1,128)S(1)}, f32[1,512]{1,0:T(1,128)}, u32[]{:S(2)}) copy-start(f32[1,512]{1,0:T(1,128)} %constant.15.clone.counts) | copy-start | bytes 6148
  5.9 2.5 %collective-permute-start = (bf16[8,264,128]{2,1,0:T(8,128)(2,1)}, bf16[8,264,128]{2,1,0:T(8,128)(2,1)S(1)}, u32[]{:S(2)}, u32[]{:S(2)}) collective-permute-start(bf16[8,264,128]{2,1,0:T(8,128)(2,1)} %get-tuple-element.31), channel_id=1, source_target_pairs={{0,1},{1,0},{2,3},{3,2},{4,5},{5,4},{6,7},{7,6},{8,9},{9,8},{10,11... | collective-permute-start | bytes 1622024 | tf_op jit(solution)/shard_map/ppermute | solution.py:149
  8.4 32.7 %copy-start.4 = (f32[8,1,512]{2,1,0:T(1,128)S(1)}, f32[8,1,512]{2,1,0:T(1,128)}, u32[]{:S(2)}) copy-start(f32[8,1,512]{2,1,0:T(1,128)} %constant.17.clone.sine) | copy-start | bytes 49156
  8.4 32.7 %copy-start.5 = (f32[8,1,512]{2,1,0:T(1,128)S(1)}, f32[8,1,512]{2,1,0:T(1,128)}, u32[]{:S(2)}) copy-start(f32[8,1,512]{2,1,0:T(1,128)} %constant.16.clone.cosine) | copy-start | bytes 49156
  8.6 5.0 %collective-permute-start.1 = (bf16[528,128]{1,0:T(8,128)(2,1)S(1)}, bf16[528,128]{1,0:T(8,128)(2,1)S(1)}, u32[]{:S(2)}, u32[]{:S(2)}) collective-permute-start(bf16[528,128]{1,0:T(8,128)(2,1)S(1)} %get-tuple-element.33), channel_id=1, source_target_pairs={{0,2},{1,3},{2,0},{3,1},{4,6},{5,7},{6,4},{7,5},{8,10},{9,11},{10,... | collective-permute-start | bytes 405512 | tf_op jit(solution)/shard_map/ppermute | solution.py:153
  8.6 8.3 %collective-permute-start.2 = (bf16[528,128]{1,0:T(8,128)(2,1)S(1)}, bf16[528,128]{1,0:T(8,128)(2,1)S(1)}, u32[]{:S(2)}, u32[]{:S(2)}) collective-permute-start(bf16[528,128]{1,0:T(8,128)(2,1)S(1)} %get-tuple-element.34), channel_id=1, source_target_pairs={{0,4},{1,5},{2,6},{3,7},{4,0},{5,1},{6,2},{7,3},{8,12},{9,13},{10,... | collective-permute-start | bytes 405512 | tf_op jit(solution)/shard_map/ppermute | solution.py:153
  10.2 11.7 %collective-permute-start.3 = (bf16[528,128]{1,0:T(8,128)(2,1)S(1)}, bf16[528,128]{1,0:T(8,128)(2,1)S(1)}, u32[]{:S(2)}, u32[]{:S(2)}) collective-permute-start(bf16[528,128]{1,0:T(8,128)(2,1)S(1)} %get-tuple-element.35), channel_id=1, source_target_pairs={{0,6},{1,7},{2,4},{3,5},{4,2},{5,3},{6,0},{7,1},{8,14},{9,15},{10,... | collective-permute-start | bytes 405512 | tf_op jit(solution)/shard_map/ppermute | solution.py:153
  11.3 10.6 %collective-permute-start.4 = (bf16[528,128]{1,0:T(8,128)(2,1)S(1)}, bf16[528,128]{1,0:T(8,128)(2,1)S(1)}, u32[]{:S(2)}, u32[]{:S(2)}) collective-permute-start(bf16[528,128]{1,0:T(8,128)(2,1)S(1)} %get-tuple-element.36), channel_id=1, source_target_pairs={{0,8},{1,9},{2,10},{3,11},{4,12},{5,13},{6,14},{7,15},{8,0},{9,1},... | collective-permute-start | bytes 405512 | tf_op jit(solution)/shard_map/ppermute | solution.py:153
  13.6 8.3 %collective-permute-start.5 = (bf16[528,128]{1,0:T(8,128)(2,1)S(1)}, bf16[528,128]{1,0:T(8,128)(2,1)S(1)}, u32[]{:S(2)}, u32[]{:S(2)}) collective-permute-start(bf16[528,128]{1,0:T(8,128)(2,1)S(1)} %get-tuple-element.37), channel_id=1, source_target_pairs={{0,10},{1,11},{2,8},{3,9},{4,14},{5,15},{6,12},{7,13},{8,2},{9,3},... | collective-permute-start | bytes 405512 | tf_op jit(solution)/shard_map/ppermute | solution.py:153
  13.6 13.8 %collective-permute-start.6 = (bf16[528,128]{1,0:T(8,128)(2,1)S(1)}, bf16[528,128]{1,0:T(8,128)(2,1)S(1)}, u32[]{:S(2)}, u32[]{:S(2)}) collective-permute-start(bf16[528,128]{1,0:T(8,128)(2,1)S(1)} %get-tuple-element.38), channel_id=1, source_target_pairs={{0,12},{1,13},{2,14},{3,15},{4,8},{5,9},{6,10},{7,11},{8,4},{9,5},... | collective-permute-start | bytes 405512 | tf_op jit(solution)/shard_map/ppermute | solution.py:153
  17.0 13.9 %collective-permute-start.7 = (bf16[528,128]{1,0:T(8,128)(2,1)S(1)}, bf16[528,128]{1,0:T(8,128)(2,1)S(1)}, u32[]{:S(2)}, u32[]{:S(2)}) collective-permute-start(bf16[528,128]{1,0:T(8,128)(2,1)S(1)} %get-tuple-element.39), channel_id=1, source_target_pairs={{0,14},{1,15},{2,12},{3,13},{4,10},{5,11},{6,8},{7,9},{8,6},{9,7},... | collective-permute-start | bytes 405512 | tf_op jit(solution)/shard_map/ppermute | solution.py:153
  32.7 11.5 %collective-permute-start.9 = (bf16[256,1024]{1,0:T(8,128)(2,1)S(1)}, bf16[256,1024]{1,0:T(8,128)(2,1)S(1)}, u32[]{:S(2)}, u32[]{:S(2)}) collective-permute-start(bf16[256,1024]{1,0:T(8,128)(2,1)S(1)} %get-tuple-element.40.white), channel_id=1, source_target_pairs={{0,2},{1,3},{2,0},{3,1},{4,6},{5,7},{6,4},{7,5},{8,10},{9,11},{10,... | collective-permute-start | bytes 1572872 | tf_op jit(solution)/shard_map/ppermute | solution.py:246
  34.7 18.6 %collective-permute-start.8 = (bf16[256,1024]{1,0:T(8,128)(2,1)S(1)}, bf16[256,1024]{1,0:T(8,128)(2,1)S(1)}, u32[]{:S(2)}, u32[]{:S(2)}) collective-permute-start(bf16[256,1024]{1,0:T(8,128)(2,1)S(1)} %get-tuple-element.40.white), channel_id=1, source_target_pairs={{4,0},{5,1},{6,2},{7,3},{8,4},{9,5},{10,6},{11,7},{12,8},{13,9},{1... | collective-permute-start | bytes 1572872 | tf_op jit(solution)/shard_map/ppermute | solution.py:246
  36.0 17.3 %collective-permute-start.10 = (bf16[256,1024]{1,0:T(8,128)(2,1)S(1)}, bf16[256,1024]{1,0:T(8,128)(2,1)S(1)}, u32[]{:S(2)}, u32[]{:S(2)}) collective-permute-start(bf16[256,1024]{1,0:T(8,128)(2,1)S(1)} %get-tuple-element.40.white), channel_id=1, source_target_pairs={{1,0},{3,2},{5,4},{7,6},{9,8},{11,10},{13,12},{15,14},{17,16},{19,... | collective-permute-start | bytes 1572872 | tf_op jit(solution)/shard_map/ppermute | solution.py:246
  53.4 13.1 %collective-permute-start.14 = (bf16[256,1024]{1,0:T(8,128)(2,1)S(1)}, bf16[256,1024]{1,0:T(8,128)(2,1)S(1)}, u32[]{:S(2)}, u32[]{:S(2)}) collective-permute-start(bf16[256,1024]{1,0:T(8,128)(2,1)S(1)} %collective-permute-done.9.across), channel_id=1, source_target_pairs={{6,2},{7,3},{10,6},{11,7},{14,10},{15,11},{22,18},{23,19},{26,22},... | collective-permute-start | bytes 1572872 | tf_op jit(solution)/shard_map/ppermute | solution.py:246
  54.6 20.2 %collective-permute-start.13 = (bf16[256,1024]{1,0:T(8,128)(2,1)S(1)}, bf16[256,1024]{1,0:T(8,128)(2,1)S(1)}, u32[]{:S(2)}, u32[]{:S(2)}) collective-permute-start(bf16[256,1024]{1,0:T(8,128)(2,1)S(1)} %collective-permute-done.8.four), channel_id=1, source_target_pairs={{4,1},{6,3},{8,5},{10,7},{12,9},{14,11},{20,17},{22,19},{24,21},{2... | collective-permute-start | bytes 1572872 | tf_op jit(solution)/shard_map/ppermute | solution.py:246
  55.9 18.9 %collective-permute-start.12 = (bf16[256,1024]{1,0:T(8,128)(2,1)S(1)}, bf16[256,1024]{1,0:T(8,128)(2,1)S(1)}, u32[]{:S(2)}, u32[]{:S(2)}) collective-permute-start(bf16[256,1024]{1,0:T(8,128)(2,1)S(1)} %collective-permute-done.8.four), channel_id=1, source_target_pairs={{0,1},{1,0},{2,3},{3,2},{4,5},{5,4},{6,7},{7,6},{8,9},{9,8},{10,11... | collective-permute-start | bytes 1572872 | tf_op jit(solution)/shard_map/ppermute | solution.py:246
  57.6 23.4 %collective-permute-start.11 = (bf16[256,1024]{1,0:T(8,128)(2,1)S(1)}, bf16[256,1024]{1,0:T(8,128)(2,1)S(1)}, u32[]{:S(2)}, u32[]{:S(2)}) collective-permute-start(bf16[256,1024]{1,0:T(8,128)(2,1)S(1)} %collective-permute-done.8.four), channel_id=1, source_target_pairs={{2,0},{3,1},{4,2},{5,3},{6,4},{7,5},{8,6},{9,7},{10,8},{11,9},{12,... | collective-permute-start | bytes 1572872 | tf_op jit(solution)/shard_map/ppermute | solution.py:246
  66.4 14.6 %collective-permute-start.15 = (bf16[256,1024]{1,0:T(8,128)(2,1)S(1)}, bf16[256,1024]{1,0:T(8,128)(2,1)S(1)}, u32[]{:S(2)}, u32[]{:S(2)}) collective-permute-start(bf16[256,1024]{1,0:T(8,128)(2,1)S(1)} %collective-permute-done.14.two), channel_id=1, source_target_pairs={{2,3},{3,2},{6,7},{7,6},{10,11},{11,10},{14,15},{15,14},{18,19},{1... | collective-permute-start | bytes 1572872 | tf_op jit(solution)/shard_map/ppermute | solution.py:246
  71.5 9.6 %collective-permute-start.17 = (bf16[256,1024]{1,0:T(8,128)(2,1)S(1)}, bf16[256,1024]{1,0:T(8,128)(2,1)S(1)}, u32[]{:S(2)}, u32[]{:S(2)}) collective-permute-start(bf16[256,1024]{1,0:T(8,128)(2,1)S(1)} %collective-permute-done.9.across), channel_id=1, source_target_pairs={{0,1},{1,0},{4,5},{5,4},{8,9},{9,8},{12,13},{13,12},{16,17},{17,16... | collective-permute-start | bytes 1572872 | tf_op jit(solution)/shard_map/ppermute | solution.py:246
  81.0 2.0 %collective-permute-start.16 = (bf16[256,1024]{1,0:T(8,128)(2,1)S(1)}, bf16[256,1024]{1,0:T(8,128)(2,1)S(1)}, u32[]{:S(2)}, u32[]{:S(2)}) collective-permute-start(bf16[256,1024]{1,0:T(8,128)(2,1)S(1)} %collective-permute-done.11.six), channel_id=1, source_target_pairs={{0,1},{1,0},{2,3},{3,2},{4,5},{5,4},{6,7},{7,6},{8,9},{9,8},{10,11... | collective-permute-start | bytes 1572872 | tf_op jit(solution)/shard_map/ppermute | solution.py:246
